TPU v7x, 32 devices: a whole 2x2x4 slice. The times are simulated.
32 devices in a mesh: ctx: 8 (over z, x), fsdp: 2 (over y), dp: 2 (over core).
Axes of the slice: x: 2, y: 2, z: 4, core: 2. Of those that a mesh axis runs over, the one named last changes fastest.
Arguments:
- inputs: bfloat16 [4, 1024, 4096], P(('fsdp', 'dp'), 'ctx'), may hold values from -6 to 6
- queries: bfloat16 [4, 1024, 4096], P(('fsdp', 'dp'), 'ctx'), may hold values from -40 to 40, as said below
- w_kv: bfloat16 [4096, 1024], P(('ctx', 'fsdp')), may hold values from -0.09375 to 0.09375
- tile_mask: int32 [8, 4], P('ctx'), may hold values from 0 to 1, as said below
- grad_out: bfloat16 [4, 1024, 4096], P(('fsdp', 'dp'), 'ctx'), may hold values from -6 to 6
Outputs:
- attn_out: bfloat16 [4, 1024, 4096], P(('fsdp', 'dp'), 'ctx')
- grad_queries: bfloat16 [4, 1024, 4096], P(('fsdp', 'dp'), 'ctx')
- grad_inputs: bfloat16 [4, 1024, 4096], P(('fsdp', 'dp'), 'ctx')
- grad_weights: float32 [4096, 1024], P(('ctx', 'fsdp'))
Inputs may be any that keep to these rules, and one draw needn't show every extreme that they name: tile_mask[b, j] = 1 marks that query tile b scores key tile b - j - 1 in full; it is 0 where b - j - 1 < 0. The tiles of at least one token shard, drawn from the seed, score all earlier tiles within reach, the others few of them. `queries`: entries of order one, on some draws some rows larger.
All inputs are finite; a program needn't handle non-finite values.
Results may differ from a plain program's by a relative error of at most 0.015.
The roundings to bfloat16 on the way count: a program that leaves them out, or rounds other values in their place, can miss the bound.
Values may be sent and summed in bfloat16 or wider, within the bound.
No kernel may reach another device: no remote copies, remote signals or barrier semaphores. Data moves between devices by JAX's collectives and lax.ppermute only.
A program may use at most 128 MiB of HBM per device.

v0:
```python
import math

import jax
import jax.numpy as jnp
from jax import lax
from jax.sharding import PartitionSpec as P

HEADS = 32
KV_HEADS = 4
HEAD_DIM = 128
BLOCK = 128
REACH = 4


def passed_along(x, axis, by):
    peers = lax.axis_size(axis)
    pairs = [(i, i + by) for i in range(peers) if 0 <= i + by < peers]
    return lax.ppermute(x, axis, pairs)


def block_allowed(mask_rows, tok_rows):
    query_count = tok_rows // BLOCK
    reach_cols = mask_rows.shape[1]
    window_count = (REACH + 1) * query_count
    query_blk = jnp.arange(query_count, dtype=jnp.int32)[:, None]
    window_blk = jnp.arange(window_count, dtype=jnp.int32)[None, :]
    shard_back = REACH - window_blk // query_count
    key_blk = window_blk % query_count
    tile_offset = query_blk - key_blk + shard_back * query_count
    columns = jnp.arange(reach_cols, dtype=jnp.int32)
    one_hot = (columns[None, None, :] == (tile_offset - 1)[:, :, None]).astype(jnp.int32)
    tile_flag = jnp.sum(mask_rows[:, None, :] * one_hot, axis=2)
    full_tiles = (tile_offset >= 1) & (tile_offset <= reach_cols) & (tile_flag > 0)
    diag_tiles = tile_offset == 0
    shape_four = (query_count, BLOCK, window_count, BLOCK)
    full_tok = jnp.broadcast_to(full_tiles[:, None, :, None], shape_four).reshape(
        tok_rows, window_count * BLOCK
    )
    diag_tok = jnp.broadcast_to(diag_tiles[:, None, :, None], shape_four).reshape(
        tok_rows, window_count * BLOCK
    )
    query_pos = (jnp.arange(tok_rows, dtype=jnp.int32) % BLOCK)[:, None]
    key_pos = (jnp.arange(window_count * BLOCK, dtype=jnp.int32) % BLOCK)[None, :]
    return full_tok | diag_tok & (key_pos <= query_pos)


def attend(query_rows, window, grad_rows, allowed):
    tok_rows = query_rows.shape[0]
    win_rows = window.shape[0]
    key_width = window.shape[1] // 2
    groups = HEADS // KV_HEADS
    score_scale = 1.0 / math.sqrt(HEAD_DIM)
    query_heads = query_rows.reshape(tok_rows, KV_HEADS, groups, HEAD_DIM)
    key_heads = window[:, :key_width].reshape(win_rows, KV_HEADS, HEAD_DIM)
    value_heads = window[:, key_width:].reshape(win_rows, KV_HEADS, HEAD_DIM)
    grad_heads = grad_rows.reshape(tok_rows, KV_HEADS, groups, HEAD_DIM)
    scores = (
        jnp.einsum("tkgd,wkd->kgtw", query_heads, key_heads, preferred_element_type=jnp.float32)
        * score_scale
    )
    scores = jnp.where(allowed, scores, -jnp.inf)
    row_top = jnp.max(scores, axis=-1, keepdims=True)
    weights = jnp.where(allowed, jnp.exp(scores - row_top), 0.0)
    prob_share = weights / jnp.sum(weights, axis=-1, keepdims=True)
    prob_bf16 = prob_share.astype(jnp.bfloat16)
    attended = jnp.einsum(
        "kgtw,wkd->tkgd", prob_bf16, value_heads, preferred_element_type=jnp.float32
    ).astype(jnp.bfloat16)
    grad_prob = jnp.einsum(
        "tkgd,wkd->kgtw", grad_heads, value_heads, preferred_element_type=jnp.float32
    )
    row_delta = jnp.einsum(
        "tkgd,tkgd->kgt", grad_heads, attended, preferred_element_type=jnp.float32
    )[..., None]
    grad_score = (prob_share * (grad_prob - row_delta) * score_scale).astype(jnp.bfloat16)
    grad_query = jnp.einsum(
        "kgtw,wkd->tkgd", grad_score, key_heads, preferred_element_type=jnp.float32
    ).astype(jnp.bfloat16)
    grad_key = jnp.einsum(
        "kgtw,tkgd->wkd", grad_score, query_heads, preferred_element_type=jnp.float32
    )
    grad_value = jnp.einsum(
        "kgtw,tkgd->wkd", prob_bf16, grad_heads, preferred_element_type=jnp.float32
    )
    grad_window = jnp.concatenate(
        [grad_key.reshape(win_rows, key_width), grad_value.reshape(win_rows, key_width)], axis=1
    )
    return (attended.reshape(tok_rows, -1), grad_query.reshape(tok_rows, -1), grad_window)


def per_device(inputs, queries, w_kv, tile_mask, grad_out):
    whole_weights = lax.all_gather(w_kv, ("ctx", "fsdp"), axis=0, tiled=True)
    rows_in = inputs[0]
    tok_rows = rows_in.shape[0]
    key_vals = jnp.dot(rows_in, whole_weights, preferred_element_type=jnp.float32).astype(
        jnp.bfloat16
    )
    pieces = [key_vals]
    moving = key_vals
    for step in range(REACH):
        moving = passed_along(moving, "ctx", 1)
        pieces = [moving] + pieces
    window = jnp.concatenate(pieces, axis=0)
    allowed = block_allowed(tile_mask, tok_rows)
    attended, grad_query, grad_window = attend(queries[0], window, grad_out[0], allowed)
    window_parts = grad_window.reshape(REACH + 1, tok_rows, grad_window.shape[1])
    running = window_parts[0]
    for window_pos in range(1, REACH + 1):
        running = passed_along(running, "ctx", -1) + window_parts[window_pos]
    grad_kv = running.astype(jnp.bfloat16)
    grad_in = lax.dot_general(
        grad_kv, whole_weights, (((1,), (1,)), ((), ())), preferred_element_type=jnp.float32
    ).astype(jnp.bfloat16)
    norm_factor = 1.0 / math.sqrt(
        lax.axis_size("fsdp") * lax.axis_size("dp") * lax.axis_size("ctx") * tok_rows
    )
    fine_grad = lax.psum_scatter(
        lax.dot_general(
            rows_in, grad_kv, (((0,), (0,)), ((), ())), preferred_element_type=jnp.float32
        ),
        ("ctx", "fsdp", "dp"),
        scatter_dimension=0,
        tiled=True,
    )
    weight_grad = lax.all_gather(fine_grad, "dp", axis=0, tiled=True)
    return (attended[None], grad_query[None], grad_in[None], weight_grad * norm_factor)


def solution(mesh):
    return jax.shard_map(
        per_device,
        mesh=mesh,
        in_specs=(
            P(("fsdp", "dp"), "ctx", None),
            P(("fsdp", "dp"), "ctx", None),
            P(("ctx", "fsdp"), None),
            P("ctx", None),
            P(("fsdp", "dp"), "ctx", None),
        ),
        out_specs=(
            P(("fsdp", "dp"), "ctx", None),
            P(("fsdp", "dp"), "ctx", None),
            P(("fsdp", "dp"), "ctx", None),
            P(("ctx", "fsdp"), None),
        ),
        check_vma=False,
    )
```

profile of v0, /device:TPU:11, one launch (start us, length us, event | category | flops | bytes accessed | tf_op | source)
XLA Modules:
  0.0 480.2 jit_solution(10707996797845339445)
XLA Ops:
  8.0 113.1 %all-gather.3.cloned.1.call-done = bf16[4096,1024]{1,0:T(8,128)(2,1)} async-done(((bf16[256,1024]{1,0:T(8,128)(2,1)}), bf16[4096,1024]{1,0:T(8,128)(2,1)}) %all-gather.3.cloned.1.call-update) | async-done | bytes 8388624 | tf_op jit(solution)/shard_map/all_gather | solution.py:92
  121.1 4.6 convolution_convert_fusion.3
  125.8 4.2 collective-permute-start
  130.1 3.8 collective-permute-done
  133.9 5.0 %collective-permute-start.1 = (bf16[128,1024]{1,0:T(8,128)(2,1)S(1)}, bf16[128,1024]{1,0:T(8,128)(2,1)S(1)}, u32[]{:S(2)}, u32[]{:S(2)}) collective-permute-start(bf16[128,1024]{1,0:T(8,128)(2,1)S(1)} %collective-permute-done), channel_id=1, source_target_pairs={{0,4},{4,8},{8,12},{12,16},{16,20},{20,24},{24,28},{1,5},{5,9},{9,... | collective-permute-start | bytes 786440 | tf_op jit(solution)/shard_map/ppermute | solution.py:18
  139.0 3.3 collective-permute-done.1
  142.2 4.7 collective-permute-start.2
  147.0 3.2 collective-permute-done.2
  150.2 4.8 %collective-permute-start.3 = (bf16[128,1024]{1,0:T(8,128)(2,1)}, bf16[128,1024]{1,0:T(8,128)(2,1)}, u32[]{:S(2)}, u32[]{:S(2)}) collective-permute-start(bf16[128,1024]{1,0:T(8,128)(2,1)} %collective-permute-done.2), channel_id=1, source_target_pairs={{0,4},{4,8},{8,12},{12,16},{16,20},{20,24},{24,28},{1,5},{5,9},{9,... | collective-permute-start | bytes 786440 | tf_op jit(solution)/shard_map/ppermute | solution.py:18
  164.7 2.3 reshape.177
  171.5 8.8 %fusion.32 = (f32[4,8,128]{2,1,0:T(8,128)S(1)}, f32[4,8,128,640]{2,3,1,0:T(8,128)}) fusion(pred[128,640]{0,1:T(8,128)(4,1)S(1)} %and_or_fusion, bf16[640,4,128,1]{0,2,3,1:T(8,128)(2,1)} %copy.50, bf16[128,4,8,128]{0,3,2,1:T(8,128)(2,1)S(1)} %bitcast.93), kind=kOutput, calls=%fused_computation.68 | convolution fusion | flops 684196480 | bytes 12288000 | tf_op jit(solution)/shard_map/sub | solution.py:63
  180.4 5.4 %fusion.9 = bf16[4,8,128,640]{2,3,1,0:T(8,128)(2,1)S(1)} fusion(f32[4,8,128,640]{2,3,1,0:T(8,128)} %get-tuple-element.15, f32[4,8,128]{2,1,0:T(8,128)S(1)} %get-tuple-element.14), kind=kLoop, calls=%fused_computation.15 | loop fusion | flops 5242880 | bytes 15745024 | tf_op jit(solution)/shard_map/convert_element_type | solution.py:65
  187.5 2.7 bitcast_convert_fusion
  190.2 3.1 copy.48
  193.3 3.0 multiply_reduce_fusion
  197.3 6.7 %fusion.3 = bf16[4,8,128,640]{2,3,1,0:T(8,128)(2,1)S(1)} fusion(f32[4,8,128]{2,1,0:T(8,128)S(1)} %copy.49, f32[4,8,128,640]{2,3,1,0:T(8,128)} %get-tuple-element.15, f32[4,8,128]{2,1,0:T(8,128)S(1)} %get-tuple-element.14, bf16[128,4,8,128]{0,3,2,1:T(8,128)(2,1)} %copy.35, bf16[640,4,128,1]{2,1,0,3:T(4,128)(2,1)} %bitcast.97), kind=kOutput, calls=%fused_computation.4 | convolution fusion | flops 684195840 | bytes 17465344 | tf_op jit(solution)/shard_map/tkgd,wkd->kgtw/dot_general | solution.py:69
  208.4 8.9 %collective-permute-done.4 = f32[128,1024]{0,1:T(8,128)S(1)} collective-permute-done((f32[128,1024]{0,1:T(8,128)S(1)}, f32[128,1024]{0,1:T(8,128)S(1)}, u32[]{:S(2)}, u32[]{:S(2)}) %collective-permute-start.4) | collective-permute-done | bytes 524320 | tf_op jit(solution)/shard_map/ppermute | solution.py:18
  219.3 9.7 %collective-permute-done.5 = f32[128,1024]{0,1:T(8,128)S(1)} collective-permute-done((f32[128,1024]{0,1:T(8,128)S(1)}, f32[128,1024]{0,1:T(8,128)S(1)}, u32[]{:S(2)}, u32[]{:S(2)}) %collective-permute-start.5) | collective-permute-done | bytes 524320 | tf_op jit(solution)/shard_map/ppermute | solution.py:18
  231.0 10.7 %collective-permute-done.6 = f32[128,1024]{0,1:T(8,128)S(1)} collective-permute-done((f32[128,1024]{0,1:T(8,128)S(1)}, f32[128,1024]{0,1:T(8,128)S(1)}, u32[]{:S(2)}, u32[]{:S(2)}) %collective-permute-start.6) | collective-permute-done | bytes 524320 | tf_op jit(solution)/shard_map/ppermute | solution.py:18
  243.7 9.6 %collective-permute-done.7 = f32[128,1024]{0,1:T(8,128)S(1)} collective-permute-done((f32[128,1024]{0,1:T(8,128)S(1)}, f32[128,1024]{0,1:T(8,128)S(1)}, u32[]{:S(2)}, u32[]{:S(2)}) %collective-permute-start.7) | collective-permute-done | bytes 524320 | tf_op jit(solution)/shard_map/ppermute | solution.py:18
  254.1 8.1 %convolution_bitcast_fusion = f32[4096,1024]{0,1:T(8,128)} fusion(bf16[128,1024]{0,1:T(8,128)(2,1)S(1)} %fusion.24, bf16[1,128,4096]{2,1,0:T(8,128)(2,1)S(1)} %copy-done), kind=kOutput, calls=%fused_computation.7 | convolution fusion | flops 1073741824 | bytes 18087936 | tf_op jit(solution)/shard_map/dot_general | solution.py:118
  262.2 195.4 %reduce-scatter.2.cloned.1.call-done = f32[128,1024]{0,1:T(8,128)} async-done(((f32[4096,1024]{0,1:T(8,128)}), f32[128,1024]{0,1:T(8,128)}) %reduce-scatter.2.cloned.1.call-update) | async-done | bytes 524304 | tf_op jit(solution)/shard_map/reduce_scatter | solution.py:117
  459.0 3.5 convolution_convert_fusion.1
  463.8 7.3 %fusion.8 = bf16[1,128,4096]{2,1,0:T(8,128)(2,1)} fusion(bf16[128,1024]{0,1:T(8,128)(2,1)S(1)} %copy-done.9, bf16[4096,1024]{1,0:T(8,128)(2,1)} %all-gather.3.cloned.1.call-done), kind=kOutput, calls=%fused_computation.14 | convolution fusion | flops 1074266112 | bytes 9699328 | tf_op jit(solution)/shard_map/dot_general | solution.py:111
  (71 shorter events, 34.2 us)
Async XLA Ops:
  7.2 114.0 %copy-start = (bf16[1,128,4096]{2,1,0:T(8,128)(2,1)S(1)}, bf16[1,128,4096]{2,1,0:T(8,128)(2,1)}, u32[]{:S(2)}) copy-start(bf16[1,128,4096]{2,1,0:T(8,128)(2,1)} %param.5) | copy-start | bytes 3145732
  7.2 113.9 %all-gather.3.cloned.1.call-start = ((), (), s32[]{:S(2)}) async-start(), calls=%async_computation.1 | async-start | bytes 8912896 | tf_op jit(solution)/shard_map/all_gather | solution.py:92
  7.9 122.1 %copy-start.13 = (s32[1,4]{1,0:T(1,128)S(1)}, s32[1,4]{1,0:T(1,128)}, u32[]{:S(2)}) copy-start(s32[1,4]{1,0:T(1,128)} %param.8) | copy-start | bytes 52
  7.9 147.2 %copy-start.10 = (bf16[1,128,4096]{2,1,0:T(8,128)(2,1)S(1)}, bf16[1,128,4096]{2,1,0:T(8,128)(2,1)}, u32[]{:S(2)}) copy-start(bf16[1,128,4096]{2,1,0:T(8,128)(2,1)} %param.6) | copy-start | bytes 3145732
  7.9 449.7 %reduce-scatter.2.cloned.1.call-start = ((), (), s32[]{:S(2)}) async-start(), calls=%async_computation.2 | async-start | bytes 17301504 | tf_op jit(solution)/shard_map/reduce_scatter | solution.py:117
  125.8 8.2 %collective-permute-start = (bf16[128,1024]{1,0:T(8,128)(2,1)S(1)}, bf16[128,1024]{1,0:T(8,128)(2,1)S(1)}, u32[]{:S(2)}, u32[]{:S(2)}) collective-permute-start(bf16[128,1024]{1,0:T(8,128)(2,1)S(1)} %convolution_convert_fusion.3), channel_id=1, source_target_pairs={{0,4},{4,8},{8,12},{12,16},{16,20},{20,24},{24,28},{1,5},{5,9},{9,... | collective-permute-start | bytes 786440 | tf_op jit(solution)/shard_map/ppermute | solution.py:18
  133.9 21.1 %copy-start.11 = (bf16[128,1024]{1,0:T(8,128)(2,1)}, bf16[128,1024]{1,0:T(8,128)(2,1)S(1)}, u32[]{:S(2)}) copy-start(bf16[128,1024]{1,0:T(8,128)(2,1)S(1)} %collective-permute-done) | copy-start | bytes 786436
  133.9 8.3 %collective-permute-start.1 = (bf16[128,1024]{1,0:T(8,128)(2,1)S(1)}, bf16[128,1024]{1,0:T(8,128)(2,1)S(1)}, u32[]{:S(2)}, u32[]{:S(2)}) collective-permute-start(bf16[128,1024]{1,0:T(8,128)(2,1)S(1)} %collective-permute-done), channel_id=1, source_target_pairs={{0,4},{4,8},{8,12},{12,16},{16,20},{20,24},{24,28},{1,5},{5,9},{9,... | collective-permute-start | bytes 786440 | tf_op jit(solution)/shard_map/ppermute | solution.py:18
  142.2 12.8 %copy-start.12 = (bf16[128,1024]{1,0:T(8,128)(2,1)}, bf16[128,1024]{1,0:T(8,128)(2,1)S(1)}, u32[]{:S(2)}) copy-start(bf16[128,1024]{1,0:T(8,128)(2,1)S(1)} %collective-permute-done.1) | copy-start | bytes 786436
  142.2 8.0 %collective-permute-start.2 = (bf16[128,1024]{1,0:T(8,128)(2,1)S(1)}, bf16[128,1024]{1,0:T(8,128)(2,1)}, u32[]{:S(2)}, u32[]{:S(2)}) collective-permute-start(bf16[128,1024]{1,0:T(8,128)(2,1)S(1)} %collective-permute-done.1), channel_id=1, source_target_pairs={{0,4},{4,8},{8,12},{12,16},{16,20},{20,24},{24,28},{1,5},{5,9},{9,... | collective-permute-start | bytes 786440 | tf_op jit(solution)/shard_map/ppermute | solution.py:18
  150.2 9.4 %collective-permute-start.3 = (bf16[128,1024]{1,0:T(8,128)(2,1)}, bf16[128,1024]{1,0:T(8,128)(2,1)}, u32[]{:S(2)}, u32[]{:S(2)}) collective-permute-start(bf16[128,1024]{1,0:T(8,128)(2,1)} %collective-permute-done.2), channel_id=1, source_target_pairs={{0,4},{4,8},{8,12},{12,16},{16,20},{20,24},{24,28},{1,5},{5,9},{9,... | collective-permute-start | bytes 786440 | tf_op jit(solution)/shard_map/ppermute | solution.py:18
  155.8 15.8 %copy-start.2 = (bf16[1,128,4096]{1,2,0:T(8,128)(2,1)}, bf16[1,128,4096]{1,2,0:T(8,128)(2,1)S(1)}, u32[]{:S(2)}) copy-start(bf16[1,128,4096]{1,2,0:T(8,128)(2,1)S(1)} %copy.64) | copy-start | bytes 3145732
  180.4 5.4 %copy-start.4 = (bf16[128,4,8,128]{0,3,2,1:T(8,128)(2,1)S(1)}, bf16[128,4,8,128]{0,3,2,1:T(8,128)(2,1)}, u32[]{:S(2)}) copy-start(bf16[128,4,8,128]{0,3,2,1:T(8,128)(2,1)} %copy.35) | copy-start | bytes 3145732
  185.7 1.7 copy-start.6
  197.3 6.7 %copy-start.3 = (bf16[1,128,4096]{1,2,0:T(8,128)(2,1)S(1)}, bf16[1,128,4096]{1,2,0:T(8,128)(2,1)}, u32[]{:S(2)}) copy-start(bf16[1,128,4096]{1,2,0:T(8,128)(2,1)} %copy-done.2) | copy-start | bytes 3145732
  204.0 2.4 copy-start.1
  206.5 10.8 %collective-permute-start.4 = (f32[128,1024]{0,1:T(8,128)S(1)}, f32[128,1024]{0,1:T(8,128)S(1)}, u32[]{:S(2)}, u32[]{:S(2)}) collective-permute-start(f32[128,1024]{0,1:T(8,128)S(1)} %fusion.18), channel_id=1, source_target_pairs={{4,0},{8,4},{12,8},{16,12},{20,16},{24,20},{28,24},{5,1},{9,5},{13... | collective-permute-start | bytes 1572872 | tf_op jit(solution)/shard_map/ppermute | solution.py:18
  217.4 11.7 %collective-permute-start.5 = (f32[128,1024]{0,1:T(8,128)S(1)}, f32[128,1024]{0,1:T(8,128)S(1)}, u32[]{:S(2)}, u32[]{:S(2)}) collective-permute-start(f32[128,1024]{0,1:T(8,128)S(1)} %fusion.20), channel_id=1, source_target_pairs={{4,0},{8,4},{12,8},{16,12},{20,16},{24,20},{28,24},{5,1},{9,5},{13... | collective-permute-start | bytes 1572872 | tf_op jit(solution)/shard_map/ppermute | solution.py:18
  229.1 12.6 %collective-permute-start.6 = (f32[128,1024]{0,1:T(8,128)S(1)}, f32[128,1024]{0,1:T(8,128)S(1)}, u32[]{:S(2)}, u32[]{:S(2)}) collective-permute-start(f32[128,1024]{0,1:T(8,128)S(1)} %fusion.22), channel_id=1, source_target_pairs={{4,0},{8,4},{12,8},{16,12},{20,16},{24,20},{28,24},{5,1},{9,5},{13... | collective-permute-start | bytes 1572872 | tf_op jit(solution)/shard_map/ppermute | solution.py:18
  241.8 11.5 %collective-permute-start.7 = (f32[128,1024]{0,1:T(8,128)S(1)}, f32[128,1024]{0,1:T(8,128)S(1)}, u32[]{:S(2)}, u32[]{:S(2)}) collective-permute-start(f32[128,1024]{0,1:T(8,128)S(1)} %fusion.17), channel_id=1, source_target_pairs={{4,0},{8,4},{12,8},{16,12},{20,16},{24,20},{28,24},{5,1},{9,5},{13... | collective-permute-start | bytes 1572872 | tf_op jit(solution)/shard_map/ppermute | solution.py:18
  262.2 195.5 %copy-start.5 = (bf16[4,128,8,128]{3,1,2,0:T(8,128)(2,1)S(1)}, bf16[4,128,8,128]{3,1,2,0:T(8,128)(2,1)}, u32[]{:S(2)}) copy-start(bf16[4,128,8,128]{3,1,2,0:T(8,128)(2,1)} %get-tuple-element.17) | copy-start | bytes 3145732
  262.2 196.8 %copy-start.7 = (bf16[640,4,128,1]{0,2,3,1:T(8,128)(2,1)S(1)}, bf16[640,4,128,1]{0,2,3,1:T(8,128)(2,1)}, u32[]{:S(2)}) copy-start(bf16[640,4,128,1]{0,2,3,1:T(8,128)(2,1)} %copy.50) | copy-start | bytes 1966084
  262.2 208.9 %all-gather.5.cloned.1.call-start = ((), (), s32[]{:S(2)}) async-start(), calls=%async_computation.3 | async-start | bytes 1572864 | tf_op jit(solution)/shard_map/all_gather | solution.py:125
  457.7 6.1 %copy-start.9 = (bf16[128,1024]{0,1:T(8,128)(2,1)S(1)}, bf16[128,1024]{0,1:T(8,128)(2,1)}, u32[]{:S(2)}) copy-start(bf16[128,1024]{0,1:T(8,128)(2,1)} %copy-done.8) | copy-start | bytes 786436
  (1 other events, 0.7 us)
Sparse Core Ops, SparseCore 0:
  10.7 110.3 all-gather.2
  262.3 195.2 reduce-scatter.1
  459.2 10.7 all-gather.4
where the time goes:
time: 483 us; the launch traced here: 480 us
  waiting for transfers between devices  358 us (74%)
  matrix products  45.2 us (9%)
  starting transfers between devices  26.5 us (5%)
  local copies, waits for them, and re-layouts  25.6 us (5%)
  between operations  14.1 us (3%)
  other arithmetic  10.4 us (2%)
    reduce_scatter x1, waiting for transfers between devices, per_device(): lax.psum_scatter(lax.dot_general(rows_in, grad_kv, (((0,), (0,)), ((), ()...  195 us
    all_gather x1, waiting for transfers between devices, per_device(): whole_weights = lax.all_gather(w_kv, ('ctx', 'fsdp'), axis=0, tiled=True)  113 us
    ppermute x8, waiting for transfers between devices, passed_along(): return lax.ppermute(x, axis, pairs)  49.2 us
    ppermute x8, starting transfers between devices, passed_along(): return lax.ppermute(x, axis, pairs)  26.4 us
    unnamed x37, local copies, waits for them, and re-layouts  14.1 us
  transfers between devices with their start and end apart: 11, of which 9 were waited for; matrix products, arithmetic and copies ran while one was open for 4% of the time, Pallas kernels for 0%

commit v1 on v0

v1 whole, which is shorter than its diff:
```python
import functools
import math

import jax
import jax.numpy as jnp
from jax import lax
from jax.experimental import pallas as pl
from jax.experimental.pallas import tpu as pltpu
from jax.sharding import PartitionSpec as P

HEADS = 32
KV_HEADS = 4
HEAD_DIM = 128
BLOCK = 128
REACH = 4
GROUPS = HEADS // KV_HEADS
INNER = 2

NT = (((1,), (1,)), ((), ()))
NN = (((1,), (0,)), ((), ()))
TN = (((0,), (0,)), ((), ()))


def dot(a, b, dims):
    return lax.dot_general(a, b, dims, preferred_element_type=jnp.float32)


def attend_kernel(flags, q_ref, g_ref, *refs):
    pieces = refs[: REACH + 1]
    o_ref, dq_ref, far_ref, near_ref, bias, acc_k, acc_v = refs[REACH + 1 :]
    tok = q_ref.shape[0]
    scale = 1.0 / math.sqrt(HEAD_DIM)
    scale_log2 = scale * math.log2(math.e)

    @pl.when(pl.program_id(0) == 0)
    def _():
        row = lax.broadcasted_iota(jnp.int32, (2 * tok, BLOCK), 0) % tok
        col = lax.broadcasted_iota(jnp.int32, (2 * tok, BLOCK), 1)
        for j in range(REACH):
            flag = jnp.full((2 * tok, BLOCK), flags[0, REACH - 1 - j], jnp.int32)
            bias[:, j * BLOCK : (j + 1) * BLOCK] = jnp.where(flag > 0, 0.0, -jnp.inf)
        bias[:, REACH * BLOCK :] = jnp.where(col <= row, 0.0, -jnp.inf)

    k = jnp.concatenate([p[0] for p in pieces], axis=0)
    v = jnp.concatenate([p[1] for p in pieces], axis=0)
    pairs = GROUPS // 2
    for p in range(pairs):
        lo = slice(2 * p * HEAD_DIM, (2 * p + 1) * HEAD_DIM)
        hi = slice((2 * p + 1) * HEAD_DIM, (2 * p + 2) * HEAD_DIM)
        q2 = jnp.concatenate([q_ref[:, lo], q_ref[:, hi]], axis=0)
        g2 = jnp.concatenate([g_ref[:, lo], g_ref[:, hi]], axis=0)
        s = dot(q2, k, NT) * scale_log2 + bias[...]
        top = jnp.max(s, axis=1, keepdims=True)
        e = jnp.exp2(s - top)
        share = e * (1.0 / jnp.sum(e, axis=1, keepdims=True))
        prob = share.astype(jnp.bfloat16)
        o = dot(prob, v, NN).astype(jnp.bfloat16)
        o_ref[:, lo] = o[:tok]
        o_ref[:, hi] = o[tok:]
        delta = jnp.sum(g2.astype(jnp.float32) * o.astype(jnp.float32), axis=1, keepdims=True)
        dp = dot(g2, v, NT)
        ds = (share * ((dp - delta) * scale)).astype(jnp.bfloat16)
        dq = dot(ds, k, NN).astype(jnp.bfloat16)
        dq_ref[:, lo] = dq[:tok]
        dq_ref[:, hi] = dq[tok:]
        part_k = dot(q2, ds, TN)
        part_v = dot(g2, prob, TN)
        if p == 0:
            acc_k[...] = part_k
            acc_v[...] = part_v
        elif p < pairs - 1:
            acc_k[...] += part_k
            acc_v[...] += part_v
        else:
            for slot, total in ((0, (acc_k[...] + part_k).T), (1, (acc_v[...] + part_v).T)):
                for j in range(REACH):
                    far_ref[j, slot] = total[j * BLOCK : (j + 1) * BLOCK].astype(jnp.bfloat16)
                near_ref[slot] = total[REACH * BLOCK :]


def attend(queries, grads, pieces, flags):
    tok = queries.shape[0]
    key_width = pieces[0].shape[2]
    wide = pl.BlockSpec((tok, GROUPS * HEAD_DIM), lambda i: (0, i))
    piece = pl.BlockSpec((2, tok, HEAD_DIM), lambda i: (0, 0, i))
    win = (REACH + 1) * tok
    return pl.pallas_call(
        attend_kernel,
        grid=(key_width // HEAD_DIM,),
        in_specs=[pl.BlockSpec(memory_space=pltpu.SMEM), wide, wide] + [piece] * (REACH + 1),
        out_specs=[wide, wide, pl.BlockSpec((REACH, 2, tok, HEAD_DIM), lambda i: (0, 0, 0, i)), piece],
        out_shape=[
            jax.ShapeDtypeStruct(queries.shape, jnp.bfloat16),
            jax.ShapeDtypeStruct(queries.shape, jnp.bfloat16),
            jax.ShapeDtypeStruct((REACH, 2, tok, key_width), jnp.bfloat16),
            jax.ShapeDtypeStruct((2, tok, key_width), jnp.float32),
        ],
        scratch_shapes=[
            pltpu.VMEM((2 * tok, win), jnp.float32),
            pltpu.VMEM((HEAD_DIM, win), jnp.float32),
            pltpu.VMEM((HEAD_DIM, win), jnp.float32),
        ],
        compiler_params=pltpu.CompilerParams(vmem_limit_bytes=40 << 20),
        name="attend",
    )(flags, queries, grads, *pieces)


def along(x, by):
    peers = lax.axis_size("ctx")
    return lax.ppermute(x, "ctx", [(i, i + by) for i in range(peers) if 0 <= i + by < peers])


def outer_shift(x, by):
    peers = lax.axis_size("ctx")
    return lax.ppermute(x, "ctx", [(i, (i + INNER * by) % peers) for i in range(peers)])


def swap_inner(x):
    return lax.ppermute(x, "ctx", [(i, i ^ 1) for i in range(lax.axis_size("ctx"))])


def swap_fsdp(x):
    return lax.ppermute(x, "fsdp", [(0, 1), (1, 0)])


def swap_core(x):
    return lax.ppermute(x, "dp", [(0, 1), (1, 0)])


def part(x, index, size, axis):
    return lax.dynamic_slice_in_dim(x, index * size, size, axis)


def per_device(inputs, queries, w_kv, tile_mask, grad_out):
    rows_in = inputs[0]
    tok, width = rows_in.shape
    rows, pair_width = w_kv.shape
    half = pair_width // 2
    ctx, fsdp, core = (lax.axis_index(a) for a in ("ctx", "fsdp", "dp"))
    outer = lax.axis_size("ctx") // INNER
    z, x = ctx // INNER, ctx % INNER

    own = part(w_kv, core, half, 1)
    cols = [own] + [outer_shift(own, r) for r in range(1, outer)]
    rows_both = jnp.concatenate([rows_in, swap_core(rows_in)], axis=0)
    kv_sum = None
    weights = []
    for r, col in enumerate(cols):
        by_x, by_y = swap_inner(col), swap_fsdp(col)
        diag_top = swap_fsdp(by_x[: rows // 2])
        diag_bottom = swap_inner(by_y[rows // 2 :])
        blocks = jnp.concatenate([col, by_y, by_x, diag_top, diag_bottom], axis=0)
        weights.append(blocks)
        zr = (z - r) % outer
        lhs = jnp.concatenate(
            [
                part(rows_both, (zr * INNER + (x ^ a)) * 2 + (fsdp ^ b), rows, 1)
                for a in range(2)
                for b in range(2)
            ],
            axis=1,
        )
        term = dot(lhs, blocks, NN)
        kv_sum = term if kv_sum is None else kv_sum + term
    kv = kv_sum.astype(jnp.bfloat16)
    mine, theirs = kv[:tok], swap_core(kv[tok:])
    key_vals = jnp.where(core == 0, jnp.stack([mine, theirs]), jnp.stack([theirs, mine]))
    weight_half = jnp.concatenate(weights, axis=0)
    weight_other = swap_core(weight_half)

    pieces = [along(key_vals, s) for s in range(REACH, 0, -1)] + [key_vals]
    attended, grad_query, far, near = attend(queries[0], grad_out[0], pieces, tile_mask)
    total = near
    for s in range(1, REACH + 1):
        total = total + along(far[REACH - s], -s).astype(jnp.float32)
    grad_kv = total.astype(jnp.bfloat16)
    grad_mine = jnp.where(core == 0, grad_kv[0], grad_kv[1])
    grad_theirs = jnp.where(core == 0, grad_kv[1], grad_kv[0])

    grad_rel = (dot(grad_mine, weight_half, NT) + dot(grad_theirs, weight_other, NT)).astype(
        jnp.bfloat16
    )
    spots = [
        ((z - zz) % outer * INNER + (x ^ xx)) * 2 + (fsdp ^ yy)
        for zz in range(outer)
        for xx in range(2)
        for yy in range(2)
    ]
    grad_in = jnp.concatenate([part(grad_rel, s, rows, 1) for s in spots], axis=1)

    block = width // outer
    in_cols = [part(rows_in, z, block, 1)] + [
        outer_shift(part(rows_in, (z + r) % outer, block, 1), r) for r in range(1, outer)
    ]
    in_mine = jnp.stack(in_cols)
    in_other = swap_core(in_mine)
    grad_pair = jnp.concatenate([grad_mine, swap_core(grad_theirs)], axis=0)
    tile = None
    for r in range(outer):
        gathered = grad_pair if r == 0 else outer_shift(grad_pair, r)
        term = dot(jnp.concatenate([in_mine[r], in_other[r]], axis=0), gathered, TN)
        tile = term if tile is None else tile + term
    tile = tile.reshape(2, 2, rows, half)
    first, second = tile[..., : half // 2], tile[..., half // 2 :]

    def pick(t, index, axis):
        return lax.dynamic_index_in_dim(t, index, axis, keepdims=False)

    def sent(t, swap):
        return swap(t.astype(jnp.bfloat16)).astype(jnp.float32)

    first = pick(first, x, 0) + sent(pick(first, 1 - x, 0), swap_inner)
    second = pick(second, fsdp, 1) + sent(pick(second, 1 - fsdp, 1), swap_fsdp)
    first = pick(first, fsdp, 0) + sent(pick(first, 1 - fsdp, 0), swap_fsdp)
    second = pick(second, x, 0) + sent(pick(second, 1 - x, 0), swap_inner)
    tokens = lax.axis_size("fsdp") * lax.axis_size("dp") * lax.axis_size("ctx") * tok
    grad_half = jnp.concatenate([first, second], axis=1) * (1.0 / math.sqrt(tokens))
    grad_rest = swap_core(grad_half)
    weight_grad = jnp.where(
        core == 0,
        jnp.concatenate([grad_half, grad_rest], axis=1),
        jnp.concatenate([grad_rest, grad_half], axis=1),
    )
    return (attended[None], grad_query[None], grad_in[None], weight_grad)


def solution(mesh):
    return jax.shard_map(
        per_device,
        mesh=mesh,
        in_specs=(
            P(("fsdp", "dp"), "ctx", None),
            P(("fsdp", "dp"), "ctx", None),
            P(("ctx", "fsdp"), None),
            P("ctx", None),
            P(("fsdp", "dp"), "ctx", None),
        ),
        out_specs=(
            P(("fsdp", "dp"), "ctx", None),
            P(("fsdp", "dp"), "ctx", None),
            P(("fsdp", "dp"), "ctx", None),
            P(("ctx", "fsdp"), None),
        ),
        check_vma=False,
    )
```

time: 483 us -> 208 us (0.43)
  waiting for transfers between devices: 358 us -> 96.2 us
  matrix products: 45.2 us -> 8.8 us
  starting transfers between devices: 26.5 us -> 56.9 us
  Pallas kernels: 0 us -> 17.6 us
  between operations: 14.1 us -> 1.32 us
  other arithmetic: 10.4 us -> 4.01 us
    reduce_scatter x1 -> x0, waiting for transfers between devices: 195 us -> none  [per_device(): lax.psum_scatter(lax.dot_general(rows_in, grad_kv, (((0,), (0,)), ((), ()...]
    all_gather x2 -> x0, waiting for transfers between devices: 113 us -> none  [the longest x1 113 us: per_device(): whole_weights = lax.all_gather(w_kv, ('ctx', 'fsdp'), axis=0, tiled=True)]
    ppermute x8 -> x43, waiting for transfers between devices: 49.2 us -> 96.2 us  [the longest x8 50.7 us: along(): lax.ppermute(x, 'ctx', [(i, i + by) for i in range(peers) if 0 <= i + by...]
    ppermute x8 -> x43, starting transfers between devices: 26.4 us -> 56.9 us  [the longest x8 16.4 us: along(): lax.ppermute(x, 'ctx', [(i, i + by) for i in range(peers) if 0 <= i + by...]
    dot_general x8 -> x10, matrix products: 36.3 us -> 8.8 us  [dot(): return lax.dot_general(a, b, dims, preferred_element_type=jnp.float32)]
    pallas_call x0 -> x1, Pallas kernels: none -> 17.6 us  [attend(): pl.pallas_call(attend_kernel, grid=(key_width // HEAD_DIM,), in_specs=[pl...]
    sub x1 -> x0, matrix products: 8.83 us -> none  [attend(): weights = jnp.where(allowed, jnp.exp(scores - row_top), 0.0)]
    reshape x3 -> x0, local copies, waits for them, and re-layouts: 6.82 us -> none  [the longest x2 4.49 us: attend(): key_heads = window[:, :key_width].reshape(win_rows, KV_HEADS, HEAD_DIM)]
  transfers between devices with their start and end apart: 11 -> 43, of which waited for: 9 -> 21; matrix products, arithmetic and copies ran while one was open for 4% -> 13% of each run, Pallas kernels for 0% -> 8%
where the time goes in v1:
time: 208 us
  waiting for transfers between devices  96.2 us (46%)
  starting transfers between devices  56.9 us (27%)
  local copies, waits for them, and re-layouts  22.9 us (11%)
  Pallas kernels  17.6 us (8%)
  matrix products  8.8 us (4%)
  other arithmetic  4.01 us (2%)
    ppermute x8, waiting for transfers between devices, along(): lax.ppermute(x, 'ctx', [(i, i + by) for i in range(peers) if 0 <= i + by...  50.7 us
    ppermute x9, waiting for transfers between devices, outer_shift(): lax.ppermute(x, 'ctx', [(i, (i + INNER * by) % peers) for i in range(peer...  30.9 us
    unnamed x67, local copies, waits for them, and re-layouts  18.8 us
    pallas_call x1, Pallas kernels, attend(): pl.pallas_call(attend_kernel, grid=(key_width // HEAD_DIM,), in_specs=[pl...  17.6 us
    ppermute x8, starting transfers between devices, along(): lax.ppermute(x, 'ctx', [(i, i + by) for i in range(peers) if 0 <= i + by...  16.4 us
    ppermute x6, starting transfers between devices, swap_core(): return lax.ppermute(x, 'dp', [(0, 1), (1, 0)])  16.3 us
    ppermute x10, starting transfers between devices, swap_inner(): lax.ppermute(x, 'ctx', [(i, i ^ 1) for i in range(lax.axis_size('ctx'))])  8.88 us
    dot_general x10, matrix products, dot(): return lax.dot_general(a, b, dims, preferred_element_type=jnp.float32)  8.8 us
  transfers between devices with their start and end apart: 43, of which 21 were waited for; matrix products, arithmetic and copies ran while one was open for 13% of the time, Pallas kernels for 8%

profile of v1, /device:TPU:11, one launch (start us, length us, event | category | flops | bytes accessed | tf_op | source)
XLA Modules:
  0.0 207.7 jit_solution(11091856691503018484)
XLA Ops:
  8.3 2.2 %constant_dynamic-slice_fusion = (bf16[1,128,1024]{2,1,0:T(8,128)(2,1)S(1)}, bf16[128,1024]{1,0:T(8,128)(2,1)S(1)}, bf16[128,1024]{1,0:T(8,128)(2,1)}, bf16[128,1024]{1,0:T(8,128)(2,1)}) fusion(bf16[1,128,4096]{2,1,0:T(8,128)(2,1)} %param.5, s32[]{:T(128)S(6)} %select_n.234, s32[]{:T(128)S(6)} %select_n.236, s32[]{:T(128)S(6)} %select_n.240, s32[]{:T(128)S(6)} %select_n.238), kind=kLoop, calls=%fused_computation.190 | loop fusion | bytes 2097168 | tf_op jit(solution)/shard_map/dynamic_slice | solution.py:131
  14.0 12.4 %collective-permute-done.10 = bf16[256,512]{1,0:T(8,128)(2,1)S(1)} collective-permute-done((bf16[256,512]{1,0:T(8,128)(2,1)S(1)}, bf16[256,512]{1,0:T(8,128)(2,1)S(1)}, u32[]{:S(2)}, u32[]{:S(2)}) %collective-permute-start.10) | collective-permute-done | bytes 262176 | tf_op jit(solution)/shard_map/ppermute | solution.py:115
  38.2 5.1 %collective-permute-start = (bf16[128,4096]{1,0:T(8,128)(2,1)S(1)}, bf16[128,4096]{1,0:T(8,128)(2,1)S(1)}, u32[]{:S(2)}, u32[]{:S(2)}) collective-permute-start(bf16[128,4096]{1,0:T(8,128)(2,1)S(1)} %bitcast.75), channel_id=1, source_target_pairs={{0,1},{1,0},{2,3},{3,2},{4,5},{5,4},{6,7},{7,6},{8,9},{9,8},{10,11... | collective-permute-start | bytes 3145736 | tf_op jit(solution)/shard_map/ppermute | solution.py:127
  43.4 3.2 %collective-permute-start.31 = (bf16[128,1024]{1,0:T(8,128)(2,1)}, bf16[128,1024]{1,0:T(8,128)(2,1)S(1)}, u32[]{:S(2)}, u32[]{:S(2)}) collective-permute-start(bf16[128,1024]{1,0:T(8,128)(2,1)} %get-tuple-element.39), channel_id=1, source_target_pairs={{0,16},{4,20},{8,24},{12,28},{16,0},{20,4},{24,8},{28,12},{1,17},{... | collective-permute-start | bytes 786440 | tf_op jit(solution)/shard_map/ppermute | solution.py:115
  62.4 6.2 %collective-permute-start.20 = (bf16[128,512]{1,0:T(8,128)(2,1)}, bf16[128,512]{1,0:T(8,128)(2,1)}, u32[]{:S(2)}, u32[]{:S(2)}) collective-permute-start(bf16[128,512]{1,0:T(8,128)(2,1)} %get-tuple-element.69), channel_id=1, source_target_pairs={{0,1},{1,0},{2,3},{3,2},{4,5},{5,4},{6,7},{7,6},{8,9},{9,8},{10,11... | collective-permute-start | bytes 393224 | tf_op jit(solution)/shard_map/ppermute | solution.py:127
  71.0 3.0 %collective-permute-start.21 = (bf16[2,128,512]{2,1,0:T(8,128)(2,1)S(1)}, bf16[2,128,512]{2,1,0:T(8,128)(2,1)S(1)}, u32[]{:S(2)}, u32[]{:S(2)}) collective-permute-start(bf16[2,128,512]{2,1,0:T(8,128)(2,1)S(1)} %maximum_select_fusion.1.refs_4_), channel_id=1, source_target_pairs={{0,16},{4,20},{8,24},{12,28},{1,17},{5,21},{9,25},{13,29},{2,18},{... | collective-permute-start | bytes 786440 | tf_op jit(solution)/shard_map/ppermute | solution.py:110
  75.9 1.9 collective-permute-start.23
  77.9 2.5 %collective-permute-start.24 = (bf16[2,128,512]{2,1,0:T(8,128)(2,1)S(1)}, bf16[2,128,512]{2,1,0:T(8,128)(2,1)S(1)}, u32[]{:S(2)}, u32[]{:S(2)}) collective-permute-start(bf16[2,128,512]{2,1,0:T(8,128)(2,1)S(1)} %maximum_select_fusion.1.refs_4_), channel_id=1, source_target_pairs={{0,4},{4,8},{8,12},{12,16},{16,20},{20,24},{24,28},{1,5},{5,9},{9,... | collective-permute-start | bytes 786440 | tf_op jit(solution)/shard_map/ppermute | solution.py:110
  83.1 8.1 %collective-permute-done.21.refs_0_ = bf16[2,128,512]{2,1,0:T(8,128)(2,1)S(1)} collective-permute-done((bf16[2,128,512]{2,1,0:T(8,128)(2,1)S(1)}, bf16[2,128,512]{2,1,0:T(8,128)(2,1)S(1)}, u32[]{:S(2)}, u32[]{:S(2)}) %collective-permute-start.21) | collective-permute-done | bytes 262176 | tf_op jit(solution)/shard_map/ppermute | solution.py:110
  91.2 5.6 %collective-permute-done.22.refs_1_ = bf16[2,128,512]{2,1,0:T(8,128)(2,1)S(1)} collective-permute-done((bf16[2,128,512]{2,1,0:T(8,128)(2,1)S(1)}, bf16[2,128,512]{2,1,0:T(8,128)(2,1)S(1)}, u32[]{:S(2)}, u32[]{:S(2)}) %collective-permute-start.22) | collective-permute-done | bytes 262176 | tf_op jit(solution)/shard_map/ppermute | solution.py:110
  96.8 5.6 %collective-permute-done.23.refs_2_ = bf16[2,128,512]{2,1,0:T(8,128)(2,1)S(1)} collective-permute-done((bf16[2,128,512]{2,1,0:T(8,128)(2,1)S(1)}, bf16[2,128,512]{2,1,0:T(8,128)(2,1)S(1)}, u32[]{:S(2)}, u32[]{:S(2)}) %collective-permute-start.23) | collective-permute-done | bytes 262176 | tf_op jit(solution)/shard_map/ppermute | solution.py:110
  102.4 5.6 %collective-permute-done.24.refs_3_ = bf16[2,128,512]{2,1,0:T(8,128)(2,1)S(1)} collective-permute-done((bf16[2,128,512]{2,1,0:T(8,128)(2,1)S(1)}, bf16[2,128,512]{2,1,0:T(8,128)(2,1)S(1)}, u32[]{:S(2)}, u32[]{:S(2)}) %collective-permute-start.24) | collective-permute-done | bytes 262176 | tf_op jit(solution)/shard_map/ppermute | solution.py:110
  108.1 17.6 %attend.1 = (bf16[128,4096]{1,0:T(8,128)(2,1)}, bf16[128,4096]{1,0:T(8,128)(2,1)}, bf16[4,2,128,512]{3,2,1,0:T(8,128)(2,1)S(1)}, f32[2,128,512]{2,1,0:T(8,128)S(1)}) custom-call(s32[1,4]{1,0:T(1,128)S(1)} %copy-done.2, bf16[128,4096]{1,0:T(8,128)(2,1)S(1)} %bitcast.73, bf16[128,4096]{1,0:T(8,128)(2,1)S(1)} %bitcast.74, ...), custom_call_target="tpu_custom_call" | custom-call | tf_op jit(solution)/shard_map/attend/pallas_call | solution.py:87
  133.0 2.8 %collective-permute-done.28 = bf16[2,128,512]{2,1,0:T(8,128)(2,1)S(1)} collective-permute-done((bf16[2,128,512]{2,1,0:T(8,128)(2,1)S(1)}, bf16[2,128,512]{2,1,0:T(8,128)(2,1)S(1)}, u32[]{:S(2)}, u32[]{:S(2)}) %collective-permute-start.28) | collective-permute-done | bytes 262176 | tf_op jit(solution)/shard_map/ppermute | solution.py:110
  135.7 2.2 %collective-permute-done.27 = bf16[2,128,512]{2,1,0:T(8,128)(2,1)S(1)} collective-permute-done((bf16[2,128,512]{2,1,0:T(8,128)(2,1)S(1)}, bf16[2,128,512]{2,1,0:T(8,128)(2,1)S(1)}, u32[]{:S(2)}, u32[]{:S(2)}) %collective-permute-start.27) | collective-permute-done | bytes 262176 | tf_op jit(solution)/shard_map/ppermute | solution.py:110
  137.9 8.0 %collective-permute-done.26 = bf16[2,128,512]{2,1,0:T(8,128)(2,1)S(1)} collective-permute-done((bf16[2,128,512]{2,1,0:T(8,128)(2,1)S(1)}, bf16[2,128,512]{2,1,0:T(8,128)(2,1)S(1)}, u32[]{:S(2)}, u32[]{:S(2)}) %collective-permute-start.26) | collective-permute-done | bytes 262176 | tf_op jit(solution)/shard_map/ppermute | solution.py:110
  146.0 12.7 %collective-permute-done.25 = bf16[2,128,512]{2,1,0:T(8,128)(2,1)S(1)} collective-permute-done((bf16[2,128,512]{2,1,0:T(8,128)(2,1)S(1)}, bf16[2,128,512]{2,1,0:T(8,128)(2,1)S(1)}, u32[]{:S(2)}, u32[]{:S(2)}) %collective-permute-start.25) | collective-permute-done | bytes 262176 | tf_op jit(solution)/shard_map/ppermute | solution.py:110
  163.5 6.3 %collective-permute-done.36 = bf16[256,512]{1,0:T(8,128)(2,1)S(1)} collective-permute-done((bf16[256,512]{1,0:T(8,128)(2,1)S(1)}, bf16[256,512]{1,0:T(8,128)(2,1)S(1)}, u32[]{:S(2)}, u32[]{:S(2)}) %collective-permute-start.36) | collective-permute-done | bytes 262176 | tf_op jit(solution)/shard_map/ppermute | solution.py:115
  170.3 7.9 %collective-permute-done.35 = bf16[256,512]{1,0:T(8,128)(2,1)S(1)} collective-permute-done((bf16[256,512]{1,0:T(8,128)(2,1)S(1)}, bf16[256,512]{1,0:T(8,128)(2,1)S(1)}, u32[]{:S(2)}, u32[]{:S(2)}) %collective-permute-start.35) | collective-permute-done | bytes 262176 | tf_op jit(solution)/shard_map/ppermute | solution.py:115
  178.7 3.0 %collective-permute-done.37 = bf16[256,512]{1,0:T(8,128)(2,1)S(1)} collective-permute-done((bf16[256,512]{1,0:T(8,128)(2,1)S(1)}, bf16[256,512]{1,0:T(8,128)(2,1)S(1)}, u32[]{:S(2)}, u32[]{:S(2)}) %collective-permute-start.37) | collective-permute-done | bytes 262176 | tf_op jit(solution)/shard_map/ppermute | solution.py:115
  184.3 5.7 %collective-permute-done.40 = bf16[2,256,256]{2,1,0:T(8,128)(2,1)S(1)} collective-permute-done((bf16[2,256,256]{2,1,0:T(8,128)(2,1)S(1)}, bf16[2,256,256]{2,1,0:T(8,128)(2,1)S(1)}, u32[]{:S(2)}, u32[]{:S(2)}) %collective-permute-start.40) | collective-permute-done | bytes 262176 | tf_op jit(solution)/shard_map/ppermute | solution.py:123
  192.0 2.0 collective-permute-done.41
  195.9 2.5 %collective-permute-start.42 = (f32[256,512]{1,0:T(8,128)S(1)}, f32[256,512]{1,0:T(8,128)S(1)}, u32[]{:S(2)}, u32[]{:S(2)}) collective-permute-start(f32[256,512]{1,0:T(8,128)S(1)} %maximum_multiply_fusion), channel_id=1, source_target_pairs={{0,1},{1,0},{2,3},{3,2},{4,5},{5,4},{6,7},{7,6},{8,9},{9,8},{10,11... | collective-permute-start | bytes 1572872 | tf_op jit(solution)/shard_map/ppermute | solution.py:127
  201.1 3.7 %fusion.82 = f32[128,4096]{1,0:T(8,128)S(1)} fusion(bf16[128,512]{1,0:T(8,128)(2,1)S(1)} %copy-done.12, bf16[4096,512]{1,0:T(8,128)(2,1)} %collective-permute-done.29), kind=kOutput, calls=%fused_computation.201 | convolution fusion | flops 536870912 | bytes 6422528 | tf_op jit(solution)/shard_map/dot_general | solution.py:25
  (173 shorter events, 70.7 us)
Async XLA Ops:
  5.1 21.3 %collective-permute-start.10 = (bf16[256,512]{1,0:T(8,128)(2,1)S(1)}, bf16[256,512]{1,0:T(8,128)(2,1)S(1)}, u32[]{:S(2)}, u32[]{:S(2)}) collective-permute-start(bf16[256,512]{1,0:T(8,128)(2,1)S(1)} %get-tuple-element.13), channel_id=1, source_target_pairs={{0,16},{4,20},{8,24},{12,28},{16,0},{20,4},{24,8},{28,12},{1,17},{... | collective-permute-start | bytes 786440 | tf_op jit(solution)/shard_map/ppermute | solution.py:115
  6.1 23.7 %collective-permute-start.15 = (bf16[256,512]{1,0:T(8,128)(2,1)S(1)}, bf16[256,512]{1,0:T(8,128)(2,1)S(1)}, u32[]{:S(2)}, u32[]{:S(2)}) collective-permute-start(bf16[256,512]{1,0:T(8,128)(2,1)S(1)} %get-tuple-element.13), channel_id=1, source_target_pairs={{0,24},{4,28},{8,0},{12,4},{16,8},{20,12},{24,16},{28,20},{1,25},{... | collective-permute-start | bytes 786440 | tf_op jit(solution)/shard_map/ppermute | solution.py:115
  10.5 16.1 %collective-permute-start.3 = (bf16[128,512]{1,0:T(8,128)(2,1)S(1)}, bf16[128,512]{1,0:T(8,128)(2,1)S(1)}, u32[]{:S(2)}, u32[]{:S(2)}) collective-permute-start(bf16[128,512]{1,0:T(8,128)(2,1)S(1)} %slice.90), channel_id=1, source_target_pairs={{0,2},{2,0},{1,3},{3,1},{4,6},{6,4},{5,7},{7,5},{8,10},{10,8},{9,1... | collective-permute-start | bytes 393224 | tf_op jit(solution)/shard_map/ppermute | solution.py:123
  10.9 20.2 %collective-permute-start.4 = (bf16[128,512]{1,0:T(8,128)(2,1)S(1)}, bf16[128,512]{1,0:T(8,128)(2,1)S(1)}, u32[]{:S(2)}, u32[]{:S(2)}) collective-permute-start(bf16[128,512]{1,0:T(8,128)(2,1)S(1)} %slice.91), channel_id=1, source_target_pairs={{0,4},{4,0},{8,12},{12,8},{16,20},{20,16},{24,28},{28,24},{1,5},{5... | collective-permute-start | bytes 393224 | tf_op jit(solution)/shard_map/ppermute | solution.py:119
  12.1 19.9 %collective-permute-start.7 = (bf16[256,512]{1,0:T(8,128)(2,1)S(1)}, bf16[256,512]{1,0:T(8,128)(2,1)S(1)}, u32[]{:S(2)}, u32[]{:S(2)}) collective-permute-start(bf16[256,512]{1,0:T(8,128)(2,1)S(1)} %collective-permute-done.5), channel_id=1, source_target_pairs={{0,4},{4,0},{8,12},{12,8},{16,20},{20,16},{24,28},{28,24},{1,5},{5... | collective-permute-start | bytes 786440 | tf_op jit(solution)/shard_map/ppermute | solution.py:119
  26.6 11.6 %collective-permute-start.11 = (bf16[256,512]{1,0:T(8,128)(2,1)S(1)}, bf16[256,512]{1,0:T(8,128)(2,1)S(1)}, u32[]{:S(2)}, u32[]{:S(2)}) collective-permute-start(bf16[256,512]{1,0:T(8,128)(2,1)S(1)} %collective-permute-done.10), channel_id=1, source_target_pairs={{0,2},{2,0},{1,3},{3,1},{4,6},{6,4},{5,7},{7,5},{8,10},{10,8},{9,1... | collective-permute-start | bytes 786440 | tf_op jit(solution)/shard_map/ppermute | solution.py:123
  31.0 12.4 %collective-permute-start.16 = (bf16[256,512]{1,0:T(8,128)(2,1)S(1)}, bf16[256,512]{1,0:T(8,128)(2,1)S(1)}, u32[]{:S(2)}, u32[]{:S(2)}) collective-permute-start(bf16[256,512]{1,0:T(8,128)(2,1)S(1)} %collective-permute-done.15), channel_id=1, source_target_pairs={{0,2},{2,0},{1,3},{3,1},{4,6},{6,4},{5,7},{7,5},{8,10},{10,8},{9,1... | collective-permute-start | bytes 786440 | tf_op jit(solution)/shard_map/ppermute | solution.py:123
  32.0 11.4 %collective-permute-start.17 = (bf16[256,512]{1,0:T(8,128)(2,1)S(1)}, bf16[256,512]{1,0:T(8,128)(2,1)S(1)}, u32[]{:S(2)}, u32[]{:S(2)}) collective-permute-start(bf16[256,512]{1,0:T(8,128)(2,1)S(1)} %collective-permute-done.15), channel_id=1, source_target_pairs={{0,4},{4,0},{8,12},{12,8},{16,20},{20,16},{24,28},{28,24},{1,5},{5... | collective-permute-start | bytes 786440 | tf_op jit(solution)/shard_map/ppermute | solution.py:119
  33.0 13.6 %collective-permute-start.8 = (bf16[128,512]{1,0:T(8,128)(2,1)S(1)}, bf16[128,512]{1,0:T(8,128)(2,1)S(1)}, u32[]{:S(2)}, u32[]{:S(2)}) collective-permute-start(bf16[128,512]{1,0:T(8,128)(2,1)S(1)} %slice.92), channel_id=1, source_target_pairs={{0,2},{2,0},{1,3},{3,1},{4,6},{6,4},{5,7},{7,5},{8,10},{10,8},{9,1... | collective-permute-start | bytes 393224 | tf_op jit(solution)/shard_map/ppermute | solution.py:123
  36.2 11.4 %collective-permute-start.9 = (bf16[128,512]{1,0:T(8,128)(2,1)S(1)}, bf16[128,512]{1,0:T(8,128)(2,1)S(1)}, u32[]{:S(2)}, u32[]{:S(2)}) collective-permute-start(bf16[128,512]{1,0:T(8,128)(2,1)S(1)} %slice.93), channel_id=1, source_target_pairs={{0,4},{4,0},{8,12},{12,8},{16,20},{20,16},{24,28},{28,24},{1,5},{5... | collective-permute-start | bytes 393224 | tf_op jit(solution)/shard_map/ppermute | solution.py:119
  38.2 21.2 %collective-permute-start = (bf16[128,4096]{1,0:T(8,128)(2,1)S(1)}, bf16[128,4096]{1,0:T(8,128)(2,1)S(1)}, u32[]{:S(2)}, u32[]{:S(2)}) collective-permute-start(bf16[128,4096]{1,0:T(8,128)(2,1)S(1)} %bitcast.75), channel_id=1, source_target_pairs={{0,1},{1,0},{2,3},{3,2},{4,5},{5,4},{6,7},{7,6},{8,9},{9,8},{10,11... | collective-permute-start | bytes 3145736 | tf_op jit(solution)/shard_map/ppermute | solution.py:127
  43.3 32.6 %collective-permute-start.32 = (bf16[128,1024]{1,0:T(8,128)(2,1)}, bf16[128,1024]{1,0:T(8,128)(2,1)S(1)}, u32[]{:S(2)}, u32[]{:S(2)}) collective-permute-start(bf16[128,1024]{1,0:T(8,128)(2,1)} %get-tuple-element.38), channel_id=1, source_target_pairs={{0,24},{4,28},{8,0},{12,4},{16,8},{20,12},{24,16},{28,20},{1,25},{... | collective-permute-start | bytes 786440 | tf_op jit(solution)/shard_map/ppermute | solution.py:115
  43.4 34.4 %collective-permute-start.31 = (bf16[128,1024]{1,0:T(8,128)(2,1)}, bf16[128,1024]{1,0:T(8,128)(2,1)S(1)}, u32[]{:S(2)}, u32[]{:S(2)}) collective-permute-start(bf16[128,1024]{1,0:T(8,128)(2,1)} %get-tuple-element.39), channel_id=1, source_target_pairs={{0,16},{4,20},{8,24},{12,28},{16,0},{20,4},{24,8},{28,12},{1,17},{... | collective-permute-start | bytes 786440 | tf_op jit(solution)/shard_map/ppermute | solution.py:115
  68.7 11.7 %collective-permute-start.30 = (bf16[128,1024]{1,0:T(8,128)(2,1)S(1)}, bf16[128,1024]{1,0:T(8,128)(2,1)S(1)}, u32[]{:S(2)}, u32[]{:S(2)}) collective-permute-start(bf16[128,1024]{1,0:T(8,128)(2,1)S(1)} %get-tuple-element.37), channel_id=1, source_target_pairs={{0,8},{4,12},{8,16},{12,20},{16,24},{20,28},{24,0},{28,4},{1,9},{5... | collective-permute-start | bytes 786440 | tf_op jit(solution)/shard_map/ppermute | solution.py:115
  71.0 20.2 %collective-permute-start.21 = (bf16[2,128,512]{2,1,0:T(8,128)(2,1)S(1)}, bf16[2,128,512]{2,1,0:T(8,128)(2,1)S(1)}, u32[]{:S(2)}, u32[]{:S(2)}) collective-permute-start(bf16[2,128,512]{2,1,0:T(8,128)(2,1)S(1)} %maximum_select_fusion.1.refs_4_), channel_id=1, source_target_pairs={{0,16},{4,20},{8,24},{12,28},{1,17},{5,21},{9,25},{13,29},{2,18},{... | collective-permute-start | bytes 786440 | tf_op jit(solution)/shard_map/ppermute | solution.py:110
  74.0 22.9 %collective-permute-start.22 = (bf16[2,128,512]{2,1,0:T(8,128)(2,1)S(1)}, bf16[2,128,512]{2,1,0:T(8,128)(2,1)S(1)}, u32[]{:S(2)}, u32[]{:S(2)}) collective-permute-start(bf16[2,128,512]{2,1,0:T(8,128)(2,1)S(1)} %maximum_select_fusion.1.refs_4_), channel_id=1, source_target_pairs={{0,12},{4,16},{8,20},{12,24},{16,28},{1,13},{5,17},{9,21},{13,25},... | collective-permute-start | bytes 786440 | tf_op jit(solution)/shard_map/ppermute | solution.py:110
  75.9 26.5 %collective-permute-start.23 = (bf16[2,128,512]{2,1,0:T(8,128)(2,1)S(1)}, bf16[2,128,512]{2,1,0:T(8,128)(2,1)S(1)}, u32[]{:S(2)}, u32[]{:S(2)}) collective-permute-start(bf16[2,128,512]{2,1,0:T(8,128)(2,1)S(1)} %maximum_select_fusion.1.refs_4_), channel_id=1, source_target_pairs={{0,8},{4,12},{8,16},{12,20},{16,24},{20,28},{1,9},{5,13},{9,17},{1... | collective-permute-start | bytes 786440 | tf_op jit(solution)/shard_map/ppermute | solution.py:110
  77.9 30.2 %collective-permute-start.24 = (bf16[2,128,512]{2,1,0:T(8,128)(2,1)S(1)}, bf16[2,128,512]{2,1,0:T(8,128)(2,1)S(1)}, u32[]{:S(2)}, u32[]{:S(2)}) collective-permute-start(bf16[2,128,512]{2,1,0:T(8,128)(2,1)S(1)} %maximum_select_fusion.1.refs_4_), channel_id=1, source_target_pairs={{0,4},{4,8},{8,12},{12,16},{16,20},{20,24},{24,28},{1,5},{5,9},{9,... | collective-permute-start | bytes 786440 | tf_op jit(solution)/shard_map/ppermute | solution.py:110
  82.1 79.3 %collective-permute-start.33 = (bf16[4,128,1024]{2,1,0:T(8,128)(2,1)}, bf16[4,128,1024]{2,1,0:T(8,128)(2,1)S(1)}, u32[]{:S(2)}, u32[]{:S(2)}) collective-permute-start(bf16[4,128,1024]{2,1,0:T(8,128)(2,1)} %pad_maximum_fusion), channel_id=1, source_target_pairs={{0,1},{1,0},{2,3},{3,2},{4,5},{5,4},{6,7},{7,6},{8,9},{9,8},{10,11... | collective-permute-start | bytes 3145736 | tf_op jit(solution)/shard_map/ppermute | solution.py:127
  129.1 16.9 %collective-permute-start.26 = (bf16[2,128,512]{2,1,0:T(8,128)(2,1)S(1)}, bf16[2,128,512]{2,1,0:T(8,128)(2,1)S(1)}, u32[]{:S(2)}, u32[]{:S(2)}) collective-permute-start(bf16[2,128,512]{2,1,0:T(8,128)(2,1)S(1)} %get-tuple-element.43), channel_id=1, source_target_pairs={{8,0},{12,4},{16,8},{20,12},{24,16},{28,20},{9,1},{13,5},{17,9},{2... | collective-permute-start | bytes 786440 | tf_op jit(solution)/shard_map/ppermute | solution.py:110
  131.0 27.6 %collective-permute-start.25 = (bf16[2,128,512]{2,1,0:T(8,128)(2,1)S(1)}, bf16[2,128,512]{2,1,0:T(8,128)(2,1)S(1)}, u32[]{:S(2)}, u32[]{:S(2)}) collective-permute-start(bf16[2,128,512]{2,1,0:T(8,128)(2,1)S(1)} %get-tuple-element.40), channel_id=1, source_target_pairs={{4,0},{8,4},{12,8},{16,12},{20,16},{24,20},{28,24},{5,1},{9,5},{13... | collective-permute-start | bytes 786440 | tf_op jit(solution)/shard_map/ppermute | solution.py:110
  160.3 40.8 %collective-permute-start.29 = (bf16[4096,512]{1,0:T(8,128)(2,1)}, bf16[4096,512]{1,0:T(8,128)(2,1)}, u32[]{:S(2)}, u32[]{:S(2)}) collective-permute-start(bf16[4096,512]{1,0:T(8,128)(2,1)} %get-tuple-element.70), channel_id=1, source_target_pairs={{0,1},{1,0},{2,3},{3,2},{4,5},{5,4},{6,7},{7,6},{8,9},{9,8},{10,11... | collective-permute-start | bytes 12582920 | tf_op jit(solution)/shard_map/ppermute | solution.py:127
  161.5 16.7 %collective-permute-start.35 = (bf16[256,512]{1,0:T(8,128)(2,1)S(1)}, bf16[256,512]{1,0:T(8,128)(2,1)S(1)}, u32[]{:S(2)}, u32[]{:S(2)}) collective-permute-start(bf16[256,512]{1,0:T(8,128)(2,1)S(1)} %pad_maximum_fusion.1), channel_id=1, source_target_pairs={{0,8},{4,12},{8,16},{12,20},{16,24},{20,28},{24,0},{28,4},{1,9},{5... | collective-permute-start | bytes 786440 | tf_op jit(solution)/shard_map/ppermute | solution.py:115
  161.6 20.2 %collective-permute-start.37 = (bf16[256,512]{1,0:T(8,128)(2,1)S(1)}, bf16[256,512]{1,0:T(8,128)(2,1)S(1)}, u32[]{:S(2)}, u32[]{:S(2)}) collective-permute-start(bf16[256,512]{1,0:T(8,128)(2,1)S(1)} %pad_maximum_fusion.1), channel_id=1, source_target_pairs={{0,24},{4,28},{8,0},{12,4},{16,8},{20,12},{24,16},{28,20},{1,25},{... | collective-permute-start | bytes 786440 | tf_op jit(solution)/shard_map/ppermute | solution.py:115
  (35 other events, 435.0 us)

commit v2 on v1

v2 whole, which is shorter than its diff:
```python
import functools
import math

import jax
import jax.numpy as jnp
from jax import lax
from jax.experimental import pallas as pl
from jax.experimental.pallas import tpu as pltpu
from jax.sharding import PartitionSpec as P

HEADS = 32
KV_HEADS = 4
HEAD_DIM = 128
BLOCK = 128
REACH = 4
GROUPS = HEADS // KV_HEADS
INNER = 2

NT = (((1,), (1,)), ((), ()))
NN = (((1,), (0,)), ((), ()))
TN = (((0,), (0,)), ((), ()))


def dot(a, b, dims):
    return lax.dot_general(a, b, dims, preferred_element_type=jnp.float32)


def project_kernel(count, spots, mine_ref, theirs_ref, *refs):
    blocks = refs[:count]
    carry = refs[count] if len(refs) > count + 6 else None
    out_ref, lhs, total, rhs, lhs_sems, rhs_sems = refs[-6:]
    tok = mine_ref.shape[0]
    groups, _, group = lhs.shape
    unit = rhs.shape[2]
    copies, fetches = [], []
    for g in range(groups):
        at = pl.ds(pl.multiple_of(spots[g, 0] * group, group), group)
        for i, src in enumerate((mine_ref, theirs_ref)):
            rows = pl.ds(i * tok, tok)
            copies.append(
                pltpu.make_async_copy(src.at[:, at], lhs.at[g, rows, :], lhs_sems.at[g, i])
            )
            copies[-1].start()
        for kind in range(4):
            j = 4 * g + kind
            fetches.append(pltpu.make_async_copy(blocks[j], rhs.at[g, kind], rhs_sems.at[j]))
            fetches[-1].start()
    if carry is None:
        total[...] = jnp.zeros_like(total)
    else:
        total[...] = carry[...]
    for g in range(groups):
        copies[2 * g].wait()
        copies[2 * g + 1].wait()
        for kind in range(4):
            fetches[4 * g + kind].wait()
            at = pl.ds(pl.multiple_of(spots[g, 1 + kind] * unit, unit), unit)
            total[...] += dot(lhs[g, :, at], rhs[g, kind], NN)
    out_ref[...] = total[...].astype(out_ref.dtype)


def project(spots, mine, theirs, blocks, carry, out_type):
    vmem = pl.BlockSpec(memory_space=pltpu.VMEM)
    hbm = pl.BlockSpec(memory_space=pltpu.HBM)
    extra = [] if carry is None else [carry]
    tok = mine.shape[0]
    rows, half = blocks[0].shape
    groups = len(blocks) // 4
    return pl.pallas_call(
        functools.partial(project_kernel, len(blocks)),
        in_specs=[pl.BlockSpec(memory_space=pltpu.SMEM)]
        + [hbm] * (2 + len(blocks))
        + [vmem] * len(extra),
        out_specs=vmem,
        out_shape=jax.ShapeDtypeStruct((2 * tok, half), out_type),
        scratch_shapes=[
            pltpu.VMEM((groups, 2 * tok, 4 * rows), mine.dtype),
            pltpu.VMEM((2 * tok, half), jnp.float32),
            pltpu.VMEM((groups, 4, rows, half), mine.dtype),
            pltpu.SemaphoreType.DMA((groups, 2)),
            pltpu.SemaphoreType.DMA((len(blocks),)),
        ],
        compiler_params=pltpu.CompilerParams(vmem_limit_bytes=16 << 20),
        name="project",
    )(spots, mine, theirs, *blocks, *extra)


def assemble_kernel(spots, *refs):
    blocks = refs[:-4]
    out_ref, held, sems, out_sem = refs[-4:]
    unit = blocks[0].shape[0]
    copies = []
    for j, block in enumerate(blocks):
        at = pl.ds(pl.multiple_of(spots[j] * unit, unit), unit)
        copies.append(pltpu.make_async_copy(block, held.at[at, :], sems.at[j]))
        copies[-1].start()
    for copy in copies:
        copy.wait()
    write = pltpu.make_async_copy(held, out_ref, out_sem)
    write.start()
    write.wait()


def assemble(spots, blocks):
    hbm = pl.BlockSpec(memory_space=pltpu.HBM)
    rows = sum(b.shape[0] for b in blocks)
    shape = (rows, blocks[0].shape[1])
    return pl.pallas_call(
        assemble_kernel,
        in_specs=[pl.BlockSpec(memory_space=pltpu.SMEM)] + [hbm] * len(blocks),
        out_specs=hbm,
        out_shape=jax.ShapeDtypeStruct(shape, blocks[0].dtype),
        scratch_shapes=[
            pltpu.VMEM(shape, blocks[0].dtype),
            pltpu.SemaphoreType.DMA((len(blocks),)),
            pltpu.SemaphoreType.DMA,
        ],
        compiler_params=pltpu.CompilerParams(vmem_limit_bytes=16 << 20),
        name="assemble",
    )(spots, *blocks)


def attend_kernel(inner, flags, q_ref, g_ref, *refs):
    c_ref, b_ref, e_ref, a_ref, d_ref, own_ref = refs[:6]
    o_ref, dq_ref, far_c, far_be, far_a, far_d, near, bias, acc_k, acc_v = refs[6:]
    tok = q_ref.shape[0]
    scale = 1.0 / math.sqrt(HEAD_DIM)
    scale_log2 = scale * math.log2(math.e)
    even = inner[0] == 0

    @pl.when(pl.program_id(0) == 0)
    def _():
        row = lax.broadcasted_iota(jnp.int32, (2 * tok, BLOCK), 0) % tok
        col = lax.broadcasted_iota(jnp.int32, (2 * tok, BLOCK), 1)
        backs = (
            flags[0, 3],
            jnp.where(even, flags[0, 2], flags[0, 0]),
            flags[0, 1],
            jnp.where(even, flags[0, 0], flags[0, 2]),
        )
        for j, back in enumerate(backs):
            flag = jnp.full((2 * tok, BLOCK), back, jnp.int32)
            bias[:, j * BLOCK : (j + 1) * BLOCK] = jnp.where(flag > 0, 0.0, -jnp.inf)
        bias[:, REACH * BLOCK :] = jnp.where(col <= row, 0.0, -jnp.inf)

    def window(slot):
        either = jnp.where(even, e_ref[slot], b_ref[slot])
        return jnp.concatenate(
            [c_ref[slot], either, a_ref[slot], d_ref[slot], own_ref[slot]], axis=0
        )

    k, v = window(0), window(1)
    pairs = GROUPS // 2
    for p in range(pairs):
        lo = slice(2 * p * HEAD_DIM, (2 * p + 1) * HEAD_DIM)
        hi = slice((2 * p + 1) * HEAD_DIM, (2 * p + 2) * HEAD_DIM)
        q2 = jnp.concatenate([q_ref[:, lo], q_ref[:, hi]], axis=0)
        g2 = jnp.concatenate([g_ref[:, lo], g_ref[:, hi]], axis=0)
        s = dot(q2, k, NT) * scale_log2 + bias[...]
        top = jnp.max(s, axis=1, keepdims=True)
        e = jnp.exp2(s - top)
        share = e * (1.0 / jnp.sum(e, axis=1, keepdims=True))
        prob = share.astype(jnp.bfloat16)
        o = dot(prob, v, NN).astype(jnp.bfloat16)
        o_ref[:, lo] = o[:tok]
        o_ref[:, hi] = o[tok:]
        delta = jnp.sum(g2.astype(jnp.float32) * o.astype(jnp.float32), axis=1, keepdims=True)
        dp = dot(g2, v, NT)
        ds = (share * ((dp - delta) * scale)).astype(jnp.bfloat16)
        dq = dot(ds, k, NN).astype(jnp.bfloat16)
        dq_ref[:, lo] = dq[:tok]
        dq_ref[:, hi] = dq[tok:]
        part_k = dot(q2, ds, TN)
        part_v = dot(g2, prob, TN)
        if p == 0:
            acc_k[...] = part_k
            acc_v[...] = part_v
        elif p < pairs - 1:
            acc_k[...] += part_k
            acc_v[...] += part_v
        else:
            for slot, total in ((0, (acc_k[...] + part_k).T), (1, (acc_v[...] + part_v).T)):
                for j, ref in enumerate((far_c, far_be, far_a, far_d, near)):
                    ref[slot] = total[j * BLOCK : (j + 1) * BLOCK].astype(ref.dtype)


def attend(queries, grads, pieces, flags, inner):
    tok = queries.shape[0]
    key_width = pieces[0].shape[2]
    wide = pl.BlockSpec((tok, GROUPS * HEAD_DIM), lambda i: (0, i))
    piece = pl.BlockSpec((2, tok, HEAD_DIM), lambda i: (0, 0, i))
    smem = pl.BlockSpec(memory_space=pltpu.SMEM)
    win = (REACH + 1) * tok
    types = [jnp.float32, jnp.bfloat16, jnp.float32, jnp.bfloat16, jnp.float32]
    return pl.pallas_call(
        attend_kernel,
        grid=(key_width // HEAD_DIM,),
        in_specs=[smem, smem, wide, wide] + [piece] * 6,
        out_specs=[wide, wide] + [piece] * 5,
        out_shape=[jax.ShapeDtypeStruct(queries.shape, jnp.bfloat16)] * 2
        + [jax.ShapeDtypeStruct((2, tok, key_width), t) for t in types],
        scratch_shapes=[
            pltpu.VMEM((2 * tok, win), jnp.float32),
            pltpu.VMEM((HEAD_DIM, win), jnp.float32),
            pltpu.VMEM((HEAD_DIM, win), jnp.float32),
        ],
        compiler_params=pltpu.CompilerParams(vmem_limit_bytes=16 << 20),
        name="attend",
    )(inner, flags, queries, grads, *pieces)


def outer_step(x, by):
    peers = lax.axis_size("ctx")
    by = by * INNER
    return lax.ppermute(x, "ctx", [(i, i + by) for i in range(peers) if 0 <= i + by < peers])


def to_inner(x, place):
    peers = lax.axis_size("ctx")
    return lax.ppermute(x, "ctx", [(i ^ 1, i) for i in range(peers) if i % INNER == place])


def outer_shift(x, by):
    peers = lax.axis_size("ctx")
    return lax.ppermute(x, "ctx", [(i, (i + INNER * by) % peers) for i in range(peers)])


def swap_inner(x):
    return lax.ppermute(x, "ctx", [(i, i ^ 1) for i in range(lax.axis_size("ctx"))])


def swap_fsdp(x):
    return lax.ppermute(x, "fsdp", [(0, 1), (1, 0)])


def swap_core(x):
    return lax.ppermute(x, "dp", [(0, 1), (1, 0)])


def part(x, index, size, axis):
    return lax.dynamic_slice_in_dim(x, index * size, size, axis)


def per_device(inputs, queries, w_kv, tile_mask, grad_out):
    rows_in = inputs[0]
    tok, width = rows_in.shape
    rows, pair_width = w_kv.shape
    half = pair_width // 2
    ctx, fsdp, core = (lax.axis_index(a) for a in ("ctx", "fsdp", "dp"))
    outer = lax.axis_size("ctx") // INNER
    z, x = ctx // INNER, ctx % INNER
    order = list(range(outer))
    late, early = order[-1:], order[:-1]

    plane = [(x ^ i) * 2 + (fsdp ^ j) for i, j in ((0, 0), (1, 0), (0, 1), (1, 1))]
    spots = {r: [(z - r) % outer] + plane for r in order}

    def places(which):
        return jnp.stack([v for r in which for v in spots[r]]).astype(jnp.int32).reshape(-1, 5)

    known = {
        "early": places(early or late),
        "late": places(late),
        "flat": jnp.stack([spots[r][0] * 4 + v for r in order for v in plane]).astype(jnp.int32),
        "inner": x.reshape(1).astype(jnp.int32),
        "to": [((z + r) % outer) * (width // outer) for r in range(outer)],
        "half": core * half,
        "first": core == 0,
        "x": x,
        "not_x": 1 - x,
        "even": x == 0,
        "y": fsdp,
        "not_y": 1 - fsdp,
    }
    for k in ("half", "x", "not_x", "y", "not_y"):
        known[k] = known[k].astype(jnp.uint32)
    known["to"] = [t.astype(jnp.uint32) for t in known["to"]]
    known, w_kv = lax.optimization_barrier((known, w_kv))
    x, not_x, even, y, not_y, first_core = (
        known[k] for k in ("x", "not_x", "even", "y", "not_y", "first")
    )

    own = lax.dynamic_slice_in_dim(w_kv, known["half"], half, 1)
    cols = [own]
    for r in range(1, outer):
        cols.append(outer_shift(cols[-1], 1))
    theirs_in = swap_core(rows_in)
    blocks = {}
    for r in order:
        col = cols[r]
        by_x, by_y = swap_inner(col), swap_fsdp(col)
        blocks[r] = [col, by_x, by_y, swap_fsdp(by_x) if r % 2 == 0 else swap_inner(by_y)]

    def listed(which):
        return [v for r in which for v in blocks[r]]

    by_blocks = rows % 128 == 0
    if by_blocks:
        part_sum = project(known["early"], rows_in, theirs_in, listed(early), None, jnp.float32)
        kv = project(known["late"], rows_in, theirs_in, listed(late), part_sum, jnp.bfloat16)
    else:
        weight_half = jnp.zeros((width, half), w_kv.dtype)
        for i, block in enumerate(listed(order)):
            at = known["flat"][i] * rows
            weight_half = lax.dynamic_update_slice_in_dim(weight_half, block, at, 0)
        kv = dot(jnp.concatenate([rows_in, theirs_in], axis=0), weight_half, NN).astype(jnp.bfloat16)
    block = width // outer
    held_in = lax.optimization_barrier((rows_in, cols[-1]))[0]

    def columns(t, r):
        return lax.dynamic_slice_in_dim(t, known["to"][r], block, 1)

    in_mine = [outer_shift(columns(held_in, r), r) for r in range(1, outer)]
    kv, *in_mine = lax.optimization_barrier((kv, *in_mine))
    in_theirs = [columns(theirs_in, 0)] + [swap_core(t) for t in in_mine]
    in_mine = [columns(rows_in, 0)] + in_mine

    mine, theirs = kv[:tok], swap_core(kv[tok:])
    key_vals = jnp.where(first_core, jnp.stack([mine, theirs]), jnp.stack([theirs, mine]))

    back_a = outer_step(key_vals, 1)
    back_b = to_inner(key_vals, 1)
    if by_blocks:
        tied = lax.optimization_barrier((*listed(order), kv))
        weight_half = assemble(known["flat"], list(tied[:-1]))
        weight_half, back_a = lax.optimization_barrier((weight_half, back_a))
    back_c = outer_step(back_a, 1)
    back_d = swap_inner(back_a)
    back_e = to_inner(back_c, 0)
    weight_other = swap_core(weight_half)

    queries, in_theirs = lax.optimization_barrier((queries, in_theirs))
    attended, grad_query, far_c, far_be, far_a, far_d, near = attend(
        queries[0],
        grad_out[0],
        [back_c, back_b, back_e, back_a, back_d, key_vals],
        tile_mask,
        known["inner"],
    )
    got_be = swap_inner(far_be).astype(jnp.float32)
    got_d = swap_inner(far_d).astype(jnp.float32)
    sent_c = (far_c + jnp.where(even, 0.0, got_be)).astype(jnp.bfloat16)
    got_c = outer_step(sent_c, -1).astype(jnp.float32)
    sent_a = (far_a + got_d + got_c).astype(jnp.bfloat16)
    got_a = outer_step(sent_a, -1).astype(jnp.float32)
    grad_kv = (near + jnp.where(even, got_be, 0.0) + got_a).astype(jnp.bfloat16)
    grad_mine = jnp.where(first_core, grad_kv[0], grad_kv[1])
    grad_theirs = jnp.where(first_core, grad_kv[1], grad_kv[0])

    grad_in = (dot(grad_mine, weight_half, NT) + dot(grad_theirs, weight_other, NT)).astype(
        jnp.bfloat16
    )

    grad_pair = jnp.concatenate([grad_mine, swap_core(grad_theirs)], axis=0)
    tile = None
    for r in range(outer):
        gathered = grad_pair if r == 0 else outer_shift(grad_pair, r)
        if r == min(1, outer - 1):
            gathered, grad_in = lax.optimization_barrier((gathered, grad_in))
        term = dot(jnp.concatenate([in_mine[r], in_theirs[r]], axis=0), gathered, TN)
        tile = term if tile is None else tile + term
    tile = tile.reshape(2, 2, rows, half)
    first, second = tile[..., : half // 2], tile[..., half // 2 :]

    def pick(t, index, axis):
        return lax.dynamic_index_in_dim(t, index, axis, keepdims=False)

    def sent(t, swap):
        return swap(t.astype(jnp.bfloat16)).astype(jnp.float32)

    first = pick(first, x, 0) + sent(pick(first, not_x, 0), swap_inner)
    second = pick(second, y, 1) + sent(pick(second, not_y, 1), swap_fsdp)
    first = pick(first, y, 0) + sent(pick(first, not_y, 0), swap_fsdp)
    second = pick(second, x, 0) + sent(pick(second, not_x, 0), swap_inner)
    tokens = lax.axis_size("fsdp") * lax.axis_size("dp") * lax.axis_size("ctx") * tok
    grad_half = jnp.concatenate([first, second], axis=1) * (1.0 / math.sqrt(tokens))
    grad_rest = swap_core(grad_half)
    weight_grad = jnp.where(
        first_core,
        jnp.concatenate([grad_half, grad_rest], axis=1),
        jnp.concatenate([grad_rest, grad_half], axis=1),
    )
    return (attended[None], grad_query[None], grad_in[None], weight_grad)


def solution(mesh):
    return jax.shard_map(
        per_device,
        mesh=mesh,
        in_specs=(
            P(("fsdp", "dp"), "ctx", None),
            P(("fsdp", "dp"), "ctx", None),
            P(("ctx", "fsdp"), None),
            P("ctx", None),
            P(("fsdp", "dp"), "ctx", None),
        ),
        out_specs=(
            P(("fsdp", "dp"), "ctx", None),
            P(("fsdp", "dp"), "ctx", None),
            P(("fsdp", "dp"), "ctx", None),
            P(("ctx", "fsdp"), None),
        ),
        check_vma=False,
    )
```

time: 208 us -> 187 us (0.90); the launches traced: 208 us -> 184 us
  local copies, waits for them, and re-layouts: 22.9 us -> 3.13 us
  Pallas kernels: 17.6 us -> 23.1 us
  matrix products: 8.8 us -> 5.88 us
  starting transfers between devices: 56.9 us -> 54.2 us
  other arithmetic: 4.01 us -> 1.77 us
    ppermute x8 -> x6, waiting for transfers between devices: 50.7 us -> 15.9 us  [the longest x4 13 us: outer_step(): lax.ppermute(x, 'ctx', [(i, i + by) for i in range(peers) if 0 <= i + by...]
    unnamed x67 -> x10, local copies, waits for them, and re-layouts: 18.8 us -> 0.54 us
    ppermute x10 -> x11, waiting for transfers between devices: 3.41 us -> 21.2 us  [swap_inner(): lax.ppermute(x, 'ctx', [(i, i ^ 1) for i in range(lax.axis_size('ctx'))])]
    ppermute x9, waiting for transfers between devices: 30.9 us -> 37.3 us  [outer_shift(): lax.ppermute(x, 'ctx', [(i, (i + INNER * by) % peers) for i in range(peer...]
    pallas_call x1 -> x4, Pallas kernels: 17.6 us -> 23.1 us  [the longest x1 17.9 us: attend(): pl.pallas_call(attend_kernel, grid=(key_width // HEAD_DIM,), in_specs=[sm...]
    ppermute x10 -> x8, waiting for transfers between devices: 7.54 us -> 12.2 us  [swap_fsdp(): return lax.ppermute(x, 'fsdp', [(0, 1), (1, 0)])]
    ppermute x8 -> x6, starting transfers between devices: 16.4 us -> 11.9 us  [the longest x4 7.8 us: outer_step(): lax.ppermute(x, 'ctx', [(i, i + by) for i in range(peers) if 0 <= i + by...]
    ppermute x6 -> x8, waiting for transfers between devices: 3.78 us -> 7.9 us  [swap_core(): return lax.ppermute(x, 'dp', [(0, 1), (1, 0)])]
  transfers between devices with their start and end apart: 43 -> 42, of which waited for: 21 -> 28; matrix products, arithmetic and copies ran while one was open for 13% -> 4% of each run, Pallas kernels for 8% -> 13%
where the time goes in v2:
time: 187 us; the launch traced here: 184 us
  waiting for transfers between devices  94.5 us (51%)
  starting transfers between devices  54.2 us (29%)
  Pallas kernels  23.1 us (12%)
  matrix products  5.88 us (3%)
  local copies, waits for them, and re-layouts  3.13 us (2%)
    ppermute x9, waiting for transfers between devices, outer_shift(): lax.ppermute(x, 'ctx', [(i, (i + INNER * by) % peers) for i in range(peer...  37.3 us
    ppermute x11, waiting for transfers between devices, swap_inner(): lax.ppermute(x, 'ctx', [(i, i ^ 1) for i in range(lax.axis_size('ctx'))])  21.2 us
    pallas_call x1, Pallas kernels, attend(): pl.pallas_call(attend_kernel, grid=(key_width // HEAD_DIM,), in_specs=[sm...  17.9 us
    ppermute x8, starting transfers between devices, swap_core(): return lax.ppermute(x, 'dp', [(0, 1), (1, 0)])  13.3 us
    ppermute x4, waiting for transfers between devices, outer_step(): lax.ppermute(x, 'ctx', [(i, i + by) for i in range(peers) if 0 <= i + by...  13 us
    ppermute x8, waiting for transfers between devices, swap_fsdp(): return lax.ppermute(x, 'fsdp', [(0, 1), (1, 0)])  12.2 us
    ppermute x11, starting transfers between devices, swap_inner(): lax.ppermute(x, 'ctx', [(i, i ^ 1) for i in range(lax.axis_size('ctx'))])  11.3 us
    ppermute x9, starting transfers between devices, outer_shift(): lax.ppermute(x, 'ctx', [(i, (i + INNER * by) % peers) for i in range(peer...  8.86 us
  transfers between devices with their start and end apart: 42, of which 28 were waited for; matrix products, arithmetic and copies ran while one was open for 4% of the time, Pallas kernels for 13%

profile of v2, /device:TPU:11, one launch (start us, length us, event | category | flops | bytes accessed | tf_op | source)
XLA Modules:
  0.0 183.7 jit_solution(8936796274636513313)
XLA Ops:
  5.6 3.4 %collective-permute-done.1.refs_4_ = bf16[256,512]{1,0:T(8,128)(2,1)S(1)} collective-permute-done((bf16[256,512]{1,0:T(8,128)(2,1)S(1)}, bf16[256,512]{1,0:T(8,128)(2,1)S(1)}, u32[]{:S(2)}, u32[]{:S(2)}) %collective-permute-start.1) | collective-permute-done | bytes 262176 | tf_op jit(solution)/shard_map/ppermute | solution.py:225
  13.5 2.9 %collective-permute-done.2.refs_8_ = bf16[256,512]{1,0:T(8,128)(2,1)S(1)} collective-permute-done((bf16[256,512]{1,0:T(8,128)(2,1)S(1)}, bf16[256,512]{1,0:T(8,128)(2,1)S(1)}, u32[]{:S(2)}, u32[]{:S(2)}) %collective-permute-start.2) | collective-permute-done | bytes 262176 | tf_op jit(solution)/shard_map/ppermute | solution.py:225
  18.4 3.6 %collective-permute-done.9.refs_3_ = bf16[256,512]{1,0:T(8,128)(2,1)S(1)} collective-permute-done((bf16[256,512]{1,0:T(8,128)(2,1)S(1)}, bf16[256,512]{1,0:T(8,128)(2,1)S(1)}, u32[]{:S(2)}, u32[]{:S(2)}) %collective-permute-start.9) | collective-permute-done | bytes 262176 | tf_op jit(solution)/shard_map/ppermute | solution.py:233
  29.3 3.6 %collective-permute-done.5.refs_2_.refs_14_ = bf16[256,512]{1,0:T(8,128)(2,1)S(1)} collective-permute-done((bf16[256,512]{1,0:T(8,128)(2,1)S(1)}, bf16[256,512]{1,0:T(8,128)(2,1)S(1)}, u32[]{:S(2)}, u32[]{:S(2)}) %collective-permute-start.5) | collective-permute-done | bytes 262176 | tf_op jit(solution)/shard_map/ppermute | solution.py:233
  34.9 3.6 %collective-permute-done.15.refs_11_ = bf16[256,512]{1,0:T(8,128)(2,1)S(1)} collective-permute-done((bf16[256,512]{1,0:T(8,128)(2,1)S(1)}, bf16[256,512]{1,0:T(8,128)(2,1)S(1)}, u32[]{:S(2)}, u32[]{:S(2)}) %collective-permute-start.15) | collective-permute-done | bytes 262176 | tf_op jit(solution)/shard_map/ppermute | solution.py:233
  38.5 3.0 %collective-permute-start.17 = (bf16[128,1024]{1,0:T(8,128)(2,1)S(1)}, bf16[128,1024]{1,0:T(8,128)(2,1)S(1)}, u32[]{:S(2)}, u32[]{:S(2)}) collective-permute-start(bf16[128,1024]{1,0:T(8,128)(2,1)S(1)} %get-tuple-element.113), channel_id=1, source_target_pairs={{0,16},{4,20},{8,24},{12,28},{16,0},{20,4},{24,8},{28,12},{1,17},{... | collective-permute-start | bytes 786440 | tf_op jit(solution)/shard_map/ppermute | solution.py:225
  41.5 2.5 %project.2.refs_4_ = f32[256,512]{1,0:T(8,128)S(1)} custom-call(s32[3,5]{1,0:T(4,128)S(1)} %reshape.29.spots, bf16[128,4096]{1,0:T(8,128)(2,1)S(1)} %bitcast.73, bf16[128,4096]{1,0:T(8,128)(2,1)S(1)} %collective-permute-done.theirs_ref, bf16[256,512]{1,0:T(8,128)(2,1)S(1)} %constant_dynamic-slice_fusion.3.refs_0_, ...), custom_call_target="tpu_custom_call" | custom-call | tf_op jit(solution)/shard_map/project/pallas_call | solution.py:69
  45.4 12.6 %collective-permute-done.17 = bf16[128,1024]{1,0:T(8,128)(2,1)S(1)} collective-permute-done((bf16[128,1024]{1,0:T(8,128)(2,1)S(1)}, bf16[128,1024]{1,0:T(8,128)(2,1)S(1)}, u32[]{:S(2)}, u32[]{:S(2)}) %collective-permute-start.17) | collective-permute-done | bytes 262176 | tf_op jit(solution)/shard_map/ppermute | solution.py:225
  64.6 6.1 %collective-permute-done.23.refs_3_ = bf16[2,128,512]{2,1,0:T(8,128)(2,1)S(1)} collective-permute-done((bf16[2,128,512]{2,1,0:T(8,128)(2,1)S(1)}, bf16[2,128,512]{2,1,0:T(8,128)(2,1)S(1)}, u32[]{:S(2)}, u32[]{:S(2)}) %collective-permute-start.23) | collective-permute-done | bytes 262176 | tf_op jit(solution)/shard_map/ppermute | solution.py:215
  74.7 4.4 %collective-permute-done.19 = bf16[128,1024]{1,0:T(8,128)(2,1)S(1)} collective-permute-done((bf16[128,1024]{1,0:T(8,128)(2,1)S(1)}, bf16[128,1024]{1,0:T(8,128)(2,1)S(1)}, u32[]{:S(2)}, u32[]{:S(2)}) %collective-permute-start.19) | collective-permute-done | bytes 262176 | tf_op jit(solution)/shard_map/ppermute | solution.py:237
  80.4 2.2 %collective-permute-start.27 = (bf16[2,128,512]{2,1,0:T(8,128)(2,1)S(1)}, bf16[2,128,512]{2,1,0:T(8,128)(2,1)S(1)}, u32[]{:S(2)}, u32[]{:S(2)}) collective-permute-start(bf16[2,128,512]{2,1,0:T(8,128)(2,1)S(1)} %collective-permute-done.23.refs_3_), channel_id=1, source_target_pairs={{0,4},{4,0},{8,12},{12,8},{16,20},{20,16},{24,28},{28,24},{1,5},{5... | collective-permute-start | bytes 786440 | tf_op jit(solution)/shard_map/ppermute | solution.py:229
  82.5 2.8 %collective-permute-start.26 = (bf16[2,128,512]{2,1,0:T(8,128)(2,1)S(1)}, bf16[2,128,512]{2,1,0:T(8,128)(2,1)S(1)}, u32[]{:S(2)}, u32[]{:S(2)}) collective-permute-start(bf16[2,128,512]{2,1,0:T(8,128)(2,1)S(1)} %collective-permute-done.24.refs_0_), channel_id=1, source_target_pairs={{4,0},{12,8},{20,16},{28,24},{5,1},{13,9},{21,17},{29,25},{6,2},{1... | collective-permute-start | bytes 786440 | tf_op jit(solution)/shard_map/ppermute | solution.py:220
  85.5 3.0 %collective-permute-done.25.refs_1_ = bf16[2,128,512]{2,1,0:T(8,128)(2,1)S(1)} collective-permute-done((bf16[2,128,512]{2,1,0:T(8,128)(2,1)S(1)}, bf16[2,128,512]{2,1,0:T(8,128)(2,1)S(1)}, u32[]{:S(2)}, u32[]{:S(2)}) %collective-permute-start.25) | collective-permute-done | bytes 262176 | tf_op jit(solution)/shard_map/ppermute | solution.py:220
  88.5 5.6 %collective-permute-done.27.refs_4_ = bf16[2,128,512]{2,1,0:T(8,128)(2,1)S(1)} collective-permute-done((bf16[2,128,512]{2,1,0:T(8,128)(2,1)S(1)}, bf16[2,128,512]{2,1,0:T(8,128)(2,1)S(1)}, u32[]{:S(2)}, u32[]{:S(2)}) %collective-permute-start.27) | collective-permute-done | bytes 262176 | tf_op jit(solution)/shard_map/ppermute | solution.py:229
  94.1 17.9 %attend.1 = (bf16[128,4096]{1,0:T(8,128)(2,1)}, bf16[128,4096]{1,0:T(8,128)(2,1)}, f32[2,128,512]{2,1,0:T(8,128)S(1)}, bf16[2,128,512]{2,1,0:T(8,128)(2,1)S(1)},...) custom-call(s32[1]{0:T(128)} %bitcast.23.inner, s32[1,4]{1,0:T(1,128)S(1)} %copy-done.4, ...), custom_call_target="tpu_custom_call" | custom-call | tf_op jit(solution)/shard_map/attend/pallas_call | solution.py:195
  113.4 5.2 %collective-permute-done.28 = bf16[2,128,512]{2,1,0:T(8,128)(2,1)S(1)} collective-permute-done((bf16[2,128,512]{2,1,0:T(8,128)(2,1)S(1)}, bf16[2,128,512]{2,1,0:T(8,128)(2,1)S(1)}, u32[]{:S(2)}, u32[]{:S(2)}) %collective-permute-start.28) | collective-permute-done | bytes 262176 | tf_op jit(solution)/shard_map/ppermute | solution.py:229
  120.6 3.6 %collective-permute-done.29 = bf16[2,128,512]{2,1,0:T(8,128)(2,1)S(1)} collective-permute-done((bf16[2,128,512]{2,1,0:T(8,128)(2,1)S(1)}, bf16[2,128,512]{2,1,0:T(8,128)(2,1)S(1)}, u32[]{:S(2)}, u32[]{:S(2)}) %collective-permute-start.29) | collective-permute-done | bytes 262176 | tf_op jit(solution)/shard_map/ppermute | solution.py:229
  128.0 5.2 %collective-permute-done.31 = bf16[2,128,512]{2,1,0:T(8,128)(2,1)S(1)} collective-permute-done((bf16[2,128,512]{2,1,0:T(8,128)(2,1)S(1)}, bf16[2,128,512]{2,1,0:T(8,128)(2,1)S(1)}, u32[]{:S(2)}, u32[]{:S(2)}) %collective-permute-start.31) | collective-permute-done | bytes 262176 | tf_op jit(solution)/shard_map/ppermute | solution.py:215
  133.3 6.0 %collective-permute-start.32 = (bf16[128,512]{1,0:T(8,128)(2,1)S(1)}, bf16[128,512]{1,0:T(8,128)(2,1)S(1)}, u32[]{:S(2)}, u32[]{:S(2)}) collective-permute-start(bf16[128,512]{1,0:T(8,128)(2,1)S(1)} %get-tuple-element.116), channel_id=1, source_target_pairs={{0,1},{1,0},{2,3},{3,2},{4,5},{5,4},{6,7},{7,6},{8,9},{9,8},{10,11... | collective-permute-start | bytes 393224 | tf_op jit(solution)/shard_map/ppermute | solution.py:237
  142.6 9.1 %collective-permute-done.35 = bf16[256,512]{1,0:T(8,128)(2,1)S(1)} collective-permute-done((bf16[256,512]{1,0:T(8,128)(2,1)S(1)}, bf16[256,512]{1,0:T(8,128)(2,1)S(1)}, u32[]{:S(2)}, u32[]{:S(2)}) %collective-permute-start.35) | collective-permute-done | bytes 262176 | tf_op jit(solution)/shard_map/ppermute | solution.py:225
  153.6 2.5 %fusion = bf16[128,4096]{1,0:T(8,128)(2,1)} fusion(f32[128,4096]{1,0:T(8,128)S(1)} %fusion.33, bf16[128,512]{1,0:T(8,128)(2,1)S(1)} %get-tuple-element.115, bf16[4096,512]{1,0:T(8,128)(2,1)S(1)} %assemble.1), kind=kOutput, calls=%fused_computation.1 | convolution fusion | flops 537919488 | bytes 7471104 | tf_op jit(solution)/shard_map/dot_general | solution.py:25
  156.1 6.8 %collective-permute-done.33 = bf16[256,512]{1,0:T(8,128)(2,1)S(1)} collective-permute-done((bf16[256,512]{1,0:T(8,128)(2,1)S(1)}, bf16[256,512]{1,0:T(8,128)(2,1)S(1)}, u32[]{:S(2)}, u32[]{:S(2)}) %collective-permute-start.33) | collective-permute-done | bytes 262176 | tf_op jit(solution)/shard_map/ppermute | solution.py:225
  168.0 4.1 %collective-permute-done.37 = bf16[2,256,256]{2,1,0:T(8,128)(2,1)S(1)} collective-permute-done((bf16[2,256,256]{2,1,0:T(8,128)(2,1)S(1)}, bf16[2,256,256]{2,1,0:T(8,128)(2,1)S(1)}, u32[]{:S(2)}, u32[]{:S(2)}) %collective-permute-start.37) | collective-permute-done | bytes 262176 | tf_op jit(solution)/shard_map/ppermute | solution.py:229
  177.7 3.3 %collective-permute-start.41 = (f32[256,512]{1,0:T(8,128)S(1)}, f32[256,512]{1,0:T(8,128)S(1)}, u32[]{:S(2)}, u32[]{:S(2)}) collective-permute-start(f32[256,512]{1,0:T(8,128)S(1)} %maximum_multiply_fusion), channel_id=1, source_target_pairs={{0,1},{1,0},{2,3},{3,2},{4,5},{5,4},{6,7},{7,6},{8,9},{9,8},{10,11... | collective-permute-start | bytes 1572872 | tf_op jit(solution)/shard_map/ppermute | solution.py:237
  (106 shorter events, 59.7 us)
Async XLA Ops:
  3.2 38.3 %collective-permute-start = (bf16[128,4096]{1,0:T(8,128)(2,1)}, bf16[128,4096]{1,0:T(8,128)(2,1)S(1)}, u32[]{:S(2)}, u32[]{:S(2)}) collective-permute-start(bf16[128,4096]{1,0:T(8,128)(2,1)} %bitcast.71), channel_id=1, source_target_pairs={{0,1},{1,0},{2,3},{3,2},{4,5},{5,4},{6,7},{7,6},{8,9},{9,8},{10,11... | collective-permute-start | bytes 3145736 | tf_op jit(solution)/shard_map/ppermute | solution.py:237
  4.4 7.9 %collective-permute-start.8 = (bf16[256,512]{1,0:T(8,128)(2,1)S(1)}, bf16[256,512]{1,0:T(8,128)(2,1)S(1)}, u32[]{:S(2)}, u32[]{:S(2)}) collective-permute-start(bf16[256,512]{1,0:T(8,128)(2,1)S(1)} %constant_dynamic-slice_fusion.3.refs_0_), channel_id=1, source_target_pairs={{0,2},{2,0},{1,3},{3,1},{4,6},{6,4},{5,7},{7,5},{8,10},{10,8},{9,1... | collective-permute-start | bytes 786440 | tf_op jit(solution)/shard_map/ppermute | solution.py:233
  12.3 9.8 %collective-permute-start.9 = (bf16[256,512]{1,0:T(8,128)(2,1)S(1)}, bf16[256,512]{1,0:T(8,128)(2,1)S(1)}, u32[]{:S(2)}, u32[]{:S(2)}) collective-permute-start(bf16[256,512]{1,0:T(8,128)(2,1)S(1)} %collective-permute-done.7.refs_1_), channel_id=1, source_target_pairs={{0,2},{2,0},{1,3},{3,1},{4,6},{6,4},{5,7},{7,5},{8,10},{10,8},{9,1... | collective-permute-start | bytes 786440 | tf_op jit(solution)/shard_map/ppermute | solution.py:233
  16.7 8.2 %collective-permute-start.13 = (bf16[256,512]{1,0:T(8,128)(2,1)S(1)}, bf16[256,512]{1,0:T(8,128)(2,1)S(1)}, u32[]{:S(2)}, u32[]{:S(2)}) collective-permute-start(bf16[256,512]{1,0:T(8,128)(2,1)S(1)} %collective-permute-done.2.refs_8_), channel_id=1, source_target_pairs={{0,4},{4,0},{8,12},{12,8},{16,20},{20,16},{24,28},{28,24},{1,5},{5... | collective-permute-start | bytes 786440 | tf_op jit(solution)/shard_map/ppermute | solution.py:229
  18.2 9.2 %collective-permute-start.12 = (bf16[256,512]{1,0:T(8,128)(2,1)S(1)}, bf16[256,512]{1,0:T(8,128)(2,1)S(1)}, u32[]{:S(2)}, u32[]{:S(2)}) collective-permute-start(bf16[256,512]{1,0:T(8,128)(2,1)S(1)} %collective-permute-done.11.refs_6_), channel_id=1, source_target_pairs={{0,4},{4,0},{8,12},{12,8},{16,20},{20,16},{24,28},{28,24},{1,5},{5... | collective-permute-start | bytes 786440 | tf_op jit(solution)/shard_map/ppermute | solution.py:229
  23.7 9.1 %collective-permute-start.5 = (bf16[256,512]{1,0:T(8,128)(2,1)S(1)}, bf16[256,512]{1,0:T(8,128)(2,1)S(1)}, u32[]{:S(2)}, u32[]{:S(2)}) collective-permute-start(bf16[256,512]{1,0:T(8,128)(2,1)S(1)} %collective-permute-done.3.refs_0_.refs_12_), channel_id=1, source_target_pairs={{0,2},{2,0},{1,3},{3,1},{4,6},{6,4},{5,7},{7,5},{8,10},{10,8},{9,1... | collective-permute-start | bytes 786440 | tf_op jit(solution)/shard_map/ppermute | solution.py:233
  25.0 13.5 %collective-permute-start.15 = (bf16[256,512]{1,0:T(8,128)(2,1)S(1)}, bf16[256,512]{1,0:T(8,128)(2,1)S(1)}, u32[]{:S(2)}, u32[]{:S(2)}) collective-permute-start(bf16[256,512]{1,0:T(8,128)(2,1)S(1)} %collective-permute-done.13.refs_9_), channel_id=1, source_target_pairs={{0,2},{2,0},{1,3},{3,1},{4,6},{6,4},{5,7},{7,5},{8,10},{10,8},{9,1... | collective-permute-start | bytes 786440 | tf_op jit(solution)/shard_map/ppermute | solution.py:233
  27.4 18.0 %collective-permute-start.16 = (bf16[128,1024]{1,0:T(8,128)(2,1)S(1)}, bf16[128,1024]{1,0:T(8,128)(2,1)S(1)}, u32[]{:S(2)}, u32[]{:S(2)}) collective-permute-start(bf16[128,1024]{1,0:T(8,128)(2,1)S(1)} %get-tuple-element.114), channel_id=1, source_target_pairs={{0,8},{4,12},{8,16},{12,20},{16,24},{20,28},{24,0},{28,4},{1,9},{5... | collective-permute-start | bytes 786440 | tf_op jit(solution)/shard_map/ppermute | solution.py:225
  28.7 15.4 %collective-permute-start.4 = (bf16[256,512]{1,0:T(8,128)(2,1)S(1)}, bf16[256,512]{1,0:T(8,128)(2,1)S(1)}, u32[]{:S(2)}, u32[]{:S(2)}) collective-permute-start(bf16[256,512]{1,0:T(8,128)(2,1)S(1)} %collective-permute-done.3.refs_0_.refs_12_), channel_id=1, source_target_pairs={{0,4},{4,0},{8,12},{12,8},{16,20},{20,16},{24,28},{28,24},{1,5},{5... | collective-permute-start | bytes 786440 | tf_op jit(solution)/shard_map/ppermute | solution.py:229
  32.9 11.2 %collective-permute-start.6 = (bf16[256,512]{1,0:T(8,128)(2,1)S(1)}, bf16[256,512]{1,0:T(8,128)(2,1)S(1)}, u32[]{:S(2)}, u32[]{:S(2)}) collective-permute-start(bf16[256,512]{1,0:T(8,128)(2,1)S(1)} %collective-permute-done.5.refs_2_.refs_14_), channel_id=1, source_target_pairs={{0,4},{4,0},{8,12},{12,8},{16,20},{20,16},{24,28},{28,24},{1,5},{5... | collective-permute-start | bytes 786440 | tf_op jit(solution)/shard_map/ppermute | solution.py:229
  38.5 19.5 %collective-permute-start.17 = (bf16[128,1024]{1,0:T(8,128)(2,1)S(1)}, bf16[128,1024]{1,0:T(8,128)(2,1)S(1)}, u32[]{:S(2)}, u32[]{:S(2)}) collective-permute-start(bf16[128,1024]{1,0:T(8,128)(2,1)S(1)} %get-tuple-element.113), channel_id=1, source_target_pairs={{0,16},{4,20},{8,24},{12,28},{16,0},{20,4},{24,8},{28,12},{1,17},{... | collective-permute-start | bytes 786440 | tf_op jit(solution)/shard_map/ppermute | solution.py:225
  41.5 17.6 %collective-permute-start.18 = (bf16[128,1024]{1,0:T(8,128)(2,1)S(1)}, bf16[128,1024]{1,0:T(8,128)(2,1)S(1)}, u32[]{:S(2)}, u32[]{:S(2)}) collective-permute-start(bf16[128,1024]{1,0:T(8,128)(2,1)S(1)} %get-tuple-element.112), channel_id=1, source_target_pairs={{0,24},{4,28},{8,0},{12,4},{16,8},{20,12},{24,16},{28,20},{1,25},{... | collective-permute-start | bytes 786440 | tf_op jit(solution)/shard_map/ppermute | solution.py:225
  61.2 9.5 %collective-permute-start.23 = (bf16[2,128,512]{2,1,0:T(8,128)(2,1)S(1)}, bf16[2,128,512]{2,1,0:T(8,128)(2,1)S(1)}, u32[]{:S(2)}, u32[]{:S(2)}) collective-permute-start(bf16[2,128,512]{2,1,0:T(8,128)(2,1)S(1)} %maximum_select_fusion.1.refs_5_), channel_id=1, source_target_pairs={{0,8},{4,12},{8,16},{12,20},{16,24},{20,28},{1,9},{5,13},{9,17},{1... | collective-permute-start | bytes 786440 | tf_op jit(solution)/shard_map/ppermute | solution.py:215
  70.7 81.4 %collective-permute-start.34 = (bf16[4096,512]{1,0:T(8,128)(2,1)S(1)}, bf16[4096,512]{1,0:T(8,128)(2,1)S(1)}, u32[]{:S(2)}, u32[]{:S(2)}) collective-permute-start(bf16[4096,512]{1,0:T(8,128)(2,1)S(1)} %assemble.1), channel_id=1, source_target_pairs={{0,1},{1,0},{2,3},{3,2},{4,5},{5,4},{6,7},{7,6},{8,9},{9,8},{10,11... | collective-permute-start | bytes 12582920 | tf_op jit(solution)/shard_map/ppermute | solution.py:237
  71.9 8.4 %collective-permute-start.20 = (bf16[128,1024]{1,0:T(8,128)(2,1)S(1)}, bf16[128,1024]{1,0:T(8,128)(2,1)S(1)}, u32[]{:S(2)}, u32[]{:S(2)}) collective-permute-start(bf16[128,1024]{1,0:T(8,128)(2,1)S(1)} %collective-permute-done.17), channel_id=1, source_target_pairs={{0,1},{1,0},{2,3},{3,2},{4,5},{5,4},{6,7},{7,6},{8,9},{9,8},{10,11... | collective-permute-start | bytes 786440 | tf_op jit(solution)/shard_map/ppermute | solution.py:237
  72.4 10.1 %collective-permute-start.24 = (bf16[2,128,512]{2,1,0:T(8,128)(2,1)S(1)}, bf16[2,128,512]{2,1,0:T(8,128)(2,1)S(1)}, u32[]{:S(2)}, u32[]{:S(2)}) collective-permute-start(bf16[2,128,512]{2,1,0:T(8,128)(2,1)S(1)} %collective-permute-done.23.refs_3_), channel_id=1, source_target_pairs={{0,8},{4,12},{8,16},{12,20},{16,24},{20,28},{1,9},{5,13},{9,17},{1... | collective-permute-start | bytes 786440 | tf_op jit(solution)/shard_map/ppermute | solution.py:215
  74.3 11.1 %collective-permute-start.21 = (bf16[128,1024]{1,0:T(8,128)(2,1)S(1)}, bf16[128,1024]{1,0:T(8,128)(2,1)S(1)}, u32[]{:S(2)}, u32[]{:S(2)}) collective-permute-start(bf16[128,1024]{1,0:T(8,128)(2,1)S(1)} %collective-permute-done.18), channel_id=1, source_target_pairs={{0,1},{1,0},{2,3},{3,2},{4,5},{5,4},{6,7},{7,6},{8,9},{9,8},{10,11... | collective-permute-start | bytes 786440 | tf_op jit(solution)/shard_map/ppermute | solution.py:237
  79.1 9.4 %collective-permute-start.25 = (bf16[2,128,512]{2,1,0:T(8,128)(2,1)S(1)}, bf16[2,128,512]{2,1,0:T(8,128)(2,1)S(1)}, u32[]{:S(2)}, u32[]{:S(2)}) collective-permute-start(bf16[2,128,512]{2,1,0:T(8,128)(2,1)S(1)} %maximum_select_fusion.1.refs_5_), channel_id=1, source_target_pairs={{0,4},{8,12},{16,20},{24,28},{1,5},{9,13},{17,21},{25,29},{2,6},{1... | collective-permute-start | bytes 786440 | tf_op jit(solution)/shard_map/ppermute | solution.py:220
  80.4 13.7 %collective-permute-start.27 = (bf16[2,128,512]{2,1,0:T(8,128)(2,1)S(1)}, bf16[2,128,512]{2,1,0:T(8,128)(2,1)S(1)}, u32[]{:S(2)}, u32[]{:S(2)}) collective-permute-start(bf16[2,128,512]{2,1,0:T(8,128)(2,1)S(1)} %collective-permute-done.23.refs_3_), channel_id=1, source_target_pairs={{0,4},{4,0},{8,12},{12,8},{16,20},{20,16},{24,28},{28,24},{1,5},{5... | collective-permute-start | bytes 786440 | tf_op jit(solution)/shard_map/ppermute | solution.py:229
  82.5 11.5 %collective-permute-start.26 = (bf16[2,128,512]{2,1,0:T(8,128)(2,1)S(1)}, bf16[2,128,512]{2,1,0:T(8,128)(2,1)S(1)}, u32[]{:S(2)}, u32[]{:S(2)}) collective-permute-start(bf16[2,128,512]{2,1,0:T(8,128)(2,1)S(1)} %collective-permute-done.24.refs_0_), channel_id=1, source_target_pairs={{4,0},{12,8},{20,16},{28,24},{5,1},{13,9},{21,17},{29,25},{6,2},{1... | collective-permute-start | bytes 786440 | tf_op jit(solution)/shard_map/ppermute | solution.py:220
  113.3 11.0 %collective-permute-start.29 = (bf16[2,128,512]{2,1,0:T(8,128)(2,1)S(1)}, bf16[2,128,512]{2,1,0:T(8,128)(2,1)S(1)}, u32[]{:S(2)}, u32[]{:S(2)}) collective-permute-start(bf16[2,128,512]{2,1,0:T(8,128)(2,1)S(1)} %get-tuple-element.97), channel_id=1, source_target_pairs={{0,4},{4,0},{8,12},{12,8},{16,20},{20,16},{24,28},{28,24},{1,5},{5... | collective-permute-start | bytes 786440 | tf_op jit(solution)/shard_map/ppermute | solution.py:229
  140.3 11.3 %collective-permute-start.35 = (bf16[256,512]{1,0:T(8,128)(2,1)S(1)}, bf16[256,512]{1,0:T(8,128)(2,1)S(1)}, u32[]{:S(2)}, u32[]{:S(2)}) collective-permute-start(bf16[256,512]{1,0:T(8,128)(2,1)S(1)} %pad_maximum_fusion), channel_id=1, source_target_pairs={{0,16},{4,20},{8,24},{12,28},{16,0},{20,4},{24,8},{28,12},{1,17},{... | collective-permute-start | bytes 786440 | tf_op jit(solution)/shard_map/ppermute | solution.py:225
  140.6 22.3 %collective-permute-start.33 = (bf16[256,512]{1,0:T(8,128)(2,1)S(1)}, bf16[256,512]{1,0:T(8,128)(2,1)S(1)}, u32[]{:S(2)}, u32[]{:S(2)}) collective-permute-start(bf16[256,512]{1,0:T(8,128)(2,1)S(1)} %pad_maximum_fusion), channel_id=1, source_target_pairs={{0,8},{4,12},{8,16},{12,20},{16,24},{20,28},{24,0},{28,4},{1,9},{5... | collective-permute-start | bytes 786440 | tf_op jit(solution)/shard_map/ppermute | solution.py:225
  141.5 22.7 %collective-permute-start.36 = (bf16[256,512]{1,0:T(8,128)(2,1)S(1)}, bf16[256,512]{1,0:T(8,128)(2,1)S(1)}, u32[]{:S(2)}, u32[]{:S(2)}) collective-permute-start(bf16[256,512]{1,0:T(8,128)(2,1)S(1)} %pad_maximum_fusion), channel_id=1, source_target_pairs={{0,24},{4,28},{8,0},{12,4},{16,8},{20,12},{24,16},{28,20},{1,25},{... | collective-permute-start | bytes 786440 | tf_op jit(solution)/shard_map/ppermute | solution.py:225
  (23 other events, 253.4 us)

commit v3 on v2

--- a/solution.py
+++ b/solution.py
@@ -15,6 +15,7 @@
 REACH = 4
 GROUPS = HEADS // KV_HEADS
 INNER = 2
+PLANE = ((0, 0), (1, 1), (1, 0), (0, 1))
 
 NT = (((1,), (1,)), ((), ()))
 NN = (((1,), (0,)), ((), ()))
@@ -191,7 +192,7 @@
     piece = pl.BlockSpec((2, tok, HEAD_DIM), lambda i: (0, 0, i))
     smem = pl.BlockSpec(memory_space=pltpu.SMEM)
     win = (REACH + 1) * tok
-    types = [jnp.float32, jnp.bfloat16, jnp.float32, jnp.bfloat16, jnp.float32]
+    types = [jnp.bfloat16, jnp.bfloat16, jnp.float32, jnp.bfloat16, jnp.float32]
     return pl.pallas_call(
         attend_kernel,
         grid=(key_width // HEAD_DIM,),
@@ -205,6 +206,11 @@
             pltpu.VMEM((HEAD_DIM, win), jnp.float32),
         ],
         compiler_params=pltpu.CompilerParams(vmem_limit_bytes=16 << 20),
+        cost_estimate=pl.CostEstimate(
+            flops=12 * queries.size * win,
+            transcendentals=queries.size // HEAD_DIM * win,
+            bytes_accessed=8 * queries.size + 18 * win * key_width * 2,
+        ),
         name="attend",
     )(inner, flags, queries, grads, *pieces)
 
@@ -237,8 +243,70 @@
     return lax.ppermute(x, "dp", [(0, 1), (1, 0)])
 
 
-def part(x, index, size, axis):
-    return lax.dynamic_slice_in_dim(x, index * size, size, axis)
+def odd_step(x, by):
+    peers = lax.axis_size("ctx")
+    start = 1 if by > 0 else 0
+    return lax.ppermute(
+        x, "ctx", [(i, i + by) for i in range(start, peers, 2) if 0 <= i + by < peers]
+    )
+
+
+def crossed(x, r, outer_core, plane_core=None):
+    ctx, fsdp = lax.axis_size("ctx"), lax.axis_size("fsdp")
+    flip_x, flip_y = PLANE[r]
+    pairs = []
+    for i in range(ctx):
+        for j in range(fsdp):
+            here = (i * fsdp + j) * 2
+            if outer_core is not None:
+                there = ((i + INNER * r) % ctx * fsdp + j) * 2
+                pairs.append((here + outer_core, there + outer_core))
+            if plane_core is not None:
+                there = ((i ^ flip_x) * fsdp + (j ^ flip_y)) * 2
+                pairs.append((here + plane_core, there + plane_core))
+    return lax.ppermute(x, ("ctx", "fsdp", "dp"), pairs)
+
+
+def split_kernel(offsets, mine_ref, theirs_ref, *refs):
+    outs, held, in_sems, out_sems = refs[:4], refs[4], refs[5], refs[6]
+    tok = mine_ref.shape[0]
+    unit = held.shape[2] // 4
+    reads = []
+    for r in range(4):
+        for k in range(4):
+            at = pl.ds(pl.multiple_of(offsets[r, k] * unit, unit), unit)
+            for i, src in enumerate((mine_ref, theirs_ref)):
+                dst = held.at[r, pl.ds(i * tok, tok), pl.ds(k * unit, unit)]
+                copy = pltpu.make_async_copy(src.at[:, at], dst, in_sems.at[r, k, i])
+                copy.start()
+                reads.append(copy)
+    writes = []
+    for r in range(4):
+        for copy in reads[8 * r : 8 * r + 8]:
+            copy.wait()
+        writes.append(pltpu.make_async_copy(held.at[r], outs[r], out_sems.at[r]))
+        writes[-1].start()
+    for copy in writes:
+        copy.wait()
+
+
+def split(offsets, mine, theirs):
+    hbm = pl.BlockSpec(memory_space=pltpu.HBM)
+    tok, width = mine.shape
+    shape = (2 * tok, width // 4)
+    return pl.pallas_call(
+        split_kernel,
+        in_specs=[pl.BlockSpec(memory_space=pltpu.SMEM), hbm, hbm],
+        out_specs=[hbm] * 4,
+        out_shape=[jax.ShapeDtypeStruct(shape, mine.dtype)] * 4,
+        scratch_shapes=[
+            pltpu.VMEM((4,) + shape, mine.dtype),
+            pltpu.SemaphoreType.DMA((4, 4, 2)),
+            pltpu.SemaphoreType.DMA((4,)),
+        ],
+        compiler_params=pltpu.CompilerParams(vmem_limit_bytes=8 << 20),
+        name="split",
+    )(offsets, mine, theirs)
 
 
 def per_device(inputs, queries, w_kv, tile_mask, grad_out):
@@ -258,7 +326,13 @@
     def places(which):
         return jnp.stack([v for r in which for v in spots[r]]).astype(jnp.int32).reshape(-1, 5)
 
+    mixed = outer == 4
+    to_outer = [(z + r) % outer for r in range(outer)]
+    to_plane = [(x ^ i) * 2 + (fsdp ^ j) for i, j in PLANE]
+    cut = [jnp.where(core == 0, to_outer[r] * 4 + k, k * 4 + to_plane[r]) for r in range(4) for k in range(4)] if mixed else [x]
     known = {
+        "cut": jnp.stack(cut).astype(jnp.int32).reshape(-1, 4 if mixed else 1),
+        "owner": [jnp.where(core == 0, p, o).astype(jnp.uint32) for p, o in zip(to_plane, to_outer)],
         "early": places(early or late),
         "late": places(late),
         "flat": jnp.stack([spots[r][0] * 4 + v for r in order for v in plane]).astype(jnp.int32),
@@ -281,15 +355,32 @@
     )
 
     own = lax.dynamic_slice_in_dim(w_kv, known["half"], half, 1)
-    cols = [own]
-    for r in range(1, outer):
-        cols.append(outer_shift(cols[-1], 1))
     theirs_in = swap_core(rows_in)
-    blocks = {}
+    tie = lax.optimization_barrier
+    col, blocks, cols = own, {}, [own]
     for r in order:
-        col = cols[r]
-        by_x, by_y = swap_inner(col), swap_fsdp(col)
-        blocks[r] = [col, by_x, by_y, swap_fsdp(by_x) if r % 2 == 0 else swap_inner(by_y)]
+        col_x = col_y = col
+        if r == outer - 1 and r:
+            col_x, blocks[r - 1][1] = tie((col, blocks[r - 1][1]))
+            col_y, blocks[r - 1][2] = tie((col, blocks[r - 1][2]))
+        following = outer_shift(col, 1) if r < outer - 1 else None
+        by_x, by_y = swap_inner(col_x), swap_fsdp(col_y)
+        if r == 0 and mixed:
+            early_cuts = split(known["cut"], rows_in, theirs_in)
+            following, by_x, by_y, early_cuts = tie((following, by_x, by_y, early_cuts))
+        elif r == 1 and outer > 2:
+            following, by_x = tie((following, by_x))
+        blocks[r] = [col, by_x, by_y]
+        col = following
+        cols.append(col)
+    for r in order:
+        if r == 0:
+            diagonal = swap_fsdp(blocks[0][1])
+        elif r == outer - 1:
+            diagonal = swap_inner(blocks[r][2])
+        else:
+            diagonal = outer_shift(diagonal, 1)
+        blocks[r].append(diagonal)
 
     def listed(which):
         return [v for r in which for v in blocks[r]]
@@ -305,15 +396,16 @@
             weight_half = lax.dynamic_update_slice_in_dim(weight_half, block, at, 0)
         kv = dot(jnp.concatenate([rows_in, theirs_in], axis=0), weight_half, NN).astype(jnp.bfloat16)
     block = width // outer
-    held_in = lax.optimization_barrier((rows_in, cols[-1]))[0]
 
     def columns(t, r):
         return lax.dynamic_slice_in_dim(t, known["to"][r], block, 1)
 
-    in_mine = [outer_shift(columns(held_in, r), r) for r in range(1, outer)]
-    kv, *in_mine = lax.optimization_barrier((kv, *in_mine))
-    in_theirs = [columns(theirs_in, 0)] + [swap_core(t) for t in in_mine]
-    in_mine = [columns(rows_in, 0)] + in_mine
+    if mixed:
+        cuts = early_cuts
+    else:
+        in_mine = [outer_shift(columns(rows_in, r), r) for r in range(1, outer)]
+        in_theirs = [columns(theirs_in, 0)] + [swap_core(t) for t in in_mine]
+        in_mine = [columns(rows_in, 0)] + in_mine
 
     mine, theirs = kv[:tok], swap_core(kv[tok:])
     key_vals = jnp.where(first_core, jnp.stack([mine, theirs]), jnp.stack([theirs, mine]))
@@ -321,15 +413,17 @@
     back_a = outer_step(key_vals, 1)
     back_b = to_inner(key_vals, 1)
     if by_blocks:
-        tied = lax.optimization_barrier((*listed(order), kv))
+        tied = tie((*listed(order), kv))
         weight_half = assemble(known["flat"], list(tied[:-1]))
-        weight_half, back_a = lax.optimization_barrier((weight_half, back_a))
+        weight_half, back_a = tie((weight_half, back_a))
     back_c = outer_step(back_a, 1)
     back_d = swap_inner(back_a)
-    back_e = to_inner(back_c, 0)
+    back_e = odd_step(back_a, 1)
     weight_other = swap_core(weight_half)
 
-    queries, in_theirs = lax.optimization_barrier((queries, in_theirs))
+    if mixed:
+        late_cuts, back_d = tie((cuts[1:], back_d))
+        passed = [crossed(late_cuts[r - 1], r, 0, 1) for r in range(1, 4)]
     attended, grad_query, far_c, far_be, far_a, far_d, near = attend(
         queries[0],
         grad_out[0],
@@ -337,13 +431,15 @@
         tile_mask,
         known["inner"],
     )
-    got_be = swap_inner(far_be).astype(jnp.float32)
+    got_c = outer_step(far_c, -1).astype(jnp.float32)
+    got_e = odd_step(far_be, -1).astype(jnp.float32)
     got_d = swap_inner(far_d).astype(jnp.float32)
-    sent_c = (far_c + jnp.where(even, 0.0, got_be)).astype(jnp.bfloat16)
-    got_c = outer_step(sent_c, -1).astype(jnp.float32)
-    sent_a = (far_a + got_d + got_c).astype(jnp.bfloat16)
+    got_b = to_inner(far_be, 0).astype(jnp.float32)
+    if mixed:
+        far_a, passed = tie((far_a, passed))
+    sent_a = (far_a + got_d + got_c + got_e).astype(jnp.bfloat16)
     got_a = outer_step(sent_a, -1).astype(jnp.float32)
-    grad_kv = (near + jnp.where(even, got_be, 0.0) + got_a).astype(jnp.bfloat16)
+    grad_kv = (near + got_b + got_a).astype(jnp.bfloat16)
     grad_mine = jnp.where(first_core, grad_kv[0], grad_kv[1])
     grad_theirs = jnp.where(first_core, grad_kv[1], grad_kv[0])
 
@@ -352,15 +448,17 @@
     )
 
     grad_pair = jnp.concatenate([grad_mine, swap_core(grad_theirs)], axis=0)
+    if mixed:
+        in_both = [cuts[0]] + passed
+    else:
+        in_both = [jnp.concatenate(t, axis=0) for t in zip(in_mine, in_theirs)]
     tile = None
     for r in range(outer):
-        gathered = grad_pair if r == 0 else outer_shift(grad_pair, r)
-        if r == min(1, outer - 1):
-            gathered, grad_in = lax.optimization_barrier((gathered, grad_in))
-        term = dot(jnp.concatenate([in_mine[r], in_theirs[r]], axis=0), gathered, TN)
+        gathered = grad_pair
+        if r:
+            gathered = crossed(grad_pair, r, 0, 1) if mixed else outer_shift(grad_pair, r)
+        term = dot(in_both[r], gathered, TN)
         tile = term if tile is None else tile + term
-    tile = tile.reshape(2, 2, rows, half)
-    first, second = tile[..., : half // 2], tile[..., half // 2 :]
 
     def pick(t, index, axis):
         return lax.dynamic_index_in_dim(t, index, axis, keepdims=False)
@@ -368,12 +466,27 @@
     def sent(t, swap):
         return swap(t.astype(jnp.bfloat16)).astype(jnp.float32)
 
-    first = pick(first, x, 0) + sent(pick(first, not_x, 0), swap_inner)
-    second = pick(second, y, 1) + sent(pick(second, not_y, 1), swap_fsdp)
-    first = pick(first, y, 0) + sent(pick(first, not_y, 0), swap_fsdp)
-    second = pick(second, x, 0) + sent(pick(second, not_x, 0), swap_inner)
+    if mixed:
+        tile = tile.reshape(4, rows, half)
+        tile, _ = tie((tile, swap_core(tile[0, :8, :HEAD_DIM])))
+        arrived = [
+            crossed(pick(tile, known["owner"][r], 0).astype(jnp.bfloat16), r, 1, 0)
+            for r in range(1, 4)
+        ]
+        arrived, grad_in = tie((arrived, grad_in))
+        grad_half = pick(tile, known["owner"][0], 0)
+        for t in arrived:
+            grad_half += t.astype(jnp.float32)
+    else:
+        tile = tile.reshape(2, 2, rows, half)
+        first, second = tile[..., : half // 2], tile[..., half // 2 :]
+        first = pick(first, x, 0) + sent(pick(first, not_x, 0), swap_inner)
+        second = pick(second, y, 1) + sent(pick(second, not_y, 1), swap_fsdp)
+        first = pick(first, y, 0) + sent(pick(first, not_y, 0), swap_fsdp)
+        second = pick(second, x, 0) + sent(pick(second, not_x, 0), swap_inner)
+        grad_half = jnp.concatenate([first, second], axis=1)
     tokens = lax.axis_size("fsdp") * lax.axis_size("dp") * lax.axis_size("ctx") * tok
-    grad_half = jnp.concatenate([first, second], axis=1) * (1.0 / math.sqrt(tokens))
+    grad_half = grad_half * (1.0 / math.sqrt(tokens))
     grad_rest = swap_core(grad_half)
     weight_grad = jnp.where(
         first_core,

time: 187 us -> 161 us (0.86); the launches traced: 184 us -> 161 us
  waiting for transfers between devices: 94.5 us -> 63 us
  starting transfers between devices: 54.2 us -> 62.6 us
    ppermute x9 -> x5, waiting for transfers between devices: 37.3 us -> 13.8 us  [outer_shift(): lax.ppermute(x, 'ctx', [(i, (i + INNER * by) % peers) for i in range(peer...]
    ppermute x0 -> x11, waiting for transfers between devices: none -> 22.3 us  [the longest x9 15.3 us: crossed(): return lax.ppermute(x, ('ctx', 'fsdp', 'dp'), pairs)]
    ppermute x11 -> x7, waiting for transfers between devices: 21.2 us -> 2.68 us  [swap_inner(): lax.ppermute(x, 'ctx', [(i, i ^ 1) for i in range(lax.axis_size('ctx'))])]
    ppermute x0 -> x11, starting transfers between devices: none -> 13.9 us  [the longest x2 7.22 us: odd_step(): lax.ppermute(x, 'ctx', [(i, i + by) for i in range(start, peers, 2) if 0...]
    ppermute x8 -> x5, waiting for transfers between devices: 12.2 us -> 4.23 us  [swap_fsdp(): return lax.ppermute(x, 'fsdp', [(0, 1), (1, 0)])]
    ppermute x11 -> x7, starting transfers between devices: 11.3 us -> 4.05 us  [swap_inner(): lax.ppermute(x, 'ctx', [(i, i ^ 1) for i in range(lax.axis_size('ctx'))])]
    ppermute x8 -> x5, starting transfers between devices: 13.3 us -> 19.1 us  [swap_core(): return lax.ppermute(x, 'dp', [(0, 1), (1, 0)])]
    ppermute x8 -> x5, waiting for transfers between devices: 7.9 us -> 3.51 us  [swap_core(): return lax.ppermute(x, 'dp', [(0, 1), (1, 0)])]
  transfers between devices with their start and end apart: 42 -> 39, of which waited for: 28 -> 25; matrix products, arithmetic and copies ran while one was open for 4% -> 4% of each run, Pallas kernels for 13% -> 14%
where the time goes in v3:
time: 161 us
  waiting for transfers between devices  63 us (39%)
  starting transfers between devices  62.6 us (39%)
  Pallas kernels  24.6 us (15%)
  matrix products  5.89 us (4%)
  local copies, waits for them, and re-layouts  2.09 us (1%)
  other arithmetic  1.61 us (1%)
    ppermute x5, starting transfers between devices, swap_core(): return lax.ppermute(x, 'dp', [(0, 1), (1, 0)])  19.1 us
    pallas_call x1, Pallas kernels, attend(): pl.pallas_call(attend_kernel, grid=(key_width // HEAD_DIM,), in_specs=[sm...  17.8 us
    ppermute x9, waiting for transfers between devices, crossed(): return lax.ppermute(x, ('ctx', 'fsdp', 'dp'), pairs)  15.3 us
    ppermute x4, waiting for transfers between devices, outer_step(): lax.ppermute(x, 'ctx', [(i, i + by) for i in range(peers) if 0 <= i + by...  14.4 us
    ppermute x5, waiting for transfers between devices, outer_shift(): lax.ppermute(x, 'ctx', [(i, (i + INNER * by) % peers) for i in range(peer...  13.8 us
    ppermute x4, starting transfers between devices, outer_step(): lax.ppermute(x, 'ctx', [(i, i + by) for i in range(peers) if 0 <= i + by...  11.5 us
    ppermute x2, starting transfers between devices, odd_step(): lax.ppermute(x, 'ctx', [(i, i + by) for i in range(start, peers, 2) if 0...  7.22 us
    ppermute x2, waiting for transfers between devices, odd_step(): lax.ppermute(x, 'ctx', [(i, i + by) for i in range(start, peers, 2) if 0...  7 us
  transfers between devices with their start and end apart: 39, of which 25 were waited for; matrix products, arithmetic and copies ran while one was open for 4% of the time, Pallas kernels for 14%

profile of v3, /device:TPU:11, one launch (start us, length us, event | category | flops | bytes accessed | tf_op | source)
XLA Modules:
  0.0 160.7 jit_solution(3313983673102578391)
XLA Ops:
  14.4 2.4 %collective-permute-done.5.refs_8_ = bf16[256,512]{1,0:T(8,128)(2,1)S(1)} collective-permute-done((bf16[256,512]{1,0:T(8,128)(2,1)S(1)}, bf16[256,512]{1,0:T(8,128)(2,1)S(1)}, u32[]{:S(2)}, u32[]{:S(2)}) %collective-permute-start.5) | collective-permute-done | bytes 262176 | tf_op jit(solution)/shard_map/ppermute | solution.py:231
  19.5 2.3 %collective-permute-start.8 = (bf16[256,512]{1,0:T(8,128)(2,1)S(1)}, bf16[256,512]{1,0:T(8,128)(2,1)S(1)}, u32[]{:S(2)}, u32[]{:S(2)}) collective-permute-start(bf16[256,512]{1,0:T(8,128)(2,1)S(1)} %collective-permute-done.4.refs_3_), channel_id=1, source_target_pairs={{0,8},{4,12},{8,16},{12,20},{16,24},{20,28},{24,0},{28,4},{1,9},{5... | collective-permute-start | bytes 786440 | tf_op jit(solution)/shard_map/ppermute | solution.py:231
  21.7 3.0 %collective-permute-done.11.refs_10_ = bf16[256,512]{1,0:T(8,128)(2,1)S(1)} collective-permute-done((bf16[256,512]{1,0:T(8,128)(2,1)S(1)}, bf16[256,512]{1,0:T(8,128)(2,1)S(1)}, u32[]{:S(2)}, u32[]{:S(2)}) %collective-permute-start.11) | collective-permute-done | bytes 262176 | tf_op jit(solution)/shard_map/ppermute | solution.py:239
  27.1 4.2 %collective-permute-done.8.refs_7_ = bf16[256,512]{1,0:T(8,128)(2,1)S(1)} collective-permute-done((bf16[256,512]{1,0:T(8,128)(2,1)S(1)}, bf16[256,512]{1,0:T(8,128)(2,1)S(1)}, u32[]{:S(2)}, u32[]{:S(2)}) %collective-permute-start.8) | collective-permute-done | bytes 262176 | tf_op jit(solution)/shard_map/ppermute | solution.py:231
  33.9 4.5 %collective-permute-done.12.refs_11_ = bf16[256,512]{1,0:T(8,128)(2,1)S(1)} collective-permute-done((bf16[256,512]{1,0:T(8,128)(2,1)S(1)}, bf16[256,512]{1,0:T(8,128)(2,1)S(1)}, u32[]{:S(2)}, u32[]{:S(2)}) %collective-permute-start.12) | collective-permute-done | bytes 262176 | tf_op jit(solution)/shard_map/ppermute | solution.py:231
  38.4 2.5 %project.2.refs_4_ = f32[256,512]{1,0:T(8,128)S(1)} custom-call(s32[3,5]{1,0:T(4,128)S(1)} %reshape.31.spots, bf16[128,4096]{1,0:T(8,128)(2,1)S(1)} %bitcast.83, bf16[128,4096]{1,0:T(8,128)(2,1)S(1)} %collective-permute-done.3.theirs_ref, bf16[256,512]{1,0:T(8,128)(2,1)S(1)} %constant_dynamic-slice_fusion.refs_0_, ...), custom_call_target="tpu_custom_call" | custom-call | tf_op jit(solution)/shard_map/project/pallas_call | solution.py:70
  43.0 4.0 %collective-permute-start.16 = (bf16[128,512]{1,0:T(8,128)(2,1)S(1)}, bf16[128,512]{1,0:T(8,128)(2,1)S(1)}, u32[]{:S(2)}, u32[]{:S(2)}) collective-permute-start(bf16[128,512]{1,0:T(8,128)(2,1)S(1)} %get-tuple-element.142), channel_id=1, source_target_pairs={{0,1},{1,0},{2,3},{3,2},{4,5},{5,4},{6,7},{7,6},{8,9},{9,8},{10,11... | collective-permute-start | bytes 393224 | tf_op jit(solution)/shard_map/ppermute | solution.py:243
  48.0 3.5 %collective-permute-start.17 = (bf16[2,128,512]{2,1,0:T(8,128)(2,1)S(1)}, bf16[2,128,512]{2,1,0:T(8,128)(2,1)S(1)}, u32[]{:S(2)}, u32[]{:S(2)}) collective-permute-start(bf16[2,128,512]{2,1,0:T(8,128)(2,1)S(1)} %maximum_select_fusion.1.refs_5_), channel_id=1, source_target_pairs={{0,8},{4,12},{8,16},{12,20},{16,24},{20,28},{1,9},{5,13},{9,17},{1... | collective-permute-start | bytes 786440 | tf_op jit(solution)/shard_map/ppermute | solution.py:221
  53.0 5.9 %collective-permute-done.17.refs_3_ = bf16[2,128,512]{2,1,0:T(8,128)(2,1)S(1)} collective-permute-done((bf16[2,128,512]{2,1,0:T(8,128)(2,1)S(1)}, bf16[2,128,512]{2,1,0:T(8,128)(2,1)S(1)}, u32[]{:S(2)}, u32[]{:S(2)}) %collective-permute-start.17) | collective-permute-done | bytes 262176 | tf_op jit(solution)/shard_map/ppermute | solution.py:221
  61.1 4.1 %collective-permute-start.18 = (bf16[2,128,512]{2,1,0:T(8,128)(2,1)S(1)}, bf16[2,128,512]{2,1,0:T(8,128)(2,1)S(1)}, u32[]{:S(2)}, u32[]{:S(2)}) collective-permute-start(bf16[2,128,512]{2,1,0:T(8,128)(2,1)S(1)} %collective-permute-done.17.refs_3_), channel_id=1, source_target_pairs={{0,8},{4,12},{8,16},{12,20},{16,24},{20,28},{1,9},{5,13},{9,17},{1... | collective-permute-start | bytes 786440 | tf_op jit(solution)/shard_map/ppermute | solution.py:221
  65.3 5.9 %collective-permute-start.20 = (bf16[2,128,512]{2,1,0:T(8,128)(2,1)S(1)}, bf16[2,128,512]{2,1,0:T(8,128)(2,1)S(1)}, u32[]{:S(2)}, u32[]{:S(2)}) collective-permute-start(bf16[2,128,512]{2,1,0:T(8,128)(2,1)S(1)} %collective-permute-done.17.refs_3_), channel_id=1, source_target_pairs={{4,8},{12,16},{20,24},{5,9},{13,17},{21,25},{6,10},{14,18},{22,26}... | collective-permute-start | bytes 786440 | tf_op jit(solution)/shard_map/ppermute | solution.py:249
  71.3 2.0 %collective-permute-done.19.refs_1_ = bf16[2,128,512]{2,1,0:T(8,128)(2,1)S(1)} collective-permute-done((bf16[2,128,512]{2,1,0:T(8,128)(2,1)S(1)}, bf16[2,128,512]{2,1,0:T(8,128)(2,1)S(1)}, u32[]{:S(2)}, u32[]{:S(2)}) %collective-permute-start.19) | collective-permute-done | bytes 262176 | tf_op jit(solution)/shard_map/ppermute | solution.py:226
  74.0 2.2 %collective-permute-done.20.refs_2_ = bf16[2,128,512]{2,1,0:T(8,128)(2,1)S(1)} collective-permute-done((bf16[2,128,512]{2,1,0:T(8,128)(2,1)S(1)}, bf16[2,128,512]{2,1,0:T(8,128)(2,1)S(1)}, u32[]{:S(2)}, u32[]{:S(2)}) %collective-permute-start.20) | collective-permute-done | bytes 262176 | tf_op jit(solution)/shard_map/ppermute | solution.py:249
  76.1 17.8 %attend.1 = (bf16[128,4096]{1,0:T(8,128)(2,1)}, bf16[128,4096]{1,0:T(8,128)(2,1)}, bf16[2,128,512]{2,1,0:T(8,128)(2,1)S(1)}, bf16[2,128,512]{2,1,0:T(8,128)(2,1)...) custom-call(s32[1]{0:T(128)} %bitcast.39.inner, ...), custom_call_target="tpu_custom_call" | custom-call | flops 4026531840 | bytes 15990784 | tf_op jit(solution)/shard_map/attend/pallas_call | solution.py:196
  98.4 2.3 %collective-permute-start.22 = (bf16[2,128,512]{2,1,0:T(8,128)(2,1)S(1)}, bf16[2,128,512]{2,1,0:T(8,128)(2,1)S(1)}, u32[]{:S(2)}, u32[]{:S(2)}) collective-permute-start(bf16[2,128,512]{2,1,0:T(8,128)(2,1)S(1)} %get-tuple-element.116), channel_id=1, source_target_pairs={{4,0},{12,8},{20,16},{28,24},{5,1},{13,9},{21,17},{29,25},{6,2},{1... | collective-permute-start | bytes 786440 | tf_op jit(solution)/shard_map/ppermute | solution.py:226
  100.6 3.3 %collective-permute-done.27 = bf16[2,128,512]{2,1,0:T(8,128)(2,1)S(1)} collective-permute-done((bf16[2,128,512]{2,1,0:T(8,128)(2,1)S(1)}, bf16[2,128,512]{2,1,0:T(8,128)(2,1)S(1)}, u32[]{:S(2)}, u32[]{:S(2)}) %collective-permute-start.27) | collective-permute-done | bytes 262176 | tf_op jit(solution)/shard_map/ppermute | solution.py:221
  104.0 4.8 %collective-permute-done.28 = bf16[2,128,512]{2,1,0:T(8,128)(2,1)S(1)} collective-permute-done((bf16[2,128,512]{2,1,0:T(8,128)(2,1)S(1)}, bf16[2,128,512]{2,1,0:T(8,128)(2,1)S(1)}, u32[]{:S(2)}, u32[]{:S(2)}) %collective-permute-start.28) | collective-permute-done | bytes 262176 | tf_op jit(solution)/shard_map/ppermute | solution.py:249
  110.9 5.2 %collective-permute-done.29 = bf16[2,128,512]{2,1,0:T(8,128)(2,1)S(1)} collective-permute-done((bf16[2,128,512]{2,1,0:T(8,128)(2,1)S(1)}, bf16[2,128,512]{2,1,0:T(8,128)(2,1)S(1)}, u32[]{:S(2)}, u32[]{:S(2)}) %collective-permute-start.29) | collective-permute-done | bytes 262176 | tf_op jit(solution)/shard_map/ppermute | solution.py:221
  116.2 5.0 %collective-permute-start.30 = (bf16[128,512]{1,0:T(8,128)(2,1)S(1)}, bf16[128,512]{1,0:T(8,128)(2,1)S(1)}, u32[]{:S(2)}, u32[]{:S(2)}) collective-permute-start(bf16[128,512]{1,0:T(8,128)(2,1)S(1)} %get-tuple-element.140), channel_id=1, source_target_pairs={{0,1},{1,0},{2,3},{3,2},{4,5},{5,4},{6,7},{7,6},{8,9},{9,8},{10,11... | collective-permute-start | bytes 393224 | tf_op jit(solution)/shard_map/ppermute | solution.py:243
  125.4 3.1 %collective-permute-done.31 = bf16[256,512]{1,0:T(8,128)(2,1)S(1)} collective-permute-done((bf16[256,512]{1,0:T(8,128)(2,1)S(1)}, bf16[256,512]{1,0:T(8,128)(2,1)S(1)}, u32[]{:S(2)}, u32[]{:S(2)}) %collective-permute-start.31) | collective-permute-done | bytes 262176 | tf_op jit(solution)/shard_map/ppermute | solution.py:267
  136.9 2.5 %fusion = bf16[128,4096]{1,0:T(8,128)(2,1)} fusion(f32[128,4096]{1,0:T(8,128)S(1)} %fusion.10, bf16[128,512]{1,0:T(8,128)(2,1)S(1)} %get-tuple-element.139, bf16[4096,512]{1,0:T(8,128)(2,1)S(1)} %assemble.1), kind=kOutput, calls=%fused_computation.1 | convolution fusion | flops 537919488 | bytes 7471104 | tf_op jit(solution)/shard_map/dot_general | solution.py:26
  139.4 5.3 %collective-permute-done.34 = bf16[256,512]{1,0:T(8,128)(2,1)S(1)} collective-permute-done((bf16[256,512]{1,0:T(8,128)(2,1)S(1)}, bf16[256,512]{1,0:T(8,128)(2,1)S(1)}, u32[]{:S(2)}, u32[]{:S(2)}) %collective-permute-start.34) | collective-permute-done | bytes 262176 | tf_op jit(solution)/shard_map/ppermute | solution.py:267
  144.7 2.8 %collective-permute-done.35 = bf16[256,512]{1,0:T(8,128)(2,1)S(1)} collective-permute-done((bf16[256,512]{1,0:T(8,128)(2,1)S(1)}, bf16[256,512]{1,0:T(8,128)(2,1)S(1)}, u32[]{:S(2)}, u32[]{:S(2)}) %collective-permute-start.35) | collective-permute-done | bytes 262176 | tf_op jit(solution)/shard_map/ppermute | solution.py:267
  149.7 8.4 %collective-permute-start.38 = (f32[256,512]{1,0:T(8,128)S(1)}, f32[256,512]{1,0:T(8,128)S(1)}, u32[]{:S(2)}, u32[]{:S(2)}) collective-permute-start(f32[256,512]{1,0:T(8,128)S(1)} %fusion.3), channel_id=1, source_target_pairs={{0,1},{1,0},{2,3},{3,2},{4,5},{5,4},{6,7},{7,6},{8,9},{9,8},{10,11... | collective-permute-start | bytes 1572872 | tf_op jit(solution)/shard_map/ppermute | solution.py:243
  (93 shorter events, 52.7 us)
Async XLA Ops:
  2.1 7.5 %collective-permute-start = (bf16[256,512]{1,0:T(8,128)(2,1)S(1)}, bf16[256,512]{1,0:T(8,128)(2,1)S(1)}, u32[]{:S(2)}, u32[]{:S(2)}) collective-permute-start(bf16[256,512]{1,0:T(8,128)(2,1)S(1)} %constant_dynamic-slice_fusion.refs_0_), channel_id=1, source_target_pairs={{0,8},{4,12},{8,16},{12,20},{16,24},{20,28},{24,0},{28,4},{1,9},{5... | collective-permute-start | bytes 786440 | tf_op jit(solution)/shard_map/ppermute | solution.py:231
  19.5 11.8 %collective-permute-start.8 = (bf16[256,512]{1,0:T(8,128)(2,1)S(1)}, bf16[256,512]{1,0:T(8,128)(2,1)S(1)}, u32[]{:S(2)}, u32[]{:S(2)}) collective-permute-start(bf16[256,512]{1,0:T(8,128)(2,1)S(1)} %collective-permute-done.4.refs_3_), channel_id=1, source_target_pairs={{0,8},{4,12},{8,16},{12,20},{16,24},{20,28},{24,0},{28,4},{1,9},{5... | collective-permute-start | bytes 786440 | tf_op jit(solution)/shard_map/ppermute | solution.py:231
  21.7 9.5 %collective-permute-start.10 = (bf16[256,512]{1,0:T(8,128)(2,1)S(1)}, bf16[256,512]{1,0:T(8,128)(2,1)S(1)}, u32[]{:S(2)}, u32[]{:S(2)}) collective-permute-start(bf16[256,512]{1,0:T(8,128)(2,1)S(1)} %collective-permute-done.5.refs_8_), channel_id=1, source_target_pairs={{0,4},{4,0},{8,12},{12,8},{16,20},{20,16},{24,28},{28,24},{1,5},{5... | collective-permute-start | bytes 786440 | tf_op jit(solution)/shard_map/ppermute | solution.py:235
  26.0 7.9 %collective-permute-start.7 = (bf16[256,512]{1,0:T(8,128)(2,1)S(1)}, bf16[256,512]{1,0:T(8,128)(2,1)S(1)}, u32[]{:S(2)}, u32[]{:S(2)}) collective-permute-start(bf16[256,512]{1,0:T(8,128)(2,1)S(1)} %collective-permute-done.refs_4_), channel_id=1, source_target_pairs={{0,2},{2,0},{1,3},{3,1},{4,6},{6,4},{5,7},{7,5},{8,10},{10,8},{9,1... | collective-permute-start | bytes 786440 | tf_op jit(solution)/shard_map/ppermute | solution.py:239
  31.2 9.7 %collective-permute-start.13 = (bf16[256,512]{1,0:T(8,128)(2,1)S(1)}, bf16[256,512]{1,0:T(8,128)(2,1)S(1)}, u32[]{:S(2)}, u32[]{:S(2)}) collective-permute-start(bf16[256,512]{1,0:T(8,128)(2,1)S(1)} %collective-permute-done.9.refs_0_.refs_12_), channel_id=1, source_target_pairs={{0,4},{4,0},{8,12},{12,8},{16,20},{20,16},{24,28},{28,24},{1,5},{5... | collective-permute-start | bytes 786440 | tf_op jit(solution)/shard_map/ppermute | solution.py:235
  31.3 10.4 %collective-permute-start.15 = (bf16[256,512]{1,0:T(8,128)(2,1)S(1)}, bf16[256,512]{1,0:T(8,128)(2,1)S(1)}, u32[]{:S(2)}, u32[]{:S(2)}) collective-permute-start(bf16[256,512]{1,0:T(8,128)(2,1)S(1)} %collective-permute-done.14.refs_2_.refs_14_), channel_id=1, source_target_pairs={{0,4},{4,0},{8,12},{12,8},{16,20},{20,16},{24,28},{28,24},{1,5},{5... | collective-permute-start | bytes 786440 | tf_op jit(solution)/shard_map/ppermute | solution.py:235
  48.0 10.9 %collective-permute-start.17 = (bf16[2,128,512]{2,1,0:T(8,128)(2,1)S(1)}, bf16[2,128,512]{2,1,0:T(8,128)(2,1)S(1)}, u32[]{:S(2)}, u32[]{:S(2)}) collective-permute-start(bf16[2,128,512]{2,1,0:T(8,128)(2,1)S(1)} %maximum_select_fusion.1.refs_5_), channel_id=1, source_target_pairs={{0,8},{4,12},{8,16},{12,20},{16,24},{20,28},{1,9},{5,13},{9,17},{1... | collective-permute-start | bytes 786440 | tf_op jit(solution)/shard_map/ppermute | solution.py:221
  58.9 76.6 %collective-permute-start.37 = (bf16[4096,512]{1,0:T(8,128)(2,1)S(1)}, bf16[4096,512]{1,0:T(8,128)(2,1)S(1)}, u32[]{:S(2)}, u32[]{:S(2)}) collective-permute-start(bf16[4096,512]{1,0:T(8,128)(2,1)S(1)} %assemble.1), channel_id=1, source_target_pairs={{0,1},{1,0},{2,3},{3,2},{4,5},{5,4},{6,7},{7,6},{8,9},{9,8},{10,11... | collective-permute-start | bytes 12582920 | tf_op jit(solution)/shard_map/ppermute | solution.py:243
  59.8 11.4 %collective-permute-start.21 = (bf16[2,128,512]{2,1,0:T(8,128)(2,1)S(1)}, bf16[2,128,512]{2,1,0:T(8,128)(2,1)S(1)}, u32[]{:S(2)}, u32[]{:S(2)}) collective-permute-start(bf16[2,128,512]{2,1,0:T(8,128)(2,1)S(1)} %collective-permute-done.17.refs_3_), channel_id=1, source_target_pairs={{0,4},{4,0},{8,12},{12,8},{16,20},{20,16},{24,28},{28,24},{1,5},{5... | collective-permute-start | bytes 786440 | tf_op jit(solution)/shard_map/ppermute | solution.py:235
  59.9 13.5 %collective-permute-start.19 = (bf16[2,128,512]{2,1,0:T(8,128)(2,1)S(1)}, bf16[2,128,512]{2,1,0:T(8,128)(2,1)S(1)}, u32[]{:S(2)}, u32[]{:S(2)}) collective-permute-start(bf16[2,128,512]{2,1,0:T(8,128)(2,1)S(1)} %maximum_select_fusion.1.refs_5_), channel_id=1, source_target_pairs={{0,4},{8,12},{16,20},{24,28},{1,5},{9,13},{17,21},{25,29},{2,6},{1... | collective-permute-start | bytes 786440 | tf_op jit(solution)/shard_map/ppermute | solution.py:226
  61.1 12.2 %collective-permute-start.18 = (bf16[2,128,512]{2,1,0:T(8,128)(2,1)S(1)}, bf16[2,128,512]{2,1,0:T(8,128)(2,1)S(1)}, u32[]{:S(2)}, u32[]{:S(2)}) collective-permute-start(bf16[2,128,512]{2,1,0:T(8,128)(2,1)S(1)} %collective-permute-done.17.refs_3_), channel_id=1, source_target_pairs={{0,8},{4,12},{8,16},{12,20},{16,24},{20,28},{1,9},{5,13},{9,17},{1... | collective-permute-start | bytes 786440 | tf_op jit(solution)/shard_map/ppermute | solution.py:221
  65.3 10.8 %collective-permute-start.20 = (bf16[2,128,512]{2,1,0:T(8,128)(2,1)S(1)}, bf16[2,128,512]{2,1,0:T(8,128)(2,1)S(1)}, u32[]{:S(2)}, u32[]{:S(2)}) collective-permute-start(bf16[2,128,512]{2,1,0:T(8,128)(2,1)S(1)} %collective-permute-done.17.refs_3_), channel_id=1, source_target_pairs={{4,8},{12,16},{20,24},{5,9},{13,17},{21,25},{6,10},{14,18},{22,26}... | collective-permute-start | bytes 786440 | tf_op jit(solution)/shard_map/ppermute | solution.py:249
  71.2 23.9 %collective-permute-start.23 = (bf16[256,1024]{1,0:T(8,128)(2,1)S(1)}, bf16[256,1024]{1,0:T(8,128)(2,1)S(1)}, u32[]{:S(2)}, u32[]{:S(2)}) collective-permute-start(bf16[256,1024]{1,0:T(8,128)(2,1)S(1)} %get-tuple-element.118), channel_id=1, source_target_pairs={{0,8},{1,7},{2,10},{3,5},{4,12},{5,3},{6,14},{7,1},{8,16},{9,15},{... | collective-permute-start | bytes 1572872 | tf_op jit(solution)/shard_map/ppermute | solution.py:267
  73.3 23.7 %collective-permute-start.24 = (bf16[256,1024]{1,0:T(8,128)(2,1)S(1)}, bf16[256,1024]{1,0:T(8,128)(2,1)S(1)}, u32[]{:S(2)}, u32[]{:S(2)}) collective-permute-start(bf16[256,1024]{1,0:T(8,128)(2,1)S(1)} %get-tuple-element.119), channel_id=1, source_target_pairs={{0,16},{1,5},{2,18},{3,7},{4,20},{5,1},{6,22},{7,3},{8,24},{9,13},... | collective-permute-start | bytes 1572872 | tf_op jit(solution)/shard_map/ppermute | solution.py:267
  73.3 25.0 %collective-permute-start.25 = (bf16[256,1024]{1,0:T(8,128)(2,1)S(1)}, bf16[256,1024]{1,0:T(8,128)(2,1)S(1)}, u32[]{:S(2)}, u32[]{:S(2)}) collective-permute-start(bf16[256,1024]{1,0:T(8,128)(2,1)S(1)} %get-tuple-element.120), channel_id=1, source_target_pairs={{0,24},{1,3},{2,26},{3,1},{4,28},{5,7},{6,30},{7,5},{8,0},{9,11},{... | collective-permute-start | bytes 1572872 | tf_op jit(solution)/shard_map/ppermute | solution.py:267
  95.1 8.8 %collective-permute-start.27 = (bf16[2,128,512]{2,1,0:T(8,128)(2,1)S(1)}, bf16[2,128,512]{2,1,0:T(8,128)(2,1)S(1)}, u32[]{:S(2)}, u32[]{:S(2)}) collective-permute-start(bf16[2,128,512]{2,1,0:T(8,128)(2,1)S(1)} %get-tuple-element.123), channel_id=1, source_target_pairs={{8,0},{12,4},{16,8},{20,12},{24,16},{28,20},{9,1},{13,5},{17,9},{2... | collective-permute-start | bytes 786440 | tf_op jit(solution)/shard_map/ppermute | solution.py:221
  97.0 11.8 %collective-permute-start.28 = (bf16[2,128,512]{2,1,0:T(8,128)(2,1)S(1)}, bf16[2,128,512]{2,1,0:T(8,128)(2,1)S(1)}, u32[]{:S(2)}, u32[]{:S(2)}) collective-permute-start(bf16[2,128,512]{2,1,0:T(8,128)(2,1)S(1)} %get-tuple-element.116), channel_id=1, source_target_pairs={{8,4},{16,12},{24,20},{9,5},{17,13},{25,21},{10,6},{18,14},{26,22}... | collective-permute-start | bytes 786440 | tf_op jit(solution)/shard_map/ppermute | solution.py:249
  98.4 12.5 %collective-permute-start.22 = (bf16[2,128,512]{2,1,0:T(8,128)(2,1)S(1)}, bf16[2,128,512]{2,1,0:T(8,128)(2,1)S(1)}, u32[]{:S(2)}, u32[]{:S(2)}) collective-permute-start(bf16[2,128,512]{2,1,0:T(8,128)(2,1)S(1)} %get-tuple-element.116), channel_id=1, source_target_pairs={{4,0},{12,8},{20,16},{28,24},{5,1},{13,9},{21,17},{29,25},{6,2},{1... | collective-permute-start | bytes 786440 | tf_op jit(solution)/shard_map/ppermute | solution.py:226
  122.3 8.3 %collective-permute-start.32 = (bf16[256,512]{1,0:T(8,128)(2,1)S(1)}, bf16[256,512]{1,0:T(8,128)(2,1)S(1)}, u32[]{:S(2)}, u32[]{:S(2)}) collective-permute-start(bf16[256,512]{1,0:T(8,128)(2,1)S(1)} %pad_maximum_fusion), channel_id=1, source_target_pairs={{0,16},{1,5},{2,18},{3,7},{4,20},{5,1},{6,22},{7,3},{8,24},{9,13},... | collective-permute-start | bytes 786440 | tf_op jit(solution)/shard_map/ppermute | solution.py:267
  123.7 7.8 %collective-permute-start.33 = (bf16[256,512]{1,0:T(8,128)(2,1)S(1)}, bf16[256,512]{1,0:T(8,128)(2,1)S(1)}, u32[]{:S(2)}, u32[]{:S(2)}) collective-permute-start(bf16[256,512]{1,0:T(8,128)(2,1)S(1)} %pad_maximum_fusion), channel_id=1, source_target_pairs={{0,24},{1,3},{2,26},{3,1},{4,28},{5,7},{6,30},{7,5},{8,0},{9,11},{... | collective-permute-start | bytes 786440 | tf_op jit(solution)/shard_map/ppermute | solution.py:267
  132.2 12.6 %collective-permute-start.34 = (bf16[256,512]{1,0:T(8,128)(2,1)S(1)}, bf16[256,512]{1,0:T(8,128)(2,1)S(1)}, u32[]{:S(2)}, u32[]{:S(2)}) collective-permute-start(bf16[256,512]{1,0:T(8,128)(2,1)S(1)} %get-tuple-element.138), channel_id=1, source_target_pairs={{1,9},{0,6},{3,11},{2,4},{5,13},{4,2},{7,15},{6,0},{9,17},{8,14},{... | collective-permute-start | bytes 786440 | tf_op jit(solution)/shard_map/ppermute | solution.py:267
  133.7 13.9 %collective-permute-start.35 = (bf16[256,512]{1,0:T(8,128)(2,1)S(1)}, bf16[256,512]{1,0:T(8,128)(2,1)S(1)}, u32[]{:S(2)}, u32[]{:S(2)}) collective-permute-start(bf16[256,512]{1,0:T(8,128)(2,1)S(1)} %get-tuple-element.137), channel_id=1, source_target_pairs={{1,17},{0,4},{3,19},{2,6},{5,21},{4,0},{7,23},{6,2},{9,25},{8,12},... | collective-permute-start | bytes 786440 | tf_op jit(solution)/shard_map/ppermute | solution.py:267
  135.5 14.1 %collective-permute-start.36 = (bf16[256,512]{1,0:T(8,128)(2,1)S(1)}, bf16[256,512]{1,0:T(8,128)(2,1)S(1)}, u32[]{:S(2)}, u32[]{:S(2)}) collective-permute-start(bf16[256,512]{1,0:T(8,128)(2,1)S(1)} %get-tuple-element.136), channel_id=1, source_target_pairs={{1,25},{0,2},{3,27},{2,0},{5,29},{4,6},{7,31},{6,4},{9,1},{8,10},{... | collective-permute-start | bytes 786440 | tf_op jit(solution)/shard_map/ppermute | solution.py:267
  149.7 9.9 %collective-permute-start.38 = (f32[256,512]{1,0:T(8,128)S(1)}, f32[256,512]{1,0:T(8,128)S(1)}, u32[]{:S(2)}, u32[]{:S(2)}) collective-permute-start(f32[256,512]{1,0:T(8,128)S(1)} %fusion.3), channel_id=1, source_target_pairs={{0,1},{1,0},{2,3},{3,2},{4,5},{5,4},{6,7},{7,6},{8,9},{9,8},{10,11... | collective-permute-start | bytes 1572872 | tf_op jit(solution)/shard_map/ppermute | solution.py:243
  (21 other events, 213.2 us)

commit v4 on v3

--- a/solution.py
+++ b/solution.py
@@ -123,66 +123,83 @@
 
 def attend_kernel(inner, flags, q_ref, g_ref, *refs):
     c_ref, b_ref, e_ref, a_ref, d_ref, own_ref = refs[:6]
-    o_ref, dq_ref, far_c, far_be, far_a, far_d, near, bias, acc_k, acc_v = refs[6:]
+    o_ref, dq_ref, far_c, far_be, far_a, far_d, near = refs[6:13]
+    k_held, v_held, acc_k, acc_v = refs[13:]
     tok = q_ref.shape[0]
     scale = 1.0 / math.sqrt(HEAD_DIM)
     scale_log2 = scale * math.log2(math.e)
     even = inner[0] == 0
-
-    @pl.when(pl.program_id(0) == 0)
-    def _():
+    backs = (
+        flags[0, 3],
+        jnp.where(even, flags[0, 2], flags[0, 0]),
+        flags[0, 1],
+        jnp.where(even, flags[0, 0], flags[0, 2]),
+    )
+    count, places = jnp.int32(1), []
+    for back in backs:
+        places.append(pl.ds(pl.multiple_of(count * BLOCK, BLOCK), BLOCK))
+        count = count + jnp.where(back > 0, 1, 0)
+
+    for slot, held in ((0, k_held), (1, v_held)):
+        held[:BLOCK] = own_ref[slot]
+        for j, (back, place) in enumerate(zip(backs, places)):
+
+            @pl.when(back > 0)
+            def _(slot=slot, held=held, j=j, place=place):
+                if j == 1:
+                    held[place, :] = jnp.where(even, e_ref[slot], b_ref[slot])
+                else:
+                    held[place, :] = (c_ref, None, a_ref, d_ref)[j][slot]
+
+    def work(win):
+        k, v = k_held[:win], v_held[:win]
         row = lax.broadcasted_iota(jnp.int32, (2 * tok, BLOCK), 0) % tok
         col = lax.broadcasted_iota(jnp.int32, (2 * tok, BLOCK), 1)
-        backs = (
-            flags[0, 3],
-            jnp.where(even, flags[0, 2], flags[0, 0]),
-            flags[0, 1],
-            jnp.where(even, flags[0, 0], flags[0, 2]),
-        )
-        for j, back in enumerate(backs):
-            flag = jnp.full((2 * tok, BLOCK), back, jnp.int32)
-            bias[:, j * BLOCK : (j + 1) * BLOCK] = jnp.where(flag > 0, 0.0, -jnp.inf)
-        bias[:, REACH * BLOCK :] = jnp.where(col <= row, 0.0, -jnp.inf)
-
-    def window(slot):
-        either = jnp.where(even, e_ref[slot], b_ref[slot])
-        return jnp.concatenate(
-            [c_ref[slot], either, a_ref[slot], d_ref[slot], own_ref[slot]], axis=0
-        )
-
-    k, v = window(0), window(1)
-    pairs = GROUPS // 2
-    for p in range(pairs):
-        lo = slice(2 * p * HEAD_DIM, (2 * p + 1) * HEAD_DIM)
-        hi = slice((2 * p + 1) * HEAD_DIM, (2 * p + 2) * HEAD_DIM)
-        q2 = jnp.concatenate([q_ref[:, lo], q_ref[:, hi]], axis=0)
-        g2 = jnp.concatenate([g_ref[:, lo], g_ref[:, hi]], axis=0)
-        s = dot(q2, k, NT) * scale_log2 + bias[...]
-        top = jnp.max(s, axis=1, keepdims=True)
-        e = jnp.exp2(s - top)
-        share = e * (1.0 / jnp.sum(e, axis=1, keepdims=True))
-        prob = share.astype(jnp.bfloat16)
-        o = dot(prob, v, NN).astype(jnp.bfloat16)
-        o_ref[:, lo] = o[:tok]
-        o_ref[:, hi] = o[tok:]
-        delta = jnp.sum(g2.astype(jnp.float32) * o.astype(jnp.float32), axis=1, keepdims=True)
-        dp = dot(g2, v, NT)
-        ds = (share * ((dp - delta) * scale)).astype(jnp.bfloat16)
-        dq = dot(ds, k, NN).astype(jnp.bfloat16)
-        dq_ref[:, lo] = dq[:tok]
-        dq_ref[:, hi] = dq[tok:]
-        part_k = dot(q2, ds, TN)
-        part_v = dot(g2, prob, TN)
-        if p == 0:
-            acc_k[...] = part_k
-            acc_v[...] = part_v
-        elif p < pairs - 1:
-            acc_k[...] += part_k
-            acc_v[...] += part_v
-        else:
-            for slot, total in ((0, (acc_k[...] + part_k).T), (1, (acc_v[...] + part_v).T)):
-                for j, ref in enumerate((far_c, far_be, far_a, far_d, near)):
-                    ref[slot] = total[j * BLOCK : (j + 1) * BLOCK].astype(ref.dtype)
+        seen = col <= row
+        for p in range(GROUPS // 2):
+            lo = slice(2 * p * HEAD_DIM, (2 * p + 1) * HEAD_DIM)
+            hi = slice((2 * p + 1) * HEAD_DIM, (2 * p + 2) * HEAD_DIM)
+            q2 = jnp.concatenate([q_ref[:, lo], q_ref[:, hi]], axis=0)
+            g2 = jnp.concatenate([g_ref[:, lo], g_ref[:, hi]], axis=0)
+            s = dot(q2, k, NT) * scale_log2
+            own = jnp.where(seen, s[:, :BLOCK], -jnp.inf)
+            s = jnp.concatenate([own, s[:, BLOCK:]], axis=1) if win > BLOCK else own
+            top = jnp.max(s, axis=1, keepdims=True)
+            e = jnp.exp2(s - top)
+            share = e * (1.0 / jnp.sum(e, axis=1, keepdims=True))
+            prob = share.astype(jnp.bfloat16)
+            o = dot(prob, v, NN).astype(jnp.bfloat16)
+            o_ref[:, lo] = o[:tok]
+            o_ref[:, hi] = o[tok:]
+            delta = jnp.sum(g2.astype(jnp.float32) * o.astype(jnp.float32), axis=1, keepdims=True)
+            dp = dot(g2, v, NT)
+            ds = (share * ((dp - delta) * scale)).astype(jnp.bfloat16)
+            dq = dot(ds, k, NN).astype(jnp.bfloat16)
+            dq_ref[:, lo] = dq[:tok]
+            dq_ref[:, hi] = dq[tok:]
+            part_k = dot(q2, ds, TN)
+            part_v = dot(g2, prob, TN)
+            if p == 0:
+                acc_k[:, :win] = part_k
+                acc_v[:, :win] = part_v
+            else:
+                acc_k[:, :win] += part_k
+                acc_v[:, :win] += part_v
+
+    for tiles in range(1, REACH + 2):
+        pl.when(count == tiles)(functools.partial(work, tiles * BLOCK))
+
+    for slot, acc in ((0, acc_k), (1, acc_v)):
+        near[slot] = acc[:, :BLOCK].T
+        for ref, back, place in zip((far_c, far_be, far_a, far_d), backs, places):
+
+            @pl.when(back > 0)
+            def _(slot=slot, acc=acc, ref=ref, place=place):
+                ref[slot] = acc[:, place].T.astype(ref.dtype)
+
+            @pl.when(back <= 0)
+            def _(slot=slot, ref=ref):
+                ref[slot] = jnp.zeros(ref.shape[1:], ref.dtype)
 
 
 def attend(queries, grads, pieces, flags, inner):
@@ -201,7 +218,8 @@
         out_shape=[jax.ShapeDtypeStruct(queries.shape, jnp.bfloat16)] * 2
         + [jax.ShapeDtypeStruct((2, tok, key_width), t) for t in types],
         scratch_shapes=[
-            pltpu.VMEM((2 * tok, win), jnp.float32),
+            pltpu.VMEM((win, HEAD_DIM), jnp.bfloat16),
+            pltpu.VMEM((win, HEAD_DIM), jnp.bfloat16),
             pltpu.VMEM((HEAD_DIM, win), jnp.float32),
             pltpu.VMEM((HEAD_DIM, win), jnp.float32),
         ],
@@ -213,6 +231,27 @@
         ),
         name="attend",
     )(inner, flags, queries, grads, *pieces)
+
+
+def deal_kernel(owner, tile_ref, _, own_ref, *outs):
+    rows = own_ref.shape[0]
+    for r, ref in enumerate((own_ref,) + outs):
+        at = pl.ds(pl.multiple_of(owner[r] * rows, rows), rows)
+        ref[...] = tile_ref[at, :].astype(ref.dtype)
+
+
+def deal(owner, tile, token):
+    vmem = pl.BlockSpec(memory_space=pltpu.VMEM)
+    shape = (tile.shape[0] // 4, tile.shape[1])
+    return pl.pallas_call(
+        deal_kernel,
+        in_specs=[pl.BlockSpec(memory_space=pltpu.SMEM), vmem, vmem],
+        out_specs=[vmem] * 4,
+        out_shape=[jax.ShapeDtypeStruct(shape, jnp.float32)]
+        + [jax.ShapeDtypeStruct(shape, jnp.bfloat16)] * 3,
+        compiler_params=pltpu.CompilerParams(vmem_limit_bytes=8 << 20),
+        name="deal",
+    )(owner, tile, token)
 
 
 def outer_step(x, by):
@@ -332,7 +371,7 @@
     cut = [jnp.where(core == 0, to_outer[r] * 4 + k, k * 4 + to_plane[r]) for r in range(4) for k in range(4)] if mixed else [x]
     known = {
         "cut": jnp.stack(cut).astype(jnp.int32).reshape(-1, 4 if mixed else 1),
-        "owner": [jnp.where(core == 0, p, o).astype(jnp.uint32) for p, o in zip(to_plane, to_outer)],
+        "owner": jnp.stack([jnp.where(core == 0, p, o) for p, o in zip(to_plane, to_outer)]).astype(jnp.int32),
         "early": places(early or late),
         "late": places(late),
         "flat": jnp.stack([spots[r][0] * 4 + v for r in order for v in plane]).astype(jnp.int32),
@@ -467,14 +506,10 @@
         return swap(t.astype(jnp.bfloat16)).astype(jnp.float32)
 
     if mixed:
-        tile = tile.reshape(4, rows, half)
-        tile, _ = tie((tile, swap_core(tile[0, :8, :HEAD_DIM])))
-        arrived = [
-            crossed(pick(tile, known["owner"][r], 0).astype(jnp.bfloat16), r, 1, 0)
-            for r in range(1, 4)
-        ]
+        token = swap_core(tile[:8, :HEAD_DIM])
+        grad_half, *leaving = deal(known["owner"], tile, token)
+        arrived = [crossed(leaving[r - 1], r, 1, 0) for r in range(1, 4)]
         arrived, grad_in = tie((arrived, grad_in))
-        grad_half = pick(tile, known["owner"][0], 0)
         for t in arrived:
             grad_half += t.astype(jnp.float32)
     else:

time: 161 us -> 158 us (0.981)
  starting transfers between devices: 62.6 us -> 56.6 us
  waiting for transfers between devices: 63 us -> 68 us
  Pallas kernels: 24.6 us -> 22.3 us
    ppermute x4, waiting for transfers between devices: 14.4 us -> 20.8 us  [outer_step(): lax.ppermute(x, 'ctx', [(i, i + by) for i in range(peers) if 0 <= i + by...]
    ppermute x5 -> x6, starting transfers between devices: 19.1 us -> 14.6 us  [swap_core(): return lax.ppermute(x, 'dp', [(0, 1), (1, 0)])]
    pallas_call x1, Pallas kernels: 17.8 us -> 14.9 us  [attend(): pl.pallas_call(attend_kernel, grid=(key_width // HEAD_DIM,), in_specs=[sm...]
    ppermute x5, waiting for transfers between devices: 4.23 us -> 6.77 us  [swap_fsdp(): return lax.ppermute(x, 'fsdp', [(0, 1), (1, 0)])]
    ppermute x5, waiting for transfers between devices: 13.8 us -> 11.3 us  [outer_shift(): lax.ppermute(x, 'ctx', [(i, (i + INNER * by) % peers) for i in range(peer...]
    ppermute x9, waiting for transfers between devices: 15.3 us -> 12.8 us  [crossed(): return lax.ppermute(x, ('ctx', 'fsdp', 'dp'), pairs)]
    ppermute x5, starting transfers between devices: 5.18 us -> 3.22 us  [swap_fsdp(): return lax.ppermute(x, 'fsdp', [(0, 1), (1, 0)])]
    ppermute x7, waiting for transfers between devices: 2.68 us -> 4.59 us  [swap_inner(): lax.ppermute(x, 'ctx', [(i, i ^ 1) for i in range(lax.axis_size('ctx'))])]
  transfers between devices with their start and end apart: 39 -> 40, of which waited for: 25 -> 24; matrix products, arithmetic and copies ran while one was open for 4% -> 4% of each run, Pallas kernels for 14% -> 13%
where the time goes in v4:
time: 158 us; the launch traced here: 157 us
  waiting for transfers between devices  68 us (43%)
  starting transfers between devices  56.6 us (36%)
  Pallas kernels  22.3 us (14%)
  matrix products  5.91 us (4%)
  local copies, waits for them, and re-layouts  1.97 us (1%)
  other arithmetic  1.69 us (1%)
    ppermute x4, waiting for transfers between devices, outer_step(): lax.ppermute(x, 'ctx', [(i, i + by) for i in range(peers) if 0 <= i + by...  20.8 us
    pallas_call x1, Pallas kernels, attend(): pl.pallas_call(attend_kernel, grid=(key_width // HEAD_DIM,), in_specs=[sm...  14.9 us
    ppermute x6, starting transfers between devices, swap_core(): return lax.ppermute(x, 'dp', [(0, 1), (1, 0)])  14.6 us
    ppermute x9, waiting for transfers between devices, crossed(): return lax.ppermute(x, ('ctx', 'fsdp', 'dp'), pairs)  12.8 us
    ppermute x4, starting transfers between devices, outer_step(): lax.ppermute(x, 'ctx', [(i, i + by) for i in range(peers) if 0 <= i + by...  11.7 us
    ppermute x5, waiting for transfers between devices, outer_shift(): lax.ppermute(x, 'ctx', [(i, (i + INNER * by) % peers) for i in range(peer...  11.3 us
    ppermute x2, starting transfers between devices, odd_step(): lax.ppermute(x, 'ctx', [(i, i + by) for i in range(start, peers, 2) if 0...  7.13 us
    ppermute x9, starting transfers between devices, crossed(): return lax.ppermute(x, ('ctx', 'fsdp', 'dp'), pairs)  7.03 us
  transfers between devices with their start and end apart: 40, of which 24 were waited for; matrix products, arithmetic and copies ran while one was open for 4% of the time, Pallas kernels for 13%

profile of v4, /device:TPU:11, one launch (start us, length us, event | category | flops | bytes accessed | tf_op | source)
XLA Modules:
  0.0 157.5 jit_solution(13873901416524371156)
XLA Ops:
  13.5 3.4 %collective-permute-done.6.refs_5_ = bf16[256,512]{1,0:T(8,128)(2,1)S(1)} collective-permute-done((bf16[256,512]{1,0:T(8,128)(2,1)S(1)}, bf16[256,512]{1,0:T(8,128)(2,1)S(1)}, u32[]{:S(2)}, u32[]{:S(2)}) %collective-permute-start.6) | collective-permute-done | bytes 262176 | tf_op jit(solution)/shard_map/ppermute | solution.py:274
  21.0 3.1 %collective-permute-done.11.refs_10_ = bf16[256,512]{1,0:T(8,128)(2,1)S(1)} collective-permute-done((bf16[256,512]{1,0:T(8,128)(2,1)S(1)}, bf16[256,512]{1,0:T(8,128)(2,1)S(1)}, u32[]{:S(2)}, u32[]{:S(2)}) %collective-permute-start.11) | collective-permute-done | bytes 262176 | tf_op jit(solution)/shard_map/ppermute | solution.py:278
  27.5 3.7 %collective-permute-done.8.refs_7_ = bf16[256,512]{1,0:T(8,128)(2,1)S(1)} collective-permute-done((bf16[256,512]{1,0:T(8,128)(2,1)S(1)}, bf16[256,512]{1,0:T(8,128)(2,1)S(1)}, u32[]{:S(2)}, u32[]{:S(2)}) %collective-permute-start.8) | collective-permute-done | bytes 262176 | tf_op jit(solution)/shard_map/ppermute | solution.py:270
  34.3 3.8 %collective-permute-done.12.refs_11_ = bf16[256,512]{1,0:T(8,128)(2,1)S(1)} collective-permute-done((bf16[256,512]{1,0:T(8,128)(2,1)S(1)}, bf16[256,512]{1,0:T(8,128)(2,1)S(1)}, u32[]{:S(2)}, u32[]{:S(2)}) %collective-permute-start.12) | collective-permute-done | bytes 262176 | tf_op jit(solution)/shard_map/ppermute | solution.py:270
  38.2 2.6 %project.2.refs_4_ = f32[256,512]{1,0:T(8,128)S(1)} custom-call(s32[3,5]{1,0:T(4,128)S(1)} %reshape.25.spots, bf16[128,4096]{1,0:T(8,128)(2,1)S(1)} %bitcast.72, bf16[128,4096]{1,0:T(8,128)(2,1)S(1)} %collective-permute-done.3.theirs_ref, bf16[256,512]{1,0:T(8,128)(2,1)S(1)} %constant_dynamic-slice_fusion.refs_0_, ...), custom_call_target="tpu_custom_call" | custom-call | tf_op jit(solution)/shard_map/project/pallas_call | solution.py:70
  42.3 4.6 %collective-permute-start.16 = (bf16[128,512]{1,0:T(8,128)(2,1)S(1)}, bf16[128,512]{1,0:T(8,128)(2,1)S(1)}, u32[]{:S(2)}, u32[]{:S(2)}) collective-permute-start(bf16[128,512]{1,0:T(8,128)(2,1)S(1)} %get-tuple-element.141), channel_id=1, source_target_pairs={{0,1},{1,0},{2,3},{3,2},{4,5},{5,4},{6,7},{7,6},{8,9},{9,8},{10,11... | collective-permute-start | bytes 393224 | tf_op jit(solution)/shard_map/ppermute | solution.py:282
  47.9 3.5 %collective-permute-start.17 = (bf16[2,128,512]{2,1,0:T(8,128)(2,1)S(1)}, bf16[2,128,512]{2,1,0:T(8,128)(2,1)S(1)}, u32[]{:S(2)}, u32[]{:S(2)}) collective-permute-start(bf16[2,128,512]{2,1,0:T(8,128)(2,1)S(1)} %maximum_select_fusion.1.refs_5_), channel_id=1, source_target_pairs={{0,8},{4,12},{8,16},{12,20},{16,24},{20,28},{1,9},{5,13},{9,17},{1... | collective-permute-start | bytes 786440 | tf_op jit(solution)/shard_map/ppermute | solution.py:260
  52.9 6.1 %collective-permute-done.17.refs_3_ = bf16[2,128,512]{2,1,0:T(8,128)(2,1)S(1)} collective-permute-done((bf16[2,128,512]{2,1,0:T(8,128)(2,1)S(1)}, bf16[2,128,512]{2,1,0:T(8,128)(2,1)S(1)}, u32[]{:S(2)}, u32[]{:S(2)}) %collective-permute-start.17) | collective-permute-done | bytes 262176 | tf_op jit(solution)/shard_map/ppermute | solution.py:260
  61.9 5.8 %collective-permute-start.20 = (bf16[2,128,512]{2,1,0:T(8,128)(2,1)S(1)}, bf16[2,128,512]{2,1,0:T(8,128)(2,1)S(1)}, u32[]{:S(2)}, u32[]{:S(2)}) collective-permute-start(bf16[2,128,512]{2,1,0:T(8,128)(2,1)S(1)} %collective-permute-done.17.refs_3_), channel_id=1, source_target_pairs={{4,8},{12,16},{20,24},{5,9},{13,17},{21,25},{6,10},{14,18},{22,26}... | collective-permute-start | bytes 786440 | tf_op jit(solution)/shard_map/ppermute | solution.py:288
  67.8 4.1 %collective-permute-start.18 = (bf16[2,128,512]{2,1,0:T(8,128)(2,1)S(1)}, bf16[2,128,512]{2,1,0:T(8,128)(2,1)S(1)}, u32[]{:S(2)}, u32[]{:S(2)}) collective-permute-start(bf16[2,128,512]{2,1,0:T(8,128)(2,1)S(1)} %collective-permute-done.17.refs_3_), channel_id=1, source_target_pairs={{0,8},{4,12},{8,16},{12,20},{16,24},{20,28},{1,9},{5,13},{9,17},{1... | collective-permute-start | bytes 786440 | tf_op jit(solution)/shard_map/ppermute | solution.py:260
  74.7 3.8 %collective-permute-done.18.refs_0_ = bf16[2,128,512]{2,1,0:T(8,128)(2,1)S(1)} collective-permute-done((bf16[2,128,512]{2,1,0:T(8,128)(2,1)S(1)}, bf16[2,128,512]{2,1,0:T(8,128)(2,1)S(1)}, u32[]{:S(2)}, u32[]{:S(2)}) %collective-permute-start.18) | collective-permute-done | bytes 262176 | tf_op jit(solution)/shard_map/ppermute | solution.py:260
  78.6 14.9 %attend.1 = (bf16[128,4096]{1,0:T(8,128)(2,1)}, bf16[128,4096]{1,0:T(8,128)(2,1)}, bf16[2,128,512]{2,1,0:T(8,128)(2,1)S(1)}, bf16[2,128,512]{2,1,0:T(8,128)(2,1)...) custom-call(s32[1]{0:T(128)} %bitcast.39.inner, ...), custom_call_target="tpu_custom_call" | custom-call | flops 4026531840 | bytes 15990784 | tf_op jit(solution)/shard_map/attend/pallas_call | solution.py:213
  96.8 3.4 %collective-permute-start.22 = (bf16[2,128,512]{2,1,0:T(8,128)(2,1)S(1)}, bf16[2,128,512]{2,1,0:T(8,128)(2,1)S(1)}, u32[]{:S(2)}, u32[]{:S(2)}) collective-permute-start(bf16[2,128,512]{2,1,0:T(8,128)(2,1)S(1)} %get-tuple-element.118), channel_id=1, source_target_pairs={{4,0},{12,8},{20,16},{28,24},{5,1},{13,9},{21,17},{29,25},{6,2},{1... | collective-permute-start | bytes 786440 | tf_op jit(solution)/shard_map/ppermute | solution.py:265
  100.2 5.8 %collective-permute-done.27 = bf16[2,128,512]{2,1,0:T(8,128)(2,1)S(1)} collective-permute-done((bf16[2,128,512]{2,1,0:T(8,128)(2,1)S(1)}, bf16[2,128,512]{2,1,0:T(8,128)(2,1)S(1)}, u32[]{:S(2)}, u32[]{:S(2)}) %collective-permute-start.27) | collective-permute-done | bytes 262176 | tf_op jit(solution)/shard_map/ppermute | solution.py:260
  106.0 5.6 %collective-permute-done.28 = bf16[2,128,512]{2,1,0:T(8,128)(2,1)S(1)} collective-permute-done((bf16[2,128,512]{2,1,0:T(8,128)(2,1)S(1)}, bf16[2,128,512]{2,1,0:T(8,128)(2,1)S(1)}, u32[]{:S(2)}, u32[]{:S(2)}) %collective-permute-start.28) | collective-permute-done | bytes 262176 | tf_op jit(solution)/shard_map/ppermute | solution.py:288
  111.8 2.1 %collective-permute-start.29 = (bf16[2,128,512]{2,1,0:T(8,128)(2,1)S(1)}, bf16[2,128,512]{2,1,0:T(8,128)(2,1)S(1)}, u32[]{:S(2)}, u32[]{:S(2)}) collective-permute-start(bf16[2,128,512]{2,1,0:T(8,128)(2,1)S(1)} %add_convert_fusion.1), channel_id=1, source_target_pairs={{8,0},{12,4},{16,8},{20,12},{24,16},{28,20},{9,1},{13,5},{17,9},{2... | collective-permute-start | bytes 786440 | tf_op jit(solution)/shard_map/ppermute | solution.py:260
  113.9 5.0 %collective-permute-done.29 = bf16[2,128,512]{2,1,0:T(8,128)(2,1)S(1)} collective-permute-done((bf16[2,128,512]{2,1,0:T(8,128)(2,1)S(1)}, bf16[2,128,512]{2,1,0:T(8,128)(2,1)S(1)}, u32[]{:S(2)}, u32[]{:S(2)}) %collective-permute-start.29) | collective-permute-done | bytes 262176 | tf_op jit(solution)/shard_map/ppermute | solution.py:260
  119.0 3.6 %collective-permute-start.30 = (bf16[128,512]{1,0:T(8,128)(2,1)S(1)}, bf16[128,512]{1,0:T(8,128)(2,1)S(1)}, u32[]{:S(2)}, u32[]{:S(2)}) collective-permute-start(bf16[128,512]{1,0:T(8,128)(2,1)S(1)} %get-tuple-element.139), channel_id=1, source_target_pairs={{0,1},{1,0},{2,3},{3,2},{4,5},{5,4},{6,7},{7,6},{8,9},{9,8},{10,11... | collective-permute-start | bytes 393224 | tf_op jit(solution)/shard_map/ppermute | solution.py:282
  123.7 2.2 %collective-permute-start.31 = (bf16[256,512]{1,0:T(8,128)(2,1)S(1)}, bf16[256,512]{1,0:T(8,128)(2,1)S(1)}, u32[]{:S(2)}, u32[]{:S(2)}) collective-permute-start(bf16[256,512]{1,0:T(8,128)(2,1)S(1)} %pad_maximum_fusion), channel_id=1, source_target_pairs={{0,8},{1,7},{2,10},{3,5},{4,12},{5,3},{6,14},{7,1},{8,16},{9,15},{... | collective-permute-start | bytes 786440 | tf_op jit(solution)/shard_map/ppermute | solution.py:306
  126.8 5.7 %collective-permute-done.31 = bf16[256,512]{1,0:T(8,128)(2,1)S(1)} collective-permute-done((bf16[256,512]{1,0:T(8,128)(2,1)S(1)}, bf16[256,512]{1,0:T(8,128)(2,1)S(1)}, u32[]{:S(2)}, u32[]{:S(2)}) %collective-permute-start.31) | collective-permute-done | bytes 262176 | tf_op jit(solution)/shard_map/ppermute | solution.py:306
  134.7 4.6 %collective-permute-start.34 = (f32[8,128]{1,0:T(8,128)S(1)}, f32[8,128]{1,0:T(8,128)S(1)}, u32[]{:S(2)}, u32[]{:S(2)}) collective-permute-start(f32[8,128]{1,0:T(8,128)S(1)} %slice.26), channel_id=1, source_target_pairs={{0,1},{1,0},{2,3},{3,2},{4,5},{5,4},{6,7},{7,6},{8,9},{9,8},{10,11... | collective-permute-start | bytes 12296 | tf_op jit(solution)/shard_map/ppermute | solution.py:282
  145.2 2.5 %fusion = bf16[128,4096]{1,0:T(8,128)(2,1)} fusion(f32[128,4096]{1,0:T(8,128)S(1)} %fusion.4, bf16[128,512]{1,0:T(8,128)(2,1)S(1)} %get-tuple-element.138, bf16[4096,512]{1,0:T(8,128)(2,1)S(1)} %assemble.1), kind=kOutput, calls=%fused_computation.1 | convolution fusion | flops 537919488 | bytes 7471104 | tf_op jit(solution)/shard_map/dot_general | solution.py:26
  147.7 3.7 %collective-permute-done.35 = bf16[256,512]{1,0:T(8,128)(2,1)S(1)} collective-permute-done((bf16[256,512]{1,0:T(8,128)(2,1)S(1)}, bf16[256,512]{1,0:T(8,128)(2,1)S(1)}, u32[]{:S(2)}, u32[]{:S(2)}) %collective-permute-start.35) | collective-permute-done | bytes 262176 | tf_op jit(solution)/shard_map/ppermute | solution.py:306
  151.4 2.8 %collective-permute-done.36 = bf16[256,512]{1,0:T(8,128)(2,1)S(1)} collective-permute-done((bf16[256,512]{1,0:T(8,128)(2,1)S(1)}, bf16[256,512]{1,0:T(8,128)(2,1)S(1)}, u32[]{:S(2)}, u32[]{:S(2)}) %collective-permute-start.36) | collective-permute-done | bytes 262176 | tf_op jit(solution)/shard_map/ppermute | solution.py:306
  (97 shorter events, 49.9 us)
Async XLA Ops:
  2.2 7.6 %collective-permute-start.2 = (bf16[256,512]{1,0:T(8,128)(2,1)S(1)}, bf16[256,512]{1,0:T(8,128)(2,1)S(1)}, u32[]{:S(2)}, u32[]{:S(2)}) collective-permute-start(bf16[256,512]{1,0:T(8,128)(2,1)S(1)} %constant_dynamic-slice_fusion.refs_0_), channel_id=1, source_target_pairs={{0,2},{2,0},{1,3},{3,1},{4,6},{6,4},{5,7},{7,5},{8,10},{10,8},{9,1... | collective-permute-start | bytes 786440 | tf_op jit(solution)/shard_map/ppermute | solution.py:278
  3.5 7.3 %collective-permute-start.1 = (bf16[256,512]{1,0:T(8,128)(2,1)S(1)}, bf16[256,512]{1,0:T(8,128)(2,1)S(1)}, u32[]{:S(2)}, u32[]{:S(2)}) collective-permute-start(bf16[256,512]{1,0:T(8,128)(2,1)S(1)} %constant_dynamic-slice_fusion.refs_0_), channel_id=1, source_target_pairs={{0,4},{4,0},{8,12},{12,8},{16,20},{20,16},{24,28},{28,24},{1,5},{5... | collective-permute-start | bytes 786440 | tf_op jit(solution)/shard_map/ppermute | solution.py:274
  19.3 11.8 %collective-permute-start.8 = (bf16[256,512]{1,0:T(8,128)(2,1)S(1)}, bf16[256,512]{1,0:T(8,128)(2,1)S(1)}, u32[]{:S(2)}, u32[]{:S(2)}) collective-permute-start(bf16[256,512]{1,0:T(8,128)(2,1)S(1)} %collective-permute-done.4.refs_3_), channel_id=1, source_target_pairs={{0,8},{4,12},{8,16},{12,20},{16,24},{20,28},{24,0},{28,4},{1,9},{5... | collective-permute-start | bytes 786440 | tf_op jit(solution)/shard_map/ppermute | solution.py:270
  20.6 10.6 %collective-permute-start.10 = (bf16[256,512]{1,0:T(8,128)(2,1)S(1)}, bf16[256,512]{1,0:T(8,128)(2,1)S(1)}, u32[]{:S(2)}, u32[]{:S(2)}) collective-permute-start(bf16[256,512]{1,0:T(8,128)(2,1)S(1)} %collective-permute-done.5.refs_8_), channel_id=1, source_target_pairs={{0,4},{4,0},{8,12},{12,8},{16,20},{20,16},{24,28},{28,24},{1,5},{5... | collective-permute-start | bytes 786440 | tf_op jit(solution)/shard_map/ppermute | solution.py:274
  31.1 9.6 %collective-permute-start.13 = (bf16[256,512]{1,0:T(8,128)(2,1)S(1)}, bf16[256,512]{1,0:T(8,128)(2,1)S(1)}, u32[]{:S(2)}, u32[]{:S(2)}) collective-permute-start(bf16[256,512]{1,0:T(8,128)(2,1)S(1)} %collective-permute-done.9.refs_0_.refs_12_), channel_id=1, source_target_pairs={{0,4},{4,0},{8,12},{12,8},{16,20},{20,16},{24,28},{28,24},{1,5},{5... | collective-permute-start | bytes 786440 | tf_op jit(solution)/shard_map/ppermute | solution.py:274
  32.1 8.9 %collective-permute-start.15 = (bf16[256,512]{1,0:T(8,128)(2,1)S(1)}, bf16[256,512]{1,0:T(8,128)(2,1)S(1)}, u32[]{:S(2)}, u32[]{:S(2)}) collective-permute-start(bf16[256,512]{1,0:T(8,128)(2,1)S(1)} %collective-permute-done.14.refs_2_.refs_14_), channel_id=1, source_target_pairs={{0,4},{4,0},{8,12},{12,8},{16,20},{20,16},{24,28},{28,24},{1,5},{5... | collective-permute-start | bytes 786440 | tf_op jit(solution)/shard_map/ppermute | solution.py:274
  47.9 11.0 %collective-permute-start.17 = (bf16[2,128,512]{2,1,0:T(8,128)(2,1)S(1)}, bf16[2,128,512]{2,1,0:T(8,128)(2,1)S(1)}, u32[]{:S(2)}, u32[]{:S(2)}) collective-permute-start(bf16[2,128,512]{2,1,0:T(8,128)(2,1)S(1)} %maximum_select_fusion.1.refs_5_), channel_id=1, source_target_pairs={{0,8},{4,12},{8,16},{12,20},{16,24},{20,28},{1,9},{5,13},{9,17},{1... | collective-permute-start | bytes 786440 | tf_op jit(solution)/shard_map/ppermute | solution.py:260
  59.0 84.7 %collective-permute-start.38 = (bf16[4096,512]{1,0:T(8,128)(2,1)S(1)}, bf16[4096,512]{1,0:T(8,128)(2,1)S(1)}, u32[]{:S(2)}, u32[]{:S(2)}) collective-permute-start(bf16[4096,512]{1,0:T(8,128)(2,1)S(1)} %assemble.1), channel_id=1, source_target_pairs={{0,1},{1,0},{2,3},{3,2},{4,5},{5,4},{6,7},{7,6},{8,9},{9,8},{10,11... | collective-permute-start | bytes 12582920 | tf_op jit(solution)/shard_map/ppermute | solution.py:282
  59.9 12.0 %collective-permute-start.21 = (bf16[2,128,512]{2,1,0:T(8,128)(2,1)S(1)}, bf16[2,128,512]{2,1,0:T(8,128)(2,1)S(1)}, u32[]{:S(2)}, u32[]{:S(2)}) collective-permute-start(bf16[2,128,512]{2,1,0:T(8,128)(2,1)S(1)} %collective-permute-done.17.refs_3_), channel_id=1, source_target_pairs={{0,4},{4,0},{8,12},{12,8},{16,20},{20,16},{24,28},{28,24},{1,5},{5... | collective-permute-start | bytes 786440 | tf_op jit(solution)/shard_map/ppermute | solution.py:274
  60.6 12.8 %collective-permute-start.19 = (bf16[2,128,512]{2,1,0:T(8,128)(2,1)S(1)}, bf16[2,128,512]{2,1,0:T(8,128)(2,1)S(1)}, u32[]{:S(2)}, u32[]{:S(2)}) collective-permute-start(bf16[2,128,512]{2,1,0:T(8,128)(2,1)S(1)} %maximum_select_fusion.1.refs_5_), channel_id=1, source_target_pairs={{0,4},{8,12},{16,20},{24,28},{1,5},{9,13},{17,21},{25,29},{2,6},{1... | collective-permute-start | bytes 786440 | tf_op jit(solution)/shard_map/ppermute | solution.py:265
  61.9 11.8 %collective-permute-start.20 = (bf16[2,128,512]{2,1,0:T(8,128)(2,1)S(1)}, bf16[2,128,512]{2,1,0:T(8,128)(2,1)S(1)}, u32[]{:S(2)}, u32[]{:S(2)}) collective-permute-start(bf16[2,128,512]{2,1,0:T(8,128)(2,1)S(1)} %collective-permute-done.17.refs_3_), channel_id=1, source_target_pairs={{4,8},{12,16},{20,24},{5,9},{13,17},{21,25},{6,10},{14,18},{22,26}... | collective-permute-start | bytes 786440 | tf_op jit(solution)/shard_map/ppermute | solution.py:288
  67.8 10.8 %collective-permute-start.18 = (bf16[2,128,512]{2,1,0:T(8,128)(2,1)S(1)}, bf16[2,128,512]{2,1,0:T(8,128)(2,1)S(1)}, u32[]{:S(2)}, u32[]{:S(2)}) collective-permute-start(bf16[2,128,512]{2,1,0:T(8,128)(2,1)S(1)} %collective-permute-done.17.refs_3_), channel_id=1, source_target_pairs={{0,8},{4,12},{8,16},{12,20},{16,24},{20,28},{1,9},{5,13},{9,17},{1... | collective-permute-start | bytes 786440 | tf_op jit(solution)/shard_map/ppermute | solution.py:260
  71.9 21.6 %collective-permute-start.23 = (bf16[256,1024]{1,0:T(8,128)(2,1)S(1)}, bf16[256,1024]{1,0:T(8,128)(2,1)S(1)}, u32[]{:S(2)}, u32[]{:S(2)}) collective-permute-start(bf16[256,1024]{1,0:T(8,128)(2,1)S(1)} %get-tuple-element.120), channel_id=1, source_target_pairs={{0,8},{1,7},{2,10},{3,5},{4,12},{5,3},{6,14},{7,1},{8,16},{9,15},{... | collective-permute-start | bytes 1572872 | tf_op jit(solution)/shard_map/ppermute | solution.py:306
  73.4 22.0 %collective-permute-start.24 = (bf16[256,1024]{1,0:T(8,128)(2,1)S(1)}, bf16[256,1024]{1,0:T(8,128)(2,1)S(1)}, u32[]{:S(2)}, u32[]{:S(2)}) collective-permute-start(bf16[256,1024]{1,0:T(8,128)(2,1)S(1)} %get-tuple-element.121), channel_id=1, source_target_pairs={{0,16},{1,5},{2,18},{3,7},{4,20},{5,1},{6,22},{7,3},{8,24},{9,13},... | collective-permute-start | bytes 1572872 | tf_op jit(solution)/shard_map/ppermute | solution.py:306
  73.7 23.0 %collective-permute-start.25 = (bf16[256,1024]{1,0:T(8,128)(2,1)S(1)}, bf16[256,1024]{1,0:T(8,128)(2,1)S(1)}, u32[]{:S(2)}, u32[]{:S(2)}) collective-permute-start(bf16[256,1024]{1,0:T(8,128)(2,1)S(1)} %get-tuple-element.122), channel_id=1, source_target_pairs={{0,24},{1,3},{2,26},{3,1},{4,28},{5,7},{6,30},{7,5},{8,0},{9,11},{... | collective-permute-start | bytes 1572872 | tf_op jit(solution)/shard_map/ppermute | solution.py:306
  93.5 12.5 %collective-permute-start.27 = (bf16[2,128,512]{2,1,0:T(8,128)(2,1)S(1)}, bf16[2,128,512]{2,1,0:T(8,128)(2,1)S(1)}, u32[]{:S(2)}, u32[]{:S(2)}) collective-permute-start(bf16[2,128,512]{2,1,0:T(8,128)(2,1)S(1)} %get-tuple-element.125), channel_id=1, source_target_pairs={{8,0},{12,4},{16,8},{20,12},{24,16},{28,20},{9,1},{13,5},{17,9},{2... | collective-permute-start | bytes 786440 | tf_op jit(solution)/shard_map/ppermute | solution.py:260
  95.4 16.2 %collective-permute-start.28 = (bf16[2,128,512]{2,1,0:T(8,128)(2,1)S(1)}, bf16[2,128,512]{2,1,0:T(8,128)(2,1)S(1)}, u32[]{:S(2)}, u32[]{:S(2)}) collective-permute-start(bf16[2,128,512]{2,1,0:T(8,128)(2,1)S(1)} %get-tuple-element.118), channel_id=1, source_target_pairs={{8,4},{16,12},{24,20},{9,5},{17,13},{25,21},{10,6},{18,14},{26,22}... | collective-permute-start | bytes 786440 | tf_op jit(solution)/shard_map/ppermute | solution.py:288
  96.8 17.2 %collective-permute-start.22 = (bf16[2,128,512]{2,1,0:T(8,128)(2,1)S(1)}, bf16[2,128,512]{2,1,0:T(8,128)(2,1)S(1)}, u32[]{:S(2)}, u32[]{:S(2)}) collective-permute-start(bf16[2,128,512]{2,1,0:T(8,128)(2,1)S(1)} %get-tuple-element.118), channel_id=1, source_target_pairs={{4,0},{12,8},{20,16},{28,24},{5,1},{13,9},{21,17},{29,25},{6,2},{1... | collective-permute-start | bytes 786440 | tf_op jit(solution)/shard_map/ppermute | solution.py:265
  123.6 9.4 %collective-permute-start.32 = (bf16[256,512]{1,0:T(8,128)(2,1)S(1)}, bf16[256,512]{1,0:T(8,128)(2,1)S(1)}, u32[]{:S(2)}, u32[]{:S(2)}) collective-permute-start(bf16[256,512]{1,0:T(8,128)(2,1)S(1)} %pad_maximum_fusion), channel_id=1, source_target_pairs={{0,16},{1,5},{2,18},{3,7},{4,20},{5,1},{6,22},{7,3},{8,24},{9,13},... | collective-permute-start | bytes 786440 | tf_op jit(solution)/shard_map/ppermute | solution.py:306
  123.7 8.8 %collective-permute-start.31 = (bf16[256,512]{1,0:T(8,128)(2,1)S(1)}, bf16[256,512]{1,0:T(8,128)(2,1)S(1)}, u32[]{:S(2)}, u32[]{:S(2)}) collective-permute-start(bf16[256,512]{1,0:T(8,128)(2,1)S(1)} %pad_maximum_fusion), channel_id=1, source_target_pairs={{0,8},{1,7},{2,10},{3,5},{4,12},{5,3},{6,14},{7,1},{8,16},{9,15},{... | collective-permute-start | bytes 786440 | tf_op jit(solution)/shard_map/ppermute | solution.py:306
  125.9 8.2 %collective-permute-start.33 = (bf16[256,512]{1,0:T(8,128)(2,1)S(1)}, bf16[256,512]{1,0:T(8,128)(2,1)S(1)}, u32[]{:S(2)}, u32[]{:S(2)}) collective-permute-start(bf16[256,512]{1,0:T(8,128)(2,1)S(1)} %pad_maximum_fusion), channel_id=1, source_target_pairs={{0,24},{1,3},{2,26},{3,1},{4,28},{5,7},{6,30},{7,5},{8,0},{9,11},{... | collective-permute-start | bytes 786440 | tf_op jit(solution)/shard_map/ppermute | solution.py:306
  140.8 10.6 %collective-permute-start.35 = (bf16[256,512]{1,0:T(8,128)(2,1)S(1)}, bf16[256,512]{1,0:T(8,128)(2,1)S(1)}, u32[]{:S(2)}, u32[]{:S(2)}) collective-permute-start(bf16[256,512]{1,0:T(8,128)(2,1)S(1)} %get-tuple-element.129), channel_id=1, source_target_pairs={{1,9},{0,6},{3,11},{2,4},{5,13},{4,2},{7,15},{6,0},{9,17},{8,14},{... | collective-permute-start | bytes 786440 | tf_op jit(solution)/shard_map/ppermute | solution.py:306
  142.5 11.7 %collective-permute-start.36 = (bf16[256,512]{1,0:T(8,128)(2,1)S(1)}, bf16[256,512]{1,0:T(8,128)(2,1)S(1)}, u32[]{:S(2)}, u32[]{:S(2)}) collective-permute-start(bf16[256,512]{1,0:T(8,128)(2,1)S(1)} %get-tuple-element.130), channel_id=1, source_target_pairs={{1,17},{0,4},{3,19},{2,6},{5,21},{4,0},{7,23},{6,2},{9,25},{8,12},... | collective-permute-start | bytes 786440 | tf_op jit(solution)/shard_map/ppermute | solution.py:306
  142.5 11.7 %collective-permute-start.37 = (bf16[256,512]{1,0:T(8,128)(2,1)S(1)}, bf16[256,512]{1,0:T(8,128)(2,1)S(1)}, u32[]{:S(2)}, u32[]{:S(2)}) collective-permute-start(bf16[256,512]{1,0:T(8,128)(2,1)S(1)} %get-tuple-element.131), channel_id=1, source_target_pairs={{1,25},{0,2},{3,27},{2,0},{5,29},{4,6},{7,31},{6,4},{9,1},{8,10},{... | collective-permute-start | bytes 786440 | tf_op jit(solution)/shard_map/ppermute | solution.py:306
  (22 other events, 220.7 us)

commit v5 on v4

--- a/solution.py
+++ b/solution.py
@@ -124,7 +124,7 @@
 def attend_kernel(inner, flags, q_ref, g_ref, *refs):
     c_ref, b_ref, e_ref, a_ref, d_ref, own_ref = refs[:6]
     o_ref, dq_ref, far_c, far_be, far_a, far_d, near = refs[6:13]
-    k_held, v_held, acc_k, acc_v = refs[13:]
+    k_held, v_held, acc_k, acc_v, sum_k, sum_v = refs[13:]
     tok = q_ref.shape[0]
     scale = 1.0 / math.sqrt(HEAD_DIM)
     scale_log2 = scale * math.log2(math.e)
@@ -140,12 +140,12 @@
         places.append(pl.ds(pl.multiple_of(count * BLOCK, BLOCK), BLOCK))
         count = count + jnp.where(back > 0, 1, 0)
 
-    for slot, held in ((0, k_held), (1, v_held)):
-        held[:BLOCK] = own_ref[slot]
-        for j, (back, place) in enumerate(zip(backs, places)):
-
-            @pl.when(back > 0)
-            def _(slot=slot, held=held, j=j, place=place):
+    k_held[:BLOCK], v_held[:BLOCK] = own_ref[0], own_ref[1]
+    for j, (back, place) in enumerate(zip(backs, places)):
+
+        @pl.when(back > 0)
+        def _(j=j, place=place):
+            for slot, held in ((0, k_held), (1, v_held)):
                 if j == 1:
                     held[place, :] = jnp.where(even, e_ref[slot], b_ref[slot])
                 else:
@@ -182,24 +182,27 @@
             if p == 0:
                 acc_k[:, :win] = part_k
                 acc_v[:, :win] = part_v
-            else:
+            elif p < GROUPS // 2 - 1:
                 acc_k[:, :win] += part_k
                 acc_v[:, :win] += part_v
+            else:
+                sum_k[:win] = (acc_k[:, :win] + part_k).T
+                sum_v[:win] = (acc_v[:, :win] + part_v).T
 
     for tiles in range(1, REACH + 2):
         pl.when(count == tiles)(functools.partial(work, tiles * BLOCK))
 
-    for slot, acc in ((0, acc_k), (1, acc_v)):
-        near[slot] = acc[:, :BLOCK].T
-        for ref, back, place in zip((far_c, far_be, far_a, far_d), backs, places):
-
-            @pl.when(back > 0)
-            def _(slot=slot, acc=acc, ref=ref, place=place):
-                ref[slot] = acc[:, place].T.astype(ref.dtype)
-
-            @pl.when(back <= 0)
-            def _(slot=slot, ref=ref):
-                ref[slot] = jnp.zeros(ref.shape[1:], ref.dtype)
+    near[0], near[1] = sum_k[:BLOCK], sum_v[:BLOCK]
+    for ref, back, place in zip((far_c, far_be, far_a, far_d), backs, places):
+
+        @pl.when(back > 0)
+        def _(ref=ref, place=place):
+            ref[0] = sum_k[place, :].astype(ref.dtype)
+            ref[1] = sum_v[place, :].astype(ref.dtype)
+
+        @pl.when(back <= 0)
+        def _(ref=ref):
+            ref[...] = jnp.zeros(ref.shape, ref.dtype)
 
 
 def attend(queries, grads, pieces, flags, inner):
@@ -222,6 +225,8 @@
             pltpu.VMEM((win, HEAD_DIM), jnp.bfloat16),
             pltpu.VMEM((HEAD_DIM, win), jnp.float32),
             pltpu.VMEM((HEAD_DIM, win), jnp.float32),
+            pltpu.VMEM((win, HEAD_DIM), jnp.float32),
+            pltpu.VMEM((win, HEAD_DIM), jnp.float32),
         ],
         compiler_params=pltpu.CompilerParams(vmem_limit_bytes=16 << 20),
         cost_estimate=pl.CostEstimate(

time: 158 us -> 157 us (level); the launches traced: 157 us -> 159 us
  waiting for transfers between devices: 68 us -> 72.4 us
  Pallas kernels: 22.3 us -> 19.8 us
    ppermute x4, waiting for transfers between devices: 20.8 us -> 26.6 us  [outer_step(): lax.ppermute(x, 'ctx', [(i, i + by) for i in range(peers) if 0 <= i + by...]
    pallas_call x1, Pallas kernels: 14.9 us -> 12.4 us  [attend(): pl.pallas_call(attend_kernel, grid=(key_width // HEAD_DIM,), in_specs=[sm...]
  transfers between devices with their start and end apart: 40 -> 40, of which waited for: 24 -> 24; matrix products, arithmetic and copies ran while one was open for 4% -> 4% of each run, Pallas kernels for 13% -> 12%
where the time goes in v5:
time: 157 us; the launch traced here: 159 us
  waiting for transfers between devices  72.4 us (46%)
  starting transfers between devices  56.2 us (36%)
  Pallas kernels  19.8 us (13%)
  matrix products  5.91 us (4%)
  local copies, waits for them, and re-layouts  1.97 us (1%)
  other arithmetic  1.69 us (1%)
    ppermute x4, waiting for transfers between devices, outer_step(): lax.ppermute(x, 'ctx', [(i, i + by) for i in range(peers) if 0 <= i + by...  26.6 us
    ppermute x6, starting transfers between devices, swap_core(): return lax.ppermute(x, 'dp', [(0, 1), (1, 0)])  14.2 us
    ppermute x9, waiting for transfers between devices, crossed(): return lax.ppermute(x, ('ctx', 'fsdp', 'dp'), pairs)  12.6 us
    pallas_call x1, Pallas kernels, attend(): pl.pallas_call(attend_kernel, grid=(key_width // HEAD_DIM,), in_specs=[sm...  12.4 us
    ppermute x4, starting transfers between devices, outer_step(): lax.ppermute(x, 'ctx', [(i, i + by) for i in range(peers) if 0 <= i + by...  11.5 us
    ppermute x5, waiting for transfers between devices, outer_shift(): lax.ppermute(x, 'ctx', [(i, (i + INNER * by) % peers) for i in range(peer...  11.3 us
    ppermute x2, starting transfers between devices, odd_step(): lax.ppermute(x, 'ctx', [(i, i + by) for i in range(start, peers, 2) if 0...  7.13 us
    ppermute x9, starting transfers between devices, crossed(): return lax.ppermute(x, ('ctx', 'fsdp', 'dp'), pairs)  7.02 us
  transfers between devices with their start and end apart: 40, of which 24 were waited for; matrix products, arithmetic and copies ran while one was open for 4% of the time, Pallas kernels for 12%

profile of v5, /device:TPU:11, one launch (start us, length us, event | category | flops | bytes accessed | tf_op | source)
XLA Modules:
  0.0 159.0 jit_solution(4948164357649302485)
XLA Ops:
  7.8 2.0 %collective-permute-done.2.refs_2_ = bf16[256,512]{1,0:T(8,128)(2,1)S(1)} collective-permute-done((bf16[256,512]{1,0:T(8,128)(2,1)S(1)}, bf16[256,512]{1,0:T(8,128)(2,1)S(1)}, u32[]{:S(2)}, u32[]{:S(2)}) %collective-permute-start.2) | collective-permute-done | bytes 262176 | tf_op jit(solution)/shard_map/ppermute | solution.py:283
  13.5 3.4 %collective-permute-done.6.refs_5_ = bf16[256,512]{1,0:T(8,128)(2,1)S(1)} collective-permute-done((bf16[256,512]{1,0:T(8,128)(2,1)S(1)}, bf16[256,512]{1,0:T(8,128)(2,1)S(1)}, u32[]{:S(2)}, u32[]{:S(2)}) %collective-permute-start.6) | collective-permute-done | bytes 262176 | tf_op jit(solution)/shard_map/ppermute | solution.py:279
  21.0 3.1 %collective-permute-done.11.refs_10_ = bf16[256,512]{1,0:T(8,128)(2,1)S(1)} collective-permute-done((bf16[256,512]{1,0:T(8,128)(2,1)S(1)}, bf16[256,512]{1,0:T(8,128)(2,1)S(1)}, u32[]{:S(2)}, u32[]{:S(2)}) %collective-permute-start.11) | collective-permute-done | bytes 262176 | tf_op jit(solution)/shard_map/ppermute | solution.py:283
  24.1 1.9 %collective-permute-done.9.refs_0_.refs_12_ = bf16[256,512]{1,0:T(8,128)(2,1)S(1)} collective-permute-done((bf16[256,512]{1,0:T(8,128)(2,1)S(1)}, bf16[256,512]{1,0:T(8,128)(2,1)S(1)}, u32[]{:S(2)}, u32[]{:S(2)}) %collective-permute-start.9) | collective-permute-done | bytes 262176 | tf_op jit(solution)/shard_map/ppermute | solution.py:275
  27.5 3.7 %collective-permute-done.8.refs_7_ = bf16[256,512]{1,0:T(8,128)(2,1)S(1)} collective-permute-done((bf16[256,512]{1,0:T(8,128)(2,1)S(1)}, bf16[256,512]{1,0:T(8,128)(2,1)S(1)}, u32[]{:S(2)}, u32[]{:S(2)}) %collective-permute-start.8) | collective-permute-done | bytes 262176 | tf_op jit(solution)/shard_map/ppermute | solution.py:275
  34.3 3.8 %collective-permute-done.12.refs_11_ = bf16[256,512]{1,0:T(8,128)(2,1)S(1)} collective-permute-done((bf16[256,512]{1,0:T(8,128)(2,1)S(1)}, bf16[256,512]{1,0:T(8,128)(2,1)S(1)}, u32[]{:S(2)}, u32[]{:S(2)}) %collective-permute-start.12) | collective-permute-done | bytes 262176 | tf_op jit(solution)/shard_map/ppermute | solution.py:275
  38.2 2.6 %project.2.refs_4_ = f32[256,512]{1,0:T(8,128)S(1)} custom-call(s32[3,5]{1,0:T(4,128)S(1)} %reshape.25.spots, bf16[128,4096]{1,0:T(8,128)(2,1)S(1)} %bitcast.72, bf16[128,4096]{1,0:T(8,128)(2,1)S(1)} %collective-permute-done.3.theirs_ref, bf16[256,512]{1,0:T(8,128)(2,1)S(1)} %constant_dynamic-slice_fusion.refs_0_, ...), custom_call_target="tpu_custom_call" | custom-call | tf_op jit(solution)/shard_map/project/pallas_call | solution.py:70
  42.3 4.6 %collective-permute-start.16 = (bf16[128,512]{1,0:T(8,128)(2,1)S(1)}, bf16[128,512]{1,0:T(8,128)(2,1)S(1)}, u32[]{:S(2)}, u32[]{:S(2)}) collective-permute-start(bf16[128,512]{1,0:T(8,128)(2,1)S(1)} %get-tuple-element.141), channel_id=1, source_target_pairs={{0,1},{1,0},{2,3},{3,2},{4,5},{5,4},{6,7},{7,6},{8,9},{9,8},{10,11... | collective-permute-start | bytes 393224 | tf_op jit(solution)/shard_map/ppermute | solution.py:287
  47.9 3.5 %collective-permute-start.17 = (bf16[2,128,512]{2,1,0:T(8,128)(2,1)S(1)}, bf16[2,128,512]{2,1,0:T(8,128)(2,1)S(1)}, u32[]{:S(2)}, u32[]{:S(2)}) collective-permute-start(bf16[2,128,512]{2,1,0:T(8,128)(2,1)S(1)} %maximum_select_fusion.1.refs_5_), channel_id=1, source_target_pairs={{0,8},{4,12},{8,16},{12,20},{16,24},{20,28},{1,9},{5,13},{9,17},{1... | collective-permute-start | bytes 786440 | tf_op jit(solution)/shard_map/ppermute | solution.py:265
  52.9 6.1 %collective-permute-done.17.refs_3_ = bf16[2,128,512]{2,1,0:T(8,128)(2,1)S(1)} collective-permute-done((bf16[2,128,512]{2,1,0:T(8,128)(2,1)S(1)}, bf16[2,128,512]{2,1,0:T(8,128)(2,1)S(1)}, u32[]{:S(2)}, u32[]{:S(2)}) %collective-permute-start.17) | collective-permute-done | bytes 262176 | tf_op jit(solution)/shard_map/ppermute | solution.py:265
  61.9 5.8 %collective-permute-start.20 = (bf16[2,128,512]{2,1,0:T(8,128)(2,1)S(1)}, bf16[2,128,512]{2,1,0:T(8,128)(2,1)S(1)}, u32[]{:S(2)}, u32[]{:S(2)}) collective-permute-start(bf16[2,128,512]{2,1,0:T(8,128)(2,1)S(1)} %collective-permute-done.17.refs_3_), channel_id=1, source_target_pairs={{4,8},{12,16},{20,24},{5,9},{13,17},{21,25},{6,10},{14,18},{22,26}... | collective-permute-start | bytes 786440 | tf_op jit(solution)/shard_map/ppermute | solution.py:293
  67.8 4.1 %collective-permute-start.18 = (bf16[2,128,512]{2,1,0:T(8,128)(2,1)S(1)}, bf16[2,128,512]{2,1,0:T(8,128)(2,1)S(1)}, u32[]{:S(2)}, u32[]{:S(2)}) collective-permute-start(bf16[2,128,512]{2,1,0:T(8,128)(2,1)S(1)} %collective-permute-done.17.refs_3_), channel_id=1, source_target_pairs={{0,8},{4,12},{8,16},{12,20},{16,24},{20,28},{1,9},{5,13},{9,17},{1... | collective-permute-start | bytes 786440 | tf_op jit(solution)/shard_map/ppermute | solution.py:265
  74.7 3.8 %collective-permute-done.18.refs_0_ = bf16[2,128,512]{2,1,0:T(8,128)(2,1)S(1)} collective-permute-done((bf16[2,128,512]{2,1,0:T(8,128)(2,1)S(1)}, bf16[2,128,512]{2,1,0:T(8,128)(2,1)S(1)}, u32[]{:S(2)}, u32[]{:S(2)}) %collective-permute-start.18) | collective-permute-done | bytes 262176 | tf_op jit(solution)/shard_map/ppermute | solution.py:265
  78.6 12.4 %attend.1 = (bf16[128,4096]{1,0:T(8,128)(2,1)}, bf16[128,4096]{1,0:T(8,128)(2,1)}, bf16[2,128,512]{2,1,0:T(8,128)(2,1)S(1)}, bf16[2,128,512]{2,1,0:T(8,128)(2,1)...) custom-call(s32[1]{0:T(128)} %bitcast.39.inner, ...), custom_call_target="tpu_custom_call" | custom-call | flops 4026531840 | bytes 15990784 | tf_op jit(solution)/shard_map/attend/pallas_call | solution.py:216
  94.2 3.6 %collective-permute-start.22 = (bf16[2,128,512]{2,1,0:T(8,128)(2,1)S(1)}, bf16[2,128,512]{2,1,0:T(8,128)(2,1)S(1)}, u32[]{:S(2)}, u32[]{:S(2)}) collective-permute-start(bf16[2,128,512]{2,1,0:T(8,128)(2,1)S(1)} %get-tuple-element.118), channel_id=1, source_target_pairs={{4,0},{12,8},{20,16},{28,24},{5,1},{13,9},{21,17},{29,25},{6,2},{1... | collective-permute-start | bytes 786440 | tf_op jit(solution)/shard_map/ppermute | solution.py:270
  97.9 3.3 %collective-permute-done.27 = bf16[2,128,512]{2,1,0:T(8,128)(2,1)S(1)} collective-permute-done((bf16[2,128,512]{2,1,0:T(8,128)(2,1)S(1)}, bf16[2,128,512]{2,1,0:T(8,128)(2,1)S(1)}, u32[]{:S(2)}, u32[]{:S(2)}) %collective-permute-start.27) | collective-permute-done | bytes 262176 | tf_op jit(solution)/shard_map/ppermute | solution.py:265
  101.1 4.5 %collective-permute-done.28 = bf16[2,128,512]{2,1,0:T(8,128)(2,1)S(1)} collective-permute-done((bf16[2,128,512]{2,1,0:T(8,128)(2,1)S(1)}, bf16[2,128,512]{2,1,0:T(8,128)(2,1)S(1)}, u32[]{:S(2)}, u32[]{:S(2)}) %collective-permute-start.28) | collective-permute-done | bytes 262176 | tf_op jit(solution)/shard_map/ppermute | solution.py:293
  107.7 13.4 %collective-permute-done.29 = bf16[2,128,512]{2,1,0:T(8,128)(2,1)S(1)} collective-permute-done((bf16[2,128,512]{2,1,0:T(8,128)(2,1)S(1)}, bf16[2,128,512]{2,1,0:T(8,128)(2,1)S(1)}, u32[]{:S(2)}, u32[]{:S(2)}) %collective-permute-start.29) | collective-permute-done | bytes 262176 | tf_op jit(solution)/shard_map/ppermute | solution.py:265
  121.2 2.9 %collective-permute-start.30 = (bf16[128,512]{1,0:T(8,128)(2,1)S(1)}, bf16[128,512]{1,0:T(8,128)(2,1)S(1)}, u32[]{:S(2)}, u32[]{:S(2)}) collective-permute-start(bf16[128,512]{1,0:T(8,128)(2,1)S(1)} %get-tuple-element.139), channel_id=1, source_target_pairs={{0,1},{1,0},{2,3},{3,2},{4,5},{5,4},{6,7},{7,6},{8,9},{9,8},{10,11... | collective-permute-start | bytes 393224 | tf_op jit(solution)/shard_map/ppermute | solution.py:287
  128.3 5.3 %collective-permute-done.31 = bf16[256,512]{1,0:T(8,128)(2,1)S(1)} collective-permute-done((bf16[256,512]{1,0:T(8,128)(2,1)S(1)}, bf16[256,512]{1,0:T(8,128)(2,1)S(1)}, u32[]{:S(2)}, u32[]{:S(2)}) %collective-permute-start.31) | collective-permute-done | bytes 262176 | tf_op jit(solution)/shard_map/ppermute | solution.py:311
  135.9 4.9 %collective-permute-start.34 = (f32[8,128]{1,0:T(8,128)S(1)}, f32[8,128]{1,0:T(8,128)S(1)}, u32[]{:S(2)}, u32[]{:S(2)}) collective-permute-start(f32[8,128]{1,0:T(8,128)S(1)} %slice.26), channel_id=1, source_target_pairs={{0,1},{1,0},{2,3},{3,2},{4,5},{5,4},{6,7},{7,6},{8,9},{9,8},{10,11... | collective-permute-start | bytes 12296 | tf_op jit(solution)/shard_map/ppermute | solution.py:287
  146.7 2.5 %fusion = bf16[128,4096]{1,0:T(8,128)(2,1)} fusion(f32[128,4096]{1,0:T(8,128)S(1)} %fusion.4, bf16[128,512]{1,0:T(8,128)(2,1)S(1)} %get-tuple-element.138, bf16[4096,512]{1,0:T(8,128)(2,1)S(1)} %assemble.1), kind=kOutput, calls=%fused_computation.1 | convolution fusion | flops 537919488 | bytes 7471104 | tf_op jit(solution)/shard_map/dot_general | solution.py:26
  149.1 3.7 %collective-permute-done.35 = bf16[256,512]{1,0:T(8,128)(2,1)S(1)} collective-permute-done((bf16[256,512]{1,0:T(8,128)(2,1)S(1)}, bf16[256,512]{1,0:T(8,128)(2,1)S(1)}, u32[]{:S(2)}, u32[]{:S(2)}) %collective-permute-start.35) | collective-permute-done | bytes 262176 | tf_op jit(solution)/shard_map/ppermute | solution.py:311
  152.9 2.8 %collective-permute-done.36 = bf16[256,512]{1,0:T(8,128)(2,1)S(1)} collective-permute-done((bf16[256,512]{1,0:T(8,128)(2,1)S(1)}, bf16[256,512]{1,0:T(8,128)(2,1)S(1)}, u32[]{:S(2)}, u32[]{:S(2)}) %collective-permute-start.36) | collective-permute-done | bytes 262176 | tf_op jit(solution)/shard_map/ppermute | solution.py:311
  (97 shorter events, 50.2 us)
Async XLA Ops:
  2.2 7.6 %collective-permute-start.2 = (bf16[256,512]{1,0:T(8,128)(2,1)S(1)}, bf16[256,512]{1,0:T(8,128)(2,1)S(1)}, u32[]{:S(2)}, u32[]{:S(2)}) collective-permute-start(bf16[256,512]{1,0:T(8,128)(2,1)S(1)} %constant_dynamic-slice_fusion.refs_0_), channel_id=1, source_target_pairs={{0,2},{2,0},{1,3},{3,1},{4,6},{6,4},{5,7},{7,5},{8,10},{10,8},{9,1... | collective-permute-start | bytes 786440 | tf_op jit(solution)/shard_map/ppermute | solution.py:283
  19.3 11.8 %collective-permute-start.8 = (bf16[256,512]{1,0:T(8,128)(2,1)S(1)}, bf16[256,512]{1,0:T(8,128)(2,1)S(1)}, u32[]{:S(2)}, u32[]{:S(2)}) collective-permute-start(bf16[256,512]{1,0:T(8,128)(2,1)S(1)} %collective-permute-done.4.refs_3_), channel_id=1, source_target_pairs={{0,8},{4,12},{8,16},{12,20},{16,24},{20,28},{24,0},{28,4},{1,9},{5... | collective-permute-start | bytes 786440 | tf_op jit(solution)/shard_map/ppermute | solution.py:275
  20.6 10.6 %collective-permute-start.10 = (bf16[256,512]{1,0:T(8,128)(2,1)S(1)}, bf16[256,512]{1,0:T(8,128)(2,1)S(1)}, u32[]{:S(2)}, u32[]{:S(2)}) collective-permute-start(bf16[256,512]{1,0:T(8,128)(2,1)S(1)} %collective-permute-done.5.refs_8_), channel_id=1, source_target_pairs={{0,4},{4,0},{8,12},{12,8},{16,20},{20,16},{24,28},{28,24},{1,5},{5... | collective-permute-start | bytes 786440 | tf_op jit(solution)/shard_map/ppermute | solution.py:279
  31.1 9.6 %collective-permute-start.13 = (bf16[256,512]{1,0:T(8,128)(2,1)S(1)}, bf16[256,512]{1,0:T(8,128)(2,1)S(1)}, u32[]{:S(2)}, u32[]{:S(2)}) collective-permute-start(bf16[256,512]{1,0:T(8,128)(2,1)S(1)} %collective-permute-done.9.refs_0_.refs_12_), channel_id=1, source_target_pairs={{0,4},{4,0},{8,12},{12,8},{16,20},{20,16},{24,28},{28,24},{1,5},{5... | collective-permute-start | bytes 786440 | tf_op jit(solution)/shard_map/ppermute | solution.py:279
  32.1 8.9 %collective-permute-start.15 = (bf16[256,512]{1,0:T(8,128)(2,1)S(1)}, bf16[256,512]{1,0:T(8,128)(2,1)S(1)}, u32[]{:S(2)}, u32[]{:S(2)}) collective-permute-start(bf16[256,512]{1,0:T(8,128)(2,1)S(1)} %collective-permute-done.14.refs_2_.refs_14_), channel_id=1, source_target_pairs={{0,4},{4,0},{8,12},{12,8},{16,20},{20,16},{24,28},{28,24},{1,5},{5... | collective-permute-start | bytes 786440 | tf_op jit(solution)/shard_map/ppermute | solution.py:279
  47.9 11.0 %collective-permute-start.17 = (bf16[2,128,512]{2,1,0:T(8,128)(2,1)S(1)}, bf16[2,128,512]{2,1,0:T(8,128)(2,1)S(1)}, u32[]{:S(2)}, u32[]{:S(2)}) collective-permute-start(bf16[2,128,512]{2,1,0:T(8,128)(2,1)S(1)} %maximum_select_fusion.1.refs_5_), channel_id=1, source_target_pairs={{0,8},{4,12},{8,16},{12,20},{16,24},{20,28},{1,9},{5,13},{9,17},{1... | collective-permute-start | bytes 786440 | tf_op jit(solution)/shard_map/ppermute | solution.py:265
  59.0 86.2 %collective-permute-start.38 = (bf16[4096,512]{1,0:T(8,128)(2,1)S(1)}, bf16[4096,512]{1,0:T(8,128)(2,1)S(1)}, u32[]{:S(2)}, u32[]{:S(2)}) collective-permute-start(bf16[4096,512]{1,0:T(8,128)(2,1)S(1)} %assemble.1), channel_id=1, source_target_pairs={{0,1},{1,0},{2,3},{3,2},{4,5},{5,4},{6,7},{7,6},{8,9},{9,8},{10,11... | collective-permute-start | bytes 12582920 | tf_op jit(solution)/shard_map/ppermute | solution.py:287
  59.9 12.0 %collective-permute-start.21 = (bf16[2,128,512]{2,1,0:T(8,128)(2,1)S(1)}, bf16[2,128,512]{2,1,0:T(8,128)(2,1)S(1)}, u32[]{:S(2)}, u32[]{:S(2)}) collective-permute-start(bf16[2,128,512]{2,1,0:T(8,128)(2,1)S(1)} %collective-permute-done.17.refs_3_), channel_id=1, source_target_pairs={{0,4},{4,0},{8,12},{12,8},{16,20},{20,16},{24,28},{28,24},{1,5},{5... | collective-permute-start | bytes 786440 | tf_op jit(solution)/shard_map/ppermute | solution.py:279
  60.6 12.8 %collective-permute-start.19 = (bf16[2,128,512]{2,1,0:T(8,128)(2,1)S(1)}, bf16[2,128,512]{2,1,0:T(8,128)(2,1)S(1)}, u32[]{:S(2)}, u32[]{:S(2)}) collective-permute-start(bf16[2,128,512]{2,1,0:T(8,128)(2,1)S(1)} %maximum_select_fusion.1.refs_5_), channel_id=1, source_target_pairs={{0,4},{8,12},{16,20},{24,28},{1,5},{9,13},{17,21},{25,29},{2,6},{1... | collective-permute-start | bytes 786440 | tf_op jit(solution)/shard_map/ppermute | solution.py:270
  61.9 11.8 %collective-permute-start.20 = (bf16[2,128,512]{2,1,0:T(8,128)(2,1)S(1)}, bf16[2,128,512]{2,1,0:T(8,128)(2,1)S(1)}, u32[]{:S(2)}, u32[]{:S(2)}) collective-permute-start(bf16[2,128,512]{2,1,0:T(8,128)(2,1)S(1)} %collective-permute-done.17.refs_3_), channel_id=1, source_target_pairs={{4,8},{12,16},{20,24},{5,9},{13,17},{21,25},{6,10},{14,18},{22,26}... | collective-permute-start | bytes 786440 | tf_op jit(solution)/shard_map/ppermute | solution.py:293
  67.8 10.8 %collective-permute-start.18 = (bf16[2,128,512]{2,1,0:T(8,128)(2,1)S(1)}, bf16[2,128,512]{2,1,0:T(8,128)(2,1)S(1)}, u32[]{:S(2)}, u32[]{:S(2)}) collective-permute-start(bf16[2,128,512]{2,1,0:T(8,128)(2,1)S(1)} %collective-permute-done.17.refs_3_), channel_id=1, source_target_pairs={{0,8},{4,12},{8,16},{12,20},{16,24},{20,28},{1,9},{5,13},{9,17},{1... | collective-permute-start | bytes 786440 | tf_op jit(solution)/shard_map/ppermute | solution.py:265
  71.9 19.1 %collective-permute-start.23 = (bf16[256,1024]{1,0:T(8,128)(2,1)S(1)}, bf16[256,1024]{1,0:T(8,128)(2,1)S(1)}, u32[]{:S(2)}, u32[]{:S(2)}) collective-permute-start(bf16[256,1024]{1,0:T(8,128)(2,1)S(1)} %get-tuple-element.120), channel_id=1, source_target_pairs={{0,8},{1,7},{2,10},{3,5},{4,12},{5,3},{6,14},{7,1},{8,16},{9,15},{... | collective-permute-start | bytes 1572872 | tf_op jit(solution)/shard_map/ppermute | solution.py:311
  73.4 19.5 %collective-permute-start.24 = (bf16[256,1024]{1,0:T(8,128)(2,1)S(1)}, bf16[256,1024]{1,0:T(8,128)(2,1)S(1)}, u32[]{:S(2)}, u32[]{:S(2)}) collective-permute-start(bf16[256,1024]{1,0:T(8,128)(2,1)S(1)} %get-tuple-element.121), channel_id=1, source_target_pairs={{0,16},{1,5},{2,18},{3,7},{4,20},{5,1},{6,22},{7,3},{8,24},{9,13},... | collective-permute-start | bytes 1572872 | tf_op jit(solution)/shard_map/ppermute | solution.py:311
  73.7 20.5 %collective-permute-start.25 = (bf16[256,1024]{1,0:T(8,128)(2,1)S(1)}, bf16[256,1024]{1,0:T(8,128)(2,1)S(1)}, u32[]{:S(2)}, u32[]{:S(2)}) collective-permute-start(bf16[256,1024]{1,0:T(8,128)(2,1)S(1)} %get-tuple-element.122), channel_id=1, source_target_pairs={{0,24},{1,3},{2,26},{3,1},{4,28},{5,7},{6,30},{7,5},{8,0},{9,11},{... | collective-permute-start | bytes 1572872 | tf_op jit(solution)/shard_map/ppermute | solution.py:311
  91.0 10.1 %collective-permute-start.27 = (bf16[2,128,512]{2,1,0:T(8,128)(2,1)S(1)}, bf16[2,128,512]{2,1,0:T(8,128)(2,1)S(1)}, u32[]{:S(2)}, u32[]{:S(2)}) collective-permute-start(bf16[2,128,512]{2,1,0:T(8,128)(2,1)S(1)} %get-tuple-element.125), channel_id=1, source_target_pairs={{8,0},{12,4},{16,8},{20,12},{24,16},{28,20},{9,1},{13,5},{17,9},{2... | collective-permute-start | bytes 786440 | tf_op jit(solution)/shard_map/ppermute | solution.py:265
  92.9 12.6 %collective-permute-start.28 = (bf16[2,128,512]{2,1,0:T(8,128)(2,1)S(1)}, bf16[2,128,512]{2,1,0:T(8,128)(2,1)S(1)}, u32[]{:S(2)}, u32[]{:S(2)}) collective-permute-start(bf16[2,128,512]{2,1,0:T(8,128)(2,1)S(1)} %get-tuple-element.118), channel_id=1, source_target_pairs={{8,4},{16,12},{24,20},{9,5},{17,13},{25,21},{10,6},{18,14},{26,22}... | collective-permute-start | bytes 786440 | tf_op jit(solution)/shard_map/ppermute | solution.py:293
  94.2 13.4 %collective-permute-start.22 = (bf16[2,128,512]{2,1,0:T(8,128)(2,1)S(1)}, bf16[2,128,512]{2,1,0:T(8,128)(2,1)S(1)}, u32[]{:S(2)}, u32[]{:S(2)}) collective-permute-start(bf16[2,128,512]{2,1,0:T(8,128)(2,1)S(1)} %get-tuple-element.118), channel_id=1, source_target_pairs={{4,0},{12,8},{20,16},{28,24},{5,1},{13,9},{21,17},{29,25},{6,2},{1... | collective-permute-start | bytes 786440 | tf_op jit(solution)/shard_map/ppermute | solution.py:270
  105.7 15.3 %collective-permute-start.29 = (bf16[2,128,512]{2,1,0:T(8,128)(2,1)S(1)}, bf16[2,128,512]{2,1,0:T(8,128)(2,1)S(1)}, u32[]{:S(2)}, u32[]{:S(2)}) collective-permute-start(bf16[2,128,512]{2,1,0:T(8,128)(2,1)S(1)} %add_convert_fusion.1), channel_id=1, source_target_pairs={{8,0},{12,4},{16,8},{20,12},{24,16},{28,20},{9,1},{13,5},{17,9},{2... | collective-permute-start | bytes 786440 | tf_op jit(solution)/shard_map/ppermute | solution.py:265
  125.1 9.0 %collective-permute-start.32 = (bf16[256,512]{1,0:T(8,128)(2,1)S(1)}, bf16[256,512]{1,0:T(8,128)(2,1)S(1)}, u32[]{:S(2)}, u32[]{:S(2)}) collective-permute-start(bf16[256,512]{1,0:T(8,128)(2,1)S(1)} %pad_maximum_fusion), channel_id=1, source_target_pairs={{0,16},{1,5},{2,18},{3,7},{4,20},{5,1},{6,22},{7,3},{8,24},{9,13},... | collective-permute-start | bytes 786440 | tf_op jit(solution)/shard_map/ppermute | solution.py:311
  125.2 8.4 %collective-permute-start.31 = (bf16[256,512]{1,0:T(8,128)(2,1)S(1)}, bf16[256,512]{1,0:T(8,128)(2,1)S(1)}, u32[]{:S(2)}, u32[]{:S(2)}) collective-permute-start(bf16[256,512]{1,0:T(8,128)(2,1)S(1)} %pad_maximum_fusion), channel_id=1, source_target_pairs={{0,8},{1,7},{2,10},{3,5},{4,12},{5,3},{6,14},{7,1},{8,16},{9,15},{... | collective-permute-start | bytes 786440 | tf_op jit(solution)/shard_map/ppermute | solution.py:311
  126.9 8.3 %collective-permute-start.33 = (bf16[256,512]{1,0:T(8,128)(2,1)S(1)}, bf16[256,512]{1,0:T(8,128)(2,1)S(1)}, u32[]{:S(2)}, u32[]{:S(2)}) collective-permute-start(bf16[256,512]{1,0:T(8,128)(2,1)S(1)} %pad_maximum_fusion), channel_id=1, source_target_pairs={{0,24},{1,3},{2,26},{3,1},{4,28},{5,7},{6,30},{7,5},{8,0},{9,11},{... | collective-permute-start | bytes 786440 | tf_op jit(solution)/shard_map/ppermute | solution.py:311
  142.2 10.6 %collective-permute-start.35 = (bf16[256,512]{1,0:T(8,128)(2,1)S(1)}, bf16[256,512]{1,0:T(8,128)(2,1)S(1)}, u32[]{:S(2)}, u32[]{:S(2)}) collective-permute-start(bf16[256,512]{1,0:T(8,128)(2,1)S(1)} %get-tuple-element.129), channel_id=1, source_target_pairs={{1,9},{0,6},{3,11},{2,4},{5,13},{4,2},{7,15},{6,0},{9,17},{8,14},{... | collective-permute-start | bytes 786440 | tf_op jit(solution)/shard_map/ppermute | solution.py:311
  143.9 11.7 %collective-permute-start.36 = (bf16[256,512]{1,0:T(8,128)(2,1)S(1)}, bf16[256,512]{1,0:T(8,128)(2,1)S(1)}, u32[]{:S(2)}, u32[]{:S(2)}) collective-permute-start(bf16[256,512]{1,0:T(8,128)(2,1)S(1)} %get-tuple-element.130), channel_id=1, source_target_pairs={{1,17},{0,4},{3,19},{2,6},{5,21},{4,0},{7,23},{6,2},{9,25},{8,12},... | collective-permute-start | bytes 786440 | tf_op jit(solution)/shard_map/ppermute | solution.py:311
  143.9 11.7 %collective-permute-start.37 = (bf16[256,512]{1,0:T(8,128)(2,1)S(1)}, bf16[256,512]{1,0:T(8,128)(2,1)S(1)}, u32[]{:S(2)}, u32[]{:S(2)}) collective-permute-start(bf16[256,512]{1,0:T(8,128)(2,1)S(1)} %get-tuple-element.131), channel_id=1, source_target_pairs={{1,25},{0,2},{3,27},{2,0},{5,29},{4,6},{7,31},{6,4},{9,1},{8,10},{... | collective-permute-start | bytes 786440 | tf_op jit(solution)/shard_map/ppermute | solution.py:311
  (22 other events, 220.7 us)
